TPU v7x, 32 devices: a whole 2x2x4 slice. The times are simulated.
32 devices in a mesh: dp: 4 (over y, x), seq: 8 (over z, core).
Axes of the slice: x: 2, y: 2, z: 4, core: 2. Of those that a mesh axis runs over, the one named last changes fastest.
Arguments:
- tokens: bfloat16 [4, 1280, 2048], P('dp', 'seq'), may hold values from -6 to 6
- w_query: bfloat16 [2048, 2048], P(('dp', 'seq')), may hold values from -0.125 to 0.125
- w_key: bfloat16 [2048, 2048], P(('dp', 'seq')), may hold values from -0.125 to 0.125
- w_value: bfloat16 [2048, 2048], P(('dp', 'seq')), may hold values from -0.125 to 0.125
- w_out: bfloat16 [2048, 2048], P(None, ('dp', 'seq')), may hold values from -0.125 to 0.125
- w_gate: bfloat16 [2048, 8192], P(('dp', 'seq')), may hold values from -0.125 to 0.125
- w_up: bfloat16 [2048, 8192], P(('dp', 'seq')), may hold values from -0.125 to 0.125
- w_down: bfloat16 [8192, 2048], P(None, ('dp', 'seq')), may hold values from -0.0625 to 0.0625
- gain_query: bfloat16 [2048], P(('dp', 'seq')), may hold values from 0.5 to 1.5
- gain_key: bfloat16 [2048], P(('dp', 'seq')), may hold values from 0.5 to 1.5
- gain_attn: bfloat16 [2048], P(('dp', 'seq')), may hold values from 0.5 to 1.5
- gain_mlp: bfloat16 [2048], P(('dp', 'seq')), may hold values from 0.5 to 1.5
- cotangent: bfloat16 [4, 1280, 2048], P('dp', 'seq'), may hold values from -6 to 6
- key_mask: int32 [4, 1280], P('dp', 'seq'), may hold values 0 or 1
- lengths: int32 [4], P('dp'), may hold values from 640 to 1280, as said below
- tract_order: int32 [4, 16], P('dp', 'seq'), may hold values from 0 to 15, as said below
Outputs:
- layer_out: bfloat16 [4, 1280, 2048], P('dp', 'seq')
- grad_tokens: bfloat16 [4, 1280, 2048], P('dp', 'seq')
- grad_w_query: float32 [2048, 2048], P(('dp', 'seq'))
- grad_w_key: float32 [2048, 2048], P(('dp', 'seq'))
- grad_w_value: float32 [2048, 2048], P(('dp', 'seq'))
- grad_w_out: float32 [2048, 2048], P(None, ('dp', 'seq'))
- grad_w_gate: float32 [2048, 8192], P(('dp', 'seq'))
- grad_w_up: float32 [2048, 8192], P(('dp', 'seq'))
- grad_w_down: float32 [8192, 2048], P(None, ('dp', 'seq'))
- grad_gain_query: float32 [2048], P(('dp', 'seq'))
- grad_gain_key: float32 [2048], P(('dp', 'seq'))
- grad_gain_attn: float32 [2048], P(('dp', 'seq'))
- grad_gain_mlp: float32 [2048], P(('dp', 'seq'))
Inputs may be any that keep to these rules, and one draw needn't show every extreme that they name: `lengths`: some row has all 1280 tokens valid. `tract_order`: each row is a permutation of 0 to 15: entry j is the place, in units of 80 tokens, of the row's j-th stored block.
All inputs are finite; a program needn't handle non-finite values. No bound on the sum of `key_mask` on one device may be relied on, other than what follows from the above.
Results may differ from a plain program's by a relative error of at most 0.02.
Values may be sent and summed in bfloat16 or wider, within the bound.
A program may use at most 768 MiB of HBM per device.

v0:
```python
import jax
import jax.numpy as jnp
from jax import lax
from jax.sharding import PartitionSpec as P

HEAD_DIM = 128


rope_base = 500000.0
norm_eps = 1e-06
key_block = 512


def shifted(shard, axis, by):
    devices = lax.axis_size(axis)
    return lax.ppermute(shard, axis, [(i, (i + by) % devices) for i in range(devices)])


def rms_factor(values):
    return lax.rsqrt(jnp.mean(values * values, axis=-1, keepdims=True) + norm_eps)


def norm_back(grad_normed, raw_values, factor):
    unit_values = raw_values * factor
    return factor * (
        grad_normed - unit_values * jnp.mean(grad_normed * unit_values, axis=-1, keepdims=True)
    )


def rope_tables(positions, head_dim):
    half_dim = head_dim // 2
    steps_f = jnp.arange(half_dim).astype(jnp.float32) * (2.0 / head_dim)
    inv_freq = jnp.power(rope_base, -steps_f)
    angle = positions.astype(jnp.float32)[:, None] * inv_freq[None, :]
    angle = jnp.concatenate([angle, angle], axis=-1)[:, None, :]
    return (jnp.cos(angle), jnp.sin(angle))


def rotate(values, cosine, sine):
    half_dim = values.shape[-1] // 2
    turned = jnp.concatenate([-values[..., half_dim:], values[..., :half_dim]], axis=-1)
    return values * cosine + turned * sine


def unrotate(grads, cosine, sine):
    half_dim = grads.shape[-1] // 2
    moved = grads * sine
    back_part = jnp.concatenate([moved[..., half_dim:], -moved[..., :half_dim]], axis=-1)
    return grads * cosine + back_part


def allowed_mask(query_pos, key_code):
    key_pos = key_code // 2
    usable = key_code % 2 == 1
    causal = key_pos[None, :] <= query_pos[:, None]
    return causal & (usable[None, :] | (key_pos[None, :] == query_pos[:, None]))


def attend_keys(query_low, query_pos, score_scale, carry, pieces):
    key_rows, value_rows, key_code = pieces
    key_count = key_rows.shape[0]
    block_width = key_block if key_count % key_block == 0 else key_count

    def one_block(inner, block_index):
        summed, weight_sum = inner
        begin = block_index * block_width
        key_part = lax.dynamic_slice_in_dim(key_rows, begin, block_width, 0)
        value_part = lax.dynamic_slice_in_dim(value_rows, begin, block_width, 0)
        code_part = lax.dynamic_slice_in_dim(key_code, begin, block_width, 0)
        scores = (
            jnp.einsum("qhd,khd->hqk", query_low, key_part, preferred_element_type=jnp.float32)
            * score_scale
        )
        expo = jnp.where(allowed_mask(query_pos, code_part)[None], jnp.exp(scores), 0.0)
        weight_sum = weight_sum + jnp.sum(expo, axis=-1)
        summed = summed + jnp.einsum(
            "hqk,khd->qhd",
            expo.astype(jnp.bfloat16),
            value_part,
            preferred_element_type=jnp.float32,
        )
        return ((summed, weight_sum), None)

    result, unused = lax.scan(
        one_block, carry, jnp.arange(key_count // block_width, dtype=jnp.int32)
    )
    return result


def cycle_terms(query_low, query_pos, grad_num, drop, score_scale, key_rows, value_rows, key_code):
    scores = (
        jnp.einsum("qhd,khd->hqk", query_low, key_rows, preferred_element_type=jnp.float32)
        * score_scale
    )
    expo = jnp.where(allowed_mask(query_pos, key_code)[None], jnp.exp(scores), 0.0)
    grad_expo = jnp.einsum("qhd,khd->hqk", grad_num, value_rows, preferred_element_type=jnp.float32)
    grad_scores = (expo * (grad_expo - drop[:, :, None])).astype(jnp.bfloat16)
    grad_q = (
        jnp.einsum("hqk,khd->qhd", grad_scores, key_rows, preferred_element_type=jnp.float32)
        * score_scale
    )
    grad_k = (
        jnp.einsum("hqk,qhd->khd", grad_scores, query_low, preferred_element_type=jnp.float32)
        * score_scale
    )
    grad_v = jnp.einsum(
        "hqk,qhd->khd", expo.astype(jnp.bfloat16), grad_num, preferred_element_type=jnp.float32
    )
    return (grad_q, grad_k, grad_v)


def pass_grads(grad_key, grad_value):
    return (
        shifted(grad_key.astype(jnp.bfloat16), "seq", 1).astype(grad_key.dtype),
        shifted(grad_value.astype(jnp.bfloat16), "seq", 1).astype(grad_value.dtype),
    )


def contract(left, right):
    return lax.dot_general(
        left, right, (((0,), (0,)), ((), ())), preferred_element_type=jnp.float32
    )


def contract_last(left, right):
    return lax.dot_general(
        left, right, (((1,), (1,)), ((), ())), preferred_element_type=jnp.float32
    )


def fold_rows(matrix, fold_fn, init):
    return fold_fn(init, lax.all_gather(matrix, ("dp", "seq"), axis=0, tiled=True), jnp.int32(0))


def sum_terms(term_fn, row_count):
    return lax.psum_scatter(
        term_fn(jnp.int32(0), lax.axis_size(("dp", "seq")) * row_count),
        ("dp", "seq"),
        scatter_dimension=0,
        tiled=True,
    )


def project(inputs):

    def project_fold(accum, piece, start):
        return jnp.dot(inputs, piece, preferred_element_type=jnp.float32)

    return project_fold


def expand(grads):

    def expand_fold(accum, piece, start):
        part = contract_last(grads, piece)
        return part

    return expand_fold


def fsdp_layer(
    token_rows,
    grad_out,
    key_code,
    query_pos,
    w_query,
    w_key,
    w_value,
    w_out_t,
    w_gate,
    w_up,
    w_down_t,
    gain_local,
):
    tok_count, feat_width = token_rows.shape
    head_dim = HEAD_DIM
    head_count = feat_width // head_dim
    ff_width = w_gate.shape[1]
    shard_rows = w_query.shape[0]
    score_scale = head_dim ** (-0.5)
    w_qkv = jnp.concatenate([w_query, w_key, w_value], axis=1)
    matrix = lax.all_gather(w_qkv, ("dp", "seq"), axis=0, tiled=True)
    gain_piece = lax.all_gather(gain_local, ("dp", "seq"), axis=0, tiled=True)
    accum = jnp.dot(token_rows, matrix, preferred_element_type=jnp.float32)
    gain_full = gain_piece.astype(jnp.float32)
    q_raw = accum[:, :feat_width]
    k_raw = accum[:, feat_width : 2 * feat_width]
    v_raw = accum[:, 2 * feat_width :]
    q_factor = rms_factor(q_raw)
    k_factor = rms_factor(k_raw)
    q_norm = q_raw * q_factor * gain_full[:, 0]
    k_norm = k_raw * k_factor * gain_full[:, 1]
    cosine, sine = rope_tables(query_pos, head_dim)
    head_shape = (tok_count, head_count, head_dim)
    query_low = rotate(q_norm.reshape(head_shape), cosine, sine).astype(jnp.bfloat16)
    key_low = rotate(k_norm.reshape(head_shape), cosine, sine).astype(jnp.bfloat16)
    value_low = v_raw.astype(jnp.bfloat16).reshape(head_shape)
    attn_init = (
        jnp.zeros(head_shape, jnp.float32),
        jnp.zeros((head_count, tok_count), jnp.float32),
    )
    summed, weight_sum = attend_keys(
        query_low,
        query_pos,
        score_scale,
        attn_init,
        (
            lax.all_gather(key_low, "seq", axis=0, tiled=True),
            lax.all_gather(value_low, "seq", axis=0, tiled=True),
            lax.all_gather(key_code, "seq", axis=0, tiled=True),
        ),
    )
    sum_rows = jnp.transpose(weight_sum)
    attn = summed / sum_rows[:, :, None]
    attn_low = attn.reshape(tok_count, feat_width).astype(jnp.bfloat16)
    feat_zero = jnp.zeros((tok_count, feat_width), jnp.float32)
    branch = fold_rows(w_out_t, expand(attn_low), feat_zero)
    branch_factor = rms_factor(branch)
    branch_unit = branch * branch_factor
    hidden_in = token_rows.astype(jnp.float32) + branch_unit * gain_full[:, 2]
    hidden_low = hidden_in.astype(jnp.bfloat16)
    w_gate_up = jnp.concatenate([w_gate, w_up], axis=1)

    def add_gate_up(carry, piece, start):
        gate_acc = jnp.dot(hidden_low, piece[:, :ff_width], preferred_element_type=jnp.float32)
        up_acc = jnp.dot(hidden_low, piece[:, ff_width:], preferred_element_type=jnp.float32)
        return (gate_acc, up_acc)

    ff_zero = jnp.zeros((tok_count, ff_width), jnp.float32)
    gate_val, up_val = fold_rows(w_gate_up, add_gate_up, (ff_zero, ff_zero))
    mixed_low = (jax.nn.silu(gate_val) * up_val).astype(jnp.bfloat16)
    mlp_val = fold_rows(w_down_t, expand(mixed_low), feat_zero)
    mlp_factor = rms_factor(mlp_val)
    mlp_unit = mlp_val * mlp_factor
    layer_out = hidden_in + mlp_unit * gain_full[:, 3]
    grad_gain_mlp = jnp.sum(grad_out * mlp_unit, axis=0)
    grad_mlp = norm_back(grad_out * gain_full[:, 3], mlp_val, mlp_factor).astype(jnp.bfloat16)
    grad_mixed = fold_rows(w_down_t, project(grad_mlp), ff_zero)
    sigma = jax.nn.sigmoid(gate_val)
    grad_gate = grad_mixed * up_val * sigma * (1.0 + gate_val * (1.0 - sigma))
    grad_up = grad_mixed * gate_val * sigma
    grad_gate_up = jnp.concatenate([grad_gate, grad_up], axis=1).astype(jnp.bfloat16)
    grad_hidden = grad_out + fold_rows(w_gate_up, expand(grad_gate_up), feat_zero)
    grad_gain_attn = jnp.sum(grad_hidden * branch_unit, axis=0)
    grad_branch = norm_back(grad_hidden * gain_full[:, 2], branch, branch_factor).astype(
        jnp.bfloat16
    )
    grad_attn = fold_rows(w_out_t, project(grad_branch), feat_zero).reshape(head_shape)
    grad_num = (grad_attn / sum_rows[:, :, None]).astype(jnp.bfloat16)
    drop = jnp.transpose(jnp.sum(grad_attn * attn, axis=-1) / sum_rows)
    cycle_size = lax.axis_size("seq")

    def cycle_turn(step_index, state):
        key_rows, value_rows, code_rows, grad_key, grad_value, grad_query = state
        part_q, part_k, part_v = cycle_terms(
            query_low, query_pos, grad_num, drop, score_scale, key_rows, value_rows, code_rows
        )
        key_rows, value_rows, code_rows = shifted((key_rows, value_rows, code_rows), "seq", 1)
        grad_key, grad_value = pass_grads(grad_key + part_k, grad_value + part_v)
        return (key_rows, value_rows, code_rows, grad_key, grad_value, grad_query + part_q)

    zero_heads = jnp.zeros(head_shape, jnp.float32)
    cycle_state = lax.fori_loop(
        0,
        cycle_size - 1,
        cycle_turn,
        (key_low, value_low, key_code, zero_heads, zero_heads, zero_heads),
    )
    key_rows, value_rows, code_rows, grad_key, grad_value, grad_query = cycle_state
    part_q, part_k, part_v = cycle_terms(
        query_low, query_pos, grad_num, drop, score_scale, key_rows, value_rows, code_rows
    )
    grad_key, grad_value = pass_grads(grad_key + part_k, grad_value + part_v)
    grad_query = grad_query + part_q
    grad_q_norm = unrotate(grad_query, cosine, sine).reshape(tok_count, feat_width)
    grad_k_norm = unrotate(grad_key, cosine, sine).reshape(tok_count, feat_width)
    grad_gain_query = jnp.sum(grad_q_norm * q_raw * q_factor, axis=0)
    grad_gain_key = jnp.sum(grad_k_norm * k_raw * k_factor, axis=0)
    grad_q_raw = norm_back(grad_q_norm * gain_full[:, 0], q_raw, q_factor)
    grad_k_raw = norm_back(grad_k_norm * gain_full[:, 1], k_raw, k_factor)
    grad_qkv = jnp.concatenate(
        [grad_q_raw, grad_k_raw, grad_value.reshape(tok_count, feat_width)], axis=1
    ).astype(jnp.bfloat16)
    grad_tokens = grad_hidden + fold_rows(w_qkv, expand(grad_qkv), feat_zero)

    def attn_terms(start, row_span):
        return jnp.concatenate(
            [contract(token_rows, grad_qkv), contract(grad_branch, attn_low)], axis=1
        )

    def mlp_terms(start, row_span):
        return jnp.concatenate(
            [contract(hidden_low, grad_gate_up), contract(grad_mlp, mixed_low)], axis=1
        )

    attn_grads = sum_terms(attn_terms, shard_rows)
    mlp_grads = sum_terms(mlp_terms, shard_rows)
    weight_grads = (
        attn_grads[:, :feat_width],
        attn_grads[:, feat_width : 2 * feat_width],
        attn_grads[:, 2 * feat_width : 3 * feat_width],
        jnp.transpose(attn_grads[:, 3 * feat_width :]),
        mlp_grads[:, :ff_width],
        mlp_grads[:, ff_width : 2 * ff_width],
        jnp.transpose(mlp_grads[:, 2 * ff_width :]),
    )
    gain_terms = jnp.stack([grad_gain_query, grad_gain_key, grad_gain_attn, grad_gain_mlp], axis=0)
    return (layer_out, grad_tokens, weight_grads, gain_terms)


def body(
    tokens,
    w_query,
    w_key,
    w_value,
    w_out,
    w_gate,
    w_up,
    w_down,
    gain_query,
    gain_key,
    gain_attn,
    gain_mlp,
    cotangent,
    key_mask,
    lengths,
    tract_order,
):
    token_rows = tokens[0]
    tok_count = token_rows.shape[0]
    half_len = tok_count // 2
    order_pair = tract_order[0]
    slot_index = jnp.arange(tok_count, dtype=jnp.int32)
    query_pos = (
        jnp.where(slot_index < half_len, order_pair[0], order_pair[1]) * half_len
        + slot_index % half_len
    )
    key_ok = ((key_mask[0] == 1) & (query_pos < lengths[0])).astype(jnp.int32)
    key_code = query_pos * 2 + key_ok
    gain_local = jnp.stack([gain_query, gain_key, gain_attn, gain_mlp], axis=1)
    w_out_t = jnp.transpose(w_out)
    w_down_t = jnp.transpose(w_down)
    grad_out = cotangent[0].astype(jnp.float32)
    outcome = fsdp_layer(
        token_rows,
        grad_out,
        key_code,
        query_pos,
        w_query,
        w_key,
        w_value,
        w_out_t,
        w_gate,
        w_up,
        w_down_t,
        gain_local,
    )
    layer_out, grad_tokens, weight_grads, gain_terms = outcome
    gain_grads = lax.psum_scatter(gain_terms, ("dp", "seq"), scatter_dimension=1, tiled=True)
    return (
        layer_out.astype(jnp.bfloat16)[None],
        grad_tokens.astype(jnp.bfloat16)[None],
        weight_grads[0],
        weight_grads[1],
        weight_grads[2],
        weight_grads[3],
        weight_grads[4],
        weight_grads[5],
        weight_grads[6],
        gain_grads[0],
        gain_grads[1],
        gain_grads[2],
        gain_grads[3],
    )


def solution(mesh):
    in_specs = (
        P("dp", "seq", None),
        P(("dp", "seq"), None),
        P(("dp", "seq"), None),
        P(("dp", "seq"), None),
        P(None, ("dp", "seq")),
        P(("dp", "seq"), None),
        P(("dp", "seq"), None),
        P(None, ("dp", "seq")),
        P(("dp", "seq")),
        P(("dp", "seq")),
        P(("dp", "seq")),
        P(("dp", "seq")),
        P("dp", "seq", None),
        P("dp", "seq"),
        P("dp"),
        P("dp", "seq"),
    )
    out_specs = (
        P("dp", "seq", None),
        P("dp", "seq", None),
        P(("dp", "seq"), None),
        P(("dp", "seq"), None),
        P(("dp", "seq"), None),
        P(None, ("dp", "seq")),
        P(("dp", "seq"), None),
        P(("dp", "seq"), None),
        P(None, ("dp", "seq")),
        P(("dp", "seq")),
        P(("dp", "seq")),
        P(("dp", "seq")),
        P(("dp", "seq")),
    )
    return jax.shard_map(body, mesh=mesh, in_specs=in_specs, out_specs=out_specs, check_vma=False)
```

profile of v0, /device:TPU:9, one launch (start us, length us, event | category | flops | bytes accessed | tf_op | source)
XLA Modules:
  0.0 3761.6 jit_solution(1961295207186344778)
XLA Ops:
  9.5 37.9 %all-gather = bf16[32,64,4]{1,2,0:T(4,128)(2,1)S(1)} all-gather(bf16[1,64,4]{1,2,0:T(4,128)(2,1)S(1)} %maximum_bitcast_fusion), channel_id=1, replica_groups=mesh['dp'=4,'seq'=8] {'dp','seq'}, dimensions={0}, use_global_device_ids=true | all-gather | bytes 16896 | tf_op jit(solution)/shard_map/all_gather | solution.py:183
  50.0 116.3 %all-gather.8.cloned.1.call-done = bf16[2048,6144]{1,0:T(8,128)(2,1)} async-done(((bf16[64,6144]{1,0:T(8,128)(2,1)}), bf16[2048,6144]{1,0:T(8,128)(2,1)}) %all-gather.8.cloned.1.call-update) | async-done | bytes 25165840 | tf_op jit(solution)/shard_map/all_gather | solution.py:182
  166.3 10.4 convolution_bitcast_fusion.2
  190.0 8.5 all-reduce
  200.2 36.0 all-gather.12.cloned.1.call-done
  236.2 10.7 fusion.23
  246.9 45.7 %all-gather.10.cloned.1.call-done = bf16[1280,16,128]{2,0,1:T(8,128)(2,1)} async-done(((bf16[160,16,128]{2,0,1:T(8,128)(2,1)}), bf16[1280,16,128]{2,0,1:T(8,128)(2,1)}) %all-gather.10.cloned.1.call-update) | async-done | bytes 5242896 | tf_op jit(solution)/shard_map/all_gather | solution.py:209
  292.6 8.0 fusion.69
  300.6 72.9 %all-gather.14.cloned.1.call-done = bf16[2048,2048]{1,0:T(8,128)(2,1)} async-done(((bf16[64,2048]{1,0:T(8,128)(2,1)}), bf16[2048,2048]{1,0:T(8,128)(2,1)}) %all-gather.14.cloned.1.call-update) | async-done | bytes 8388624 | tf_op jit(solution)/shard_map/all_gather | solution.py:132
  373.5 6.4 multiply_reduce_fusion.5
  381.2 348.7 %all-gather.16.cloned.1.call-done = bf16[2048,16384]{1,0:T(8,128)(2,1)} async-done(((bf16[64,16384]{1,0:T(8,128)(2,1)}), bf16[2048,16384]{1,0:T(8,128)(2,1)}) %all-gather.16.cloned.1.call-update) | async-done | bytes 67108880 | tf_op jit(solution)/shard_map/all_gather | solution.py:132
  730.0 16.0 fusion.21
  746.0 17.9 multiply_convert_fusion.3
  763.9 161.9 %all-gather.18.cloned.1.call-done = bf16[2048,8192]{1,0:T(8,128)(2,1)} async-done(((bf16[64,8192]{1,0:T(8,128)(2,1)}), bf16[2048,8192]{1,0:T(8,128)(2,1)}) %all-gather.18.cloned.1.call-update) | async-done | bytes 33554448 | tf_op jit(solution)/shard_map/all_gather | solution.py:132
  925.8 16.8 multiply_reduce_fusion.4
  944.2 20.8 multiply_convert_fusion.2
  965.0 30.9 multiply_reduce_fusion
  999.5 5.2 convolution_bitcast_fusion.4
  1005.8 261.3 %while.28 = (s32[]{:T(128)}, bf16[160,16,128]{2,0,1:T(8,128)(2,1)S(1)}, bf16[160,16,128]{2,0,1:T(8,128)(2,1)}, s32[160]{0:T(256)S(1)}, f32[160,16,128]{2,0,1:T(8...) while((s32[]{:T(128)}, ...), condition=%wide.region_9.10_spmd.clone, body=%wide.region_8.9_spmd.clone.sunk | while | flops 531605280 | bytes 46134484 | solution.py:263
  1024.4 4.7 collective-permute-done.4
  1031.5 11.6 collective-permute-done.2
  1054.0 4.3 collective-permute-start.2
  1068.8 11.6 collective-permute-done.2
  1093.1 4.3 collective-permute-start.2
  1106.1 11.6 collective-permute-done.2
  1128.6 3.7 collective-permute-start
  1132.3 4.3 collective-permute-start.2
  1144.1 11.0 collective-permute-done.2
  1165.9 5.5 collective-permute-start
  1171.4 4.3 collective-permute-start.2
  1183.2 9.2 collective-permute-done.2
  1203.5 7.0 collective-permute-start
  1210.5 4.3 collective-permute-start.2
  1222.3 7.4 collective-permute-done.2
  1242.6 7.0 collective-permute-start
  1249.7 4.3 collective-permute-start.2
  1261.5 5.6 collective-permute-done.2
  1277.6 8.2 fusion.75
  1298.3 19.5 convolution_bitcast_fusion.1
  1317.9 44.5 %pad_maximum_fusion.1 = f32[2048,8192]{0,1:T(8,128)} fusion(f32[2048,2048]{0,1:T(8,128)} %fusion.75, f32[2048,6144]{0,1:T(8,128)} %convolution_bitcast_fusion.1), kind=kLoop, calls=%fused_computation.33 | loop fusion | flops 16777216 | bytes 134217728 | tf_op jit(solution)/shard_map/concatenate | solution.py:287
  1362.4 61.3 %copy.121 = f32[2048,8192]{1,0:T(8,128)} copy(f32[2048,8192]{0,1:T(8,128)} %pad_maximum_fusion.1) | data formatting | bytes 134217728
  1425.1 25.8 fusion.108
  1450.9 47.1 %fusion.30 = f32[2048,16384]{1,0:T(8,128)} fusion(bf16[160,2048]{1,0:T(8,128)(2,1)S(1)} %copy-done.21, bf16[160,8192]{1,0:T(8,128)(2,1)} %get-tuple-element.372, bf16[160,8192]{1,0:T(8,128)(2,1)} %get-tuple-element.371), kind=kOutput, calls=%fused_computation.52 | convolution fusion | flops 10747904000 | bytes 140115968 | tf_op jit(solution)/shard_map/dot_general | solution.py:120
  1498.0 132.0 %pad_maximum_fusion = f32[2048,24576]{1,0:T(8,128)} fusion(f32[2048,8192]{1,0:T(8,128)} %fusion.108, f32[2048,16384]{1,0:T(8,128)} %fusion.30), kind=kLoop, calls=%fused_computation.32 | loop fusion | flops 50331648 | bytes 402653184 | tf_op jit(solution)/shard_map/concatenate | solution.py:292
  1632.0 14.6 fusion.34
  1649.9 493.9 %reduce-scatter.10.cloned.1.call-done = f32[64,8192]{1,0:T(8,128)} async-done(((f32[2048,8192]{1,0:T(8,128)}), f32[64,8192]{1,0:T(8,128)}) %reduce-scatter.10.cloned.1.call-update) | async-done | bytes 2097168
  2146.7 1602.2 %reduce-scatter.8.cloned.1.call-done = f32[64,24576]{1,0:T(8,128)} async-done(((f32[2048,24576]{1,0:T(8,128)}), f32[64,24576]{1,0:T(8,128)}) %reduce-scatter.8.cloned.1.call-update) | async-done | bytes 6291472 | tf_op jit(solution)/shard_map/reduce_scatter | solution.py:136
  3749.0 5.7 slice_bitcast_fusion
  (366 shorter events, 196.9 us)
Async XLA Ops:
  7.2 159.0 %all-gather.8.cloned.1.call-start = ((), (), s32[]{:S(2)}) async-start(), calls=%async_computation.3 | async-start | bytes 25952256 | tf_op jit(solution)/shard_map/all_gather | solution.py:182
  9.4 226.8 %all-gather.12.cloned.1.call-start = ((), (), s32[]{:S(2)}) async-start(), calls=%async_computation.5 | async-start | bytes 5898240 | tf_op jit(solution)/shard_map/all_gather | solution.py:208
  50.0 946.0 %copy-start.33 = (f32[2048,1]{0,1:T(1,128)}, f32[2048,1]{0,1:T(1,128)S(1)}, u32[]{:S(2)}) copy-start(f32[2048,1]{0,1:T(1,128)S(1)} %get-tuple-element.408) | copy-start | bytes 24580
  181.4 111.3 %all-gather.10.cloned.1.call-start = ((), (), s32[]{:S(2)}) async-start(), calls=%async_computation.4 | async-start | bytes 5898240 | tf_op jit(solution)/shard_map/all_gather | solution.py:209
  183.8 189.6 %all-gather.14.cloned.1.call-start = ((), (), s32[]{:S(2)}) async-start(), calls=%async_computation.6 | async-start | bytes 8650752 | tf_op jit(solution)/shard_map/all_gather | solution.py:132
  184.4 545.5 %all-gather.16.cloned.1.call-start = ((), (), s32[]{:S(2)}) async-start(), calls=%async_computation.7 | async-start | bytes 69206016 | tf_op jit(solution)/shard_map/all_gather | solution.py:132
  186.0 739.8 %all-gather.18.cloned.1.call-start = ((), (), s32[]{:S(2)}) async-start(), calls=%async_computation.8 | async-start | bytes 34603008 | tf_op jit(solution)/shard_map/all_gather | solution.py:132
  186.6 1460.0 %reduce-scatter.12.cloned.1.call-start = ((), (), s32[]{:S(2)}) async-start(), calls=%async_computation.11 | async-start | bytes 1081344
  300.6 704.1 %copy-start.7 = (f32[160,16,128]{2,0,1:T(8,128)}, f32[160,16,128]{2,0,1:T(8,128)S(1)}, u32[]{:S(2)}) copy-start(f32[160,16,128]{2,0,1:T(8,128)S(1)} %fusion.69) | copy-start | bytes 3932164
  1012.0 10.1 collective-permute-start.3
  1016.0 13.1 collective-permute-start.4
  1016.3 26.8 collective-permute-start.1
  1016.6 26.5 collective-permute-start
  1016.9 26.2 collective-permute-start.2
  1049.1 12.1 collective-permute-start.3
  1053.4 13.1 collective-permute-start.4
  1053.4 27.1 collective-permute-start.1
  1053.9 26.5 collective-permute-start
  1054.0 26.4 collective-permute-start.2
  1086.4 13.9 collective-permute-start.3
  1090.7 13.1 collective-permute-start.4
  1090.7 27.1 collective-permute-start.1
  1091.3 26.5 collective-permute-start
  1093.1 24.6 collective-permute-start.2
  1123.8 15.7 collective-permute-start.3
  1128.0 13.7 collective-permute-start.4
  1128.0 27.1 collective-permute-start.1
  1128.6 26.5 collective-permute-start
  1132.3 22.8 collective-permute-start.2
  1161.1 17.5 collective-permute-start.3
  1165.4 15.5 collective-permute-start.4
  1165.4 27.1 collective-permute-start.1
  1165.9 26.5 collective-permute-start
  1171.4 21.0 collective-permute-start.2
  1198.4 19.3 collective-permute-start.3
  1202.7 17.3 collective-permute-start.4
  1202.7 27.1 collective-permute-start.1
  1203.5 26.3 collective-permute-start
  1210.5 19.2 collective-permute-start.2
  1235.8 21.1 collective-permute-start.3
  1240.1 19.1 collective-permute-start.4
  1240.1 27.0 collective-permute-start.1
  1242.6 24.5 collective-permute-start
  1249.7 17.5 collective-permute-start.2
  1273.0 12.8 collective-permute-start.5
  1275.5 21.1 collective-permute-start.6
  1293.5 850.4 %reduce-scatter.10.cloned.1.call-start = ((), (), s32[]{:S(2)}) async-start(), calls=%async_computation.10 | async-start | bytes 69206016
  1423.7 2325.3 %reduce-scatter.8.cloned.1.call-start = ((), (), s32[]{:S(2)}) async-start(), calls=%async_computation.9 | async-start | bytes 207618048 | tf_op jit(solution)/shard_map/reduce_scatter | solution.py:136
  (66 other events, 1411.1 us)
Sparse Core Ops, SparseCore 0:
  11.7 154.5 all-gather.7
  181.5 54.6 all-gather.11
  237.8 54.7 all-gather.9
  295.5 77.9 all-gather.13
  376.9 352.9 all-gather.15
  732.8 192.9 all-gather.17
  1293.6 135.0 reduce-scatter.11
  1431.2 712.5 reduce-scatter.9
  2151.5 1597.4 reduce-scatter.7
where the time goes:
time: 3770 us; the launch traced here: 3760 us
  waiting for transfers between devices  2960 us (79%)
  matrix products  317 us (8%)
  other arithmetic  241 us (6%)
  local copies, waits for them, and re-layouts  100 us (3%)
  starting transfers between devices  82.2 us (2%)
  blocking collectives  46.4 us (1%)
    reduce_scatter x1, waiting for transfers between devices, sum_terms(): lax.psum_scatter(term_fn(jnp.int32(0), lax.axis_size(('dp', 'seq')) * row...  1600 us
    all_gather x3, waiting for transfers between devices, fold_rows(): lax.all_gather(matrix, ('dp', 'seq'), axis=0, tiled=True)  583 us
    unnamed x11, waiting for transfers between devices  495 us
    concatenate x1, other arithmetic, mlp_terms(): jnp.concatenate([contract(hidden_low, grad_gate_up), contract(grad_mlp, m...  132 us
    all_gather x1, waiting for transfers between devices, fsdp_layer(): matrix = lax.all_gather(w_qkv, ('dp', 'seq'), axis=0, tiled=True)  116 us
    dot_general x4, matrix products, contract(): lax.dot_general(left, right, (((0,), (0,)), ((), ())), preferred_element_...  101 us
    ppermute x37, starting transfers between devices, shifted(): lax.ppermute(shard, axis, [(i, (i + by) % devices) for i in range(devices)])  81.6 us
    ppermute x37, waiting for transfers between devices, shifted(): lax.ppermute(shard, axis, [(i, (i + by) % devices) for i in range(devices)])  78.6 us
  transfers between devices with their start and end apart: 46, of which 19 were waited for; matrix products, arithmetic and copies ran while one was open for 13% of the time, Pallas kernels for 0%

commit v1 on v0

v1 whole, which is shorter than its diff:
```python
import jax
import jax.numpy as jnp
from jax import lax
from jax.sharding import PartitionSpec as P

HEAD_DIM = 128

rope_base = 500000.0
norm_eps = 1e-06
f32 = jnp.float32
bf16 = jnp.bfloat16


def rms_factor(values):
    return lax.rsqrt(jnp.mean(values * values, axis=-1, keepdims=True) + norm_eps)


def norm_back(grad_normed, raw_values, factor):
    unit_values = raw_values * factor
    return factor * (
        grad_normed - unit_values * jnp.mean(grad_normed * unit_values, axis=-1, keepdims=True)
    )


def rope_tables(positions, head_dim):
    half_dim = head_dim // 2
    steps_f = jnp.arange(half_dim).astype(f32) * (2.0 / head_dim)
    inv_freq = jnp.power(rope_base, -steps_f)
    angle = positions.astype(f32)[:, None] * inv_freq[None, :]
    angle = jnp.concatenate([angle, angle], axis=-1)[:, None, :]
    return (jnp.cos(angle), jnp.sin(angle))


def rotate(values, cosine, sine):
    half_dim = values.shape[-1] // 2
    turned = jnp.concatenate([-values[..., half_dim:], values[..., :half_dim]], axis=-1)
    return values * cosine + turned * sine


def unrotate(grads, cosine, sine):
    half_dim = grads.shape[-1] // 2
    moved = grads * sine
    back_part = jnp.concatenate([moved[..., half_dim:], -moved[..., :half_dim]], axis=-1)
    return grads * cosine + back_part


def allowed_mask(query_pos, key_code):
    key_pos = key_code // 2
    usable = key_code % 2 == 1
    causal = key_pos[None, :] <= query_pos[:, None]
    return causal & (usable[None, :] | (key_pos[None, :] == query_pos[:, None]))


def dot_nn(left, right):
    return jnp.dot(left, right, preferred_element_type=f32)


def dot_nt(left, right):
    return lax.dot_general(left, right, (((1,), (1,)), ((), ())), preferred_element_type=f32)


def dot_tn(left, right):
    return lax.dot_general(left, right, (((0,), (0,)), ((), ())), preferred_element_type=f32)


def spread_columns(parts, ways):
    rows = parts[0].shape[0]
    split = [p.reshape(rows, ways, p.shape[1] // ways) for p in parts]
    joined = jnp.concatenate(split, axis=2)
    return joined.reshape(rows, ways * joined.shape[2])


def collect(matrix):
    moved = lax.all_to_all(matrix, "seq", split_axis=1, concat_axis=0, tiled=True)
    return lax.all_gather(moved, "dp", axis=0, tiled=True)


def gather_rows(rows):
    return lax.all_gather(rows, "seq", axis=0, tiled=True)


def scatter_rows(partial_rows):
    return lax.psum_scatter(
        partial_rows.astype(bf16), "seq", scatter_dimension=0, tiled=True
    ).astype(f32)


def return_grads(grad, widths, ways):
    summed = lax.psum_scatter(grad.astype(bf16), "dp", scatter_dimension=0, tiled=True)
    rows = summed.shape[0] // ways
    moved = lax.all_to_all(summed, "seq", split_axis=0, concat_axis=1, tiled=True)
    moved = moved.reshape(rows, ways, sum(widths))
    outs, begin = [], 0
    for width in widths:
        outs.append(moved[:, :, begin : begin + width].reshape(rows, ways * width).astype(f32))
        begin += width
    return outs


def body(
    tokens,
    w_query,
    w_key,
    w_value,
    w_out,
    w_gate,
    w_up,
    w_down,
    gain_query,
    gain_key,
    gain_attn,
    gain_mlp,
    cotangent,
    key_mask,
    lengths,
    tract_order,
):
    ways = lax.axis_size("seq")
    me = lax.axis_index("seq")
    token_rows = tokens[0]
    tok_count, feat_width = token_rows.shape
    ff_width = w_gate.shape[1]
    own_feat = feat_width // ways
    own_heads = own_feat // HEAD_DIM
    own_ff = ff_width // ways
    row_len = tok_count * ways
    score_scale = HEAD_DIM ** (-0.5)
    half_len = tok_count // 2
    order_pair = tract_order[0]
    slot_index = jnp.arange(tok_count, dtype=jnp.int32)
    local_pos = (
        jnp.where(slot_index < half_len, order_pair[0], order_pair[1]) * half_len
        + slot_index % half_len
    )
    key_ok = ((key_mask[0] == 1) & (local_pos < lengths[0])).astype(jnp.int32)
    grad_out = cotangent[0].astype(f32)

    gain_local = jnp.stack([gain_query, gain_key, gain_attn, gain_mlp], axis=1)
    gain_pad = jnp.pad(gain_local, ((0, 0), (0, HEAD_DIM - 4)))
    gain_all = jnp.tile(gain_pad, (1, ways))
    m_qkv = collect(spread_columns([w_query, w_key, w_value], ways))
    m_out = collect(spread_columns([jnp.transpose(w_out), gain_all], ways))
    m_gu = collect(spread_columns([w_gate, w_up], ways))
    m_down = collect(spread_columns([jnp.transpose(w_down)], ways))
    gains = jnp.transpose(m_out[:, own_feat:])[:8].astype(f32)
    m_out = m_out[:, :own_feat]
    gain_q = lax.dynamic_slice_in_dim(gains[0], me * own_feat, own_feat, 0)
    gain_k = lax.dynamic_slice_in_dim(gains[1], me * own_feat, own_feat, 0)

    x_row = gather_rows(token_rows)
    key_code = gather_rows(local_pos * 2 + key_ok)
    pos = key_code // 2
    qkv = dot_nn(x_row, m_qkv)
    q_raw, k_raw, v_raw = (qkv[:, i * own_feat : (i + 1) * own_feat] for i in range(3))
    squares = lax.psum(
        jnp.stack([jnp.sum(q_raw * q_raw, axis=-1), jnp.sum(k_raw * k_raw, axis=-1)]), "seq"
    )
    factors = lax.rsqrt(squares / feat_width + norm_eps)
    q_factor, k_factor = factors[0][:, None], factors[1][:, None]
    cosine, sine = rope_tables(pos, HEAD_DIM)
    head_shape = (row_len, own_heads, HEAD_DIM)
    query_low = rotate((q_raw * q_factor * gain_q).reshape(head_shape), cosine, sine).astype(bf16)
    key_low = rotate((k_raw * k_factor * gain_k).reshape(head_shape), cosine, sine).astype(bf16)
    value_low = v_raw.astype(bf16).reshape(head_shape)

    mask = allowed_mask(pos, key_code)[None]
    scores = jnp.einsum("qhd,khd->hqk", query_low, key_low, preferred_element_type=f32) * score_scale
    expo = jnp.where(mask, jnp.exp(scores), 0.0)
    weight_sum = jnp.transpose(jnp.sum(expo, axis=-1))[:, :, None]
    expo_low = expo.astype(bf16)
    attn = jnp.einsum("hqk,khd->qhd", expo_low, value_low, preferred_element_type=f32) / weight_sum
    attn_low = attn.astype(bf16).reshape(row_len, own_feat)

    branch = scatter_rows(dot_nt(attn_low, m_out))
    branch_factor = rms_factor(branch)
    branch_unit = branch * branch_factor
    hidden_in = token_rows.astype(f32) + branch_unit * gains[2]
    hidden_low = gather_rows(hidden_in.astype(bf16))
    gate_up = dot_nn(hidden_low, m_gu)
    gate_val, up_val = gate_up[:, :own_ff], gate_up[:, own_ff:]
    sigma = jax.nn.sigmoid(gate_val)
    mixed_low = (gate_val * sigma * up_val).astype(bf16)
    mlp_val = scatter_rows(dot_nt(mixed_low, m_down))
    mlp_factor = rms_factor(mlp_val)
    mlp_unit = mlp_val * mlp_factor
    layer_out = hidden_in + mlp_unit * gains[3]
    grad_gain_mlp = jnp.sum(grad_out * mlp_unit, axis=0)
    grad_mlp = gather_rows(norm_back(grad_out * gains[3], mlp_val, mlp_factor).astype(bf16))

    grad_mixed = dot_nn(grad_mlp, m_down)
    grad_gate = grad_mixed * up_val * sigma * (1.0 + gate_val * (1.0 - sigma))
    grad_up = grad_mixed * gate_val * sigma
    grad_gu = jnp.concatenate([grad_gate, grad_up], axis=1).astype(bf16)
    grad_hidden = grad_out + scatter_rows(dot_nt(grad_gu, m_gu))
    dw_gu = return_grads(dot_tn(hidden_low, grad_gu), [own_ff, own_ff], ways)
    dw_down = return_grads(dot_tn(grad_mlp, mixed_low), [own_ff], ways)
    grad_gain_attn = jnp.sum(grad_hidden * branch_unit, axis=0)
    grad_branch = gather_rows(
        norm_back(grad_hidden * gains[2], branch, branch_factor).astype(bf16)
    )
    grad_attn = dot_nn(grad_branch, m_out).reshape(head_shape)
    dw_out = return_grads(dot_tn(grad_branch, attn_low), [own_feat], ways)
    grad_num = (grad_attn / weight_sum).astype(bf16)
    drop = jnp.transpose(jnp.sum(grad_attn * attn, axis=-1) / weight_sum[:, :, 0])
    grad_expo = jnp.einsum("qhd,khd->hqk", grad_num, value_low, preferred_element_type=f32)
    grad_scores = (expo * (grad_expo - drop[:, :, None])).astype(bf16)
    grad_q = (
        jnp.einsum("hqk,khd->qhd", grad_scores, key_low, preferred_element_type=f32) * score_scale
    )
    grad_k = (
        jnp.einsum("hqk,qhd->khd", grad_scores, query_low, preferred_element_type=f32) * score_scale
    )
    grad_v = jnp.einsum("hqk,qhd->khd", expo_low, grad_num, preferred_element_type=f32)
    grad_q_norm = unrotate(grad_q, cosine, sine).reshape(row_len, own_feat)
    grad_k_norm = unrotate(grad_k, cosine, sine).reshape(row_len, own_feat)
    q_unit, k_unit = q_raw * q_factor, k_raw * k_factor
    grad_gain_query = jnp.sum(grad_q_norm * q_unit, axis=0)
    grad_gain_key = jnp.sum(grad_k_norm * k_unit, axis=0)
    c_q, c_k = grad_q_norm * gain_q, grad_k_norm * gain_k
    means = (
        lax.psum(jnp.stack([jnp.sum(c_q * q_unit, axis=-1), jnp.sum(c_k * k_unit, axis=-1)]), "seq")
        / feat_width
    )
    grad_q_raw = q_factor * (c_q - q_unit * means[0][:, None])
    grad_k_raw = k_factor * (c_k - k_unit * means[1][:, None])
    grad_qkv = jnp.concatenate(
        [grad_q_raw, grad_k_raw, grad_v.reshape(row_len, own_feat)], axis=1
    ).astype(bf16)
    grad_tokens = grad_hidden + scatter_rows(dot_nt(grad_qkv, m_qkv))

    own_slot = jnp.zeros((2, feat_width), f32)
    own_slot = lax.dynamic_update_slice(
        own_slot, jnp.stack([grad_gain_query, grad_gain_key]), (0, me * own_feat)
    )
    gain_terms = jnp.concatenate([own_slot, jnp.stack([grad_gain_attn, grad_gain_mlp])])
    gain_columns = jnp.pad(jnp.transpose(gain_terms), ((0, 0), (0, HEAD_DIM - 4)))
    dw_qkv = return_grads(
        jnp.concatenate([dot_tn(x_row, grad_qkv), gain_columns], axis=1),
        [own_feat] * 3 + [HEAD_DIM],
        ways,
    )
    gain_grads = jnp.sum(dw_qkv[3].reshape(-1, ways, HEAD_DIM), axis=1)
    gain_grads = jnp.transpose(gain_grads[:, :8])
    return (
        layer_out.astype(bf16)[None],
        grad_tokens.astype(bf16)[None],
        dw_qkv[0],
        dw_qkv[1],
        dw_qkv[2],
        jnp.transpose(dw_out[0]),
        dw_gu[0],
        dw_gu[1],
        jnp.transpose(dw_down[0]),
        gain_grads[0],
        gain_grads[1],
        gain_grads[2],
        gain_grads[3],
    )


def solution(mesh):
    both = ("dp", "seq")
    in_specs = (
        P("dp", "seq", None),
        P(both, None),
        P(both, None),
        P(both, None),
        P(None, both),
        P(both, None),
        P(both, None),
        P(None, both),
        P(both),
        P(both),
        P(both),
        P(both),
        P("dp", "seq", None),
        P("dp", "seq"),
        P("dp"),
        P("dp", "seq"),
    )
    out_specs = (
        P("dp", "seq", None),
        P("dp", "seq", None),
        P(both, None),
        P(both, None),
        P(both, None),
        P(None, both),
        P(both, None),
        P(both, None),
        P(None, both),
        P(both),
        P(both),
        P(both),
        P(both),
    )
    return jax.shard_map(body, mesh=mesh, in_specs=in_specs, out_specs=out_specs, check_vma=False)
```

time: 3770 us -> 1120 us (0.30)
  waiting for transfers between devices: 2960 us -> 573 us
  blocking collectives: 46.4 us -> 292 us
  other arithmetic: 241 us -> 38.8 us
  matrix products: 317 us -> 138 us
  starting transfers between devices: 82.2 us -> 13.3 us
  local copies, waits for them, and re-layouts: 100 us -> 36.8 us
    reduce_scatter x1 -> x8, waiting for transfers between devices: 1600 us -> 227 us  [the longest x4 166 us: scatter_rows(): lax.psum_scatter(partial_rows.astype(bf16), 'seq', scatter_dimension=0, t...]
    unnamed x11 -> x16, waiting for transfers between devices: 495 us -> 0.93 us
    all_gather x6 -> x8, waiting for transfers between devices: 782 us -> 318 us  [the longest x4 195 us: gather_rows(): return lax.all_gather(rows, 'seq', axis=0, tiled=True)]
    all_to_all x0 -> x6, blocking collectives: none -> 240 us  [the longest x4 155 us: collect(): lax.all_to_all(matrix, 'seq', split_axis=1, concat_axis=0, tiled=True)]
    dot_general x55 -> x18, matrix products: 317 us -> 138 us  [the longest x4 40.8 us: dot_nn(): return jnp.dot(left, right, preferred_element_type=f32)]
    concatenate x4, other arithmetic: 180 us -> 2.57 us  [the longest x1 2.29 us: body(): jnp.concatenate([dot_tn(x_row, grad_qkv), gain_columns], axis=1)]
    ppermute x37 -> x0, starting transfers between devices: 81.6 us -> none  [shifted(): lax.ppermute(shard, axis, [(i, (i + by) % devices) for i in range(devices)])]
    ppermute x37 -> x0, waiting for transfers between devices: 78.6 us -> none  [shifted(): lax.ppermute(shard, axis, [(i, (i + by) % devices) for i in range(devices)])]
  transfers between devices with their start and end apart: 46 -> 18, of which waited for: 19 -> 14; matrix products, arithmetic and copies ran while one was open for 13% -> 11% of each run, Pallas kernels for 0% -> 0%
where the time goes in v1:
time: 1120 us; the launch traced here: 1110 us
  waiting for transfers between devices  573 us (51%)
  blocking collectives  292 us (26%)
  matrix products  138 us (12%)
  other arithmetic  38.8 us (3%)
  local copies, waits for them, and re-layouts  36.8 us (3%)
  between operations  16.6 us (1%)
  starting transfers between devices  13.3 us (1%)
    all_gather x4, waiting for transfers between devices, gather_rows(): return lax.all_gather(rows, 'seq', axis=0, tiled=True)  195 us
    reduce_scatter x4, waiting for transfers between devices, scatter_rows(): lax.psum_scatter(partial_rows.astype(bf16), 'seq', scatter_dimension=0, t...  166 us
    all_to_all x4, blocking collectives, collect(): lax.all_to_all(matrix, 'seq', split_axis=1, concat_axis=0, tiled=True)  155 us
    all_gather x4, waiting for transfers between devices, collect(): return lax.all_gather(moved, 'dp', axis=0, tiled=True)  123 us
    all_to_all x2, blocking collectives, return_grads(): lax.all_to_all(summed, 'seq', split_axis=0, concat_axis=1, tiled=True)  85.1 us
    reduce_scatter x4, waiting for transfers between devices, return_grads(): lax.psum_scatter(grad.astype(bf16), 'dp', scatter_dimension=0, tiled=True)  61.6 us
    dot_general x4, matrix products, dot_nn(): return jnp.dot(left, right, preferred_element_type=f32)  40.8 us
    dot_general x4, matrix products, dot_tn(): lax.dot_general(left, right, (((0,), (0,)), ((), ())), preferred_element_...  37.7 us
  transfers between devices with their start and end apart: 18, of which 14 were waited for; matrix products, arithmetic and copies ran while one was open for 11% of the time, Pallas kernels for 0%

profile of v1, /device:TPU:9, one launch (start us, length us, event | category | flops | bytes accessed | tf_op | source)
XLA Modules:
  0.0 1109.0 jit_solution(11077632735175738909)
XLA Ops:
  9.3 15.8 %all_to_all.125 = bf16[64,8,384]{2,0,1:T(8,128)(2,1)} all-to-all(bf16[64,8,384]{2,0,1:T(8,128)(2,1)S(1)} %copy.115), channel_id=1, replica_groups=mesh['dp'=4,'seq'=8] {'seq'}, dimensions={1} | all-to-all | bytes 786432 | tf_op jit(solution)/shard_map/all_to_all | solution.py:74
  25.6 23.3 %all_to_all.126 = bf16[64,8,768]{2,0,1:T(8,128)(2,1)} all-to-all(bf16[64,8,768]{2,0,1:T(8,128)(2,1)S(1)} %copy.113), channel_id=1, replica_groups=mesh['dp'=4,'seq'=8] {'seq'}, dimensions={1} | all-to-all | bytes 1572864 | tf_op jit(solution)/shard_map/all_to_all | solution.py:74
  53.6 6.9 all-reduce.2
  60.7 3.3 broadcast_multiply_fusion.3
  64.0 2.8 or_and_fusion
  69.7 32.8 %all-gather.10.cloned.1.call-done = bf16[2048,768]{1,0:T(8,128)(2,1)} async-done(((bf16[512,768]{1,0:T(8,128)(2,1)}), bf16[2048,768]{1,0:T(8,128)(2,1)}) %all-gather.10.cloned.1.call-update) | async-done | bytes 3145744 | tf_op jit(solution)/shard_map/all_gather | solution.py:75
  102.5 56.4 %all-gather.24.cloned.1.call-done = bf16[1,1280,2048]{2,1,0:T(8,128)(2,1)} async-done(((bf16[1,160,2048]{2,1,0:T(8,128)(2,1)}), bf16[1,1280,2048]{2,1,0:T(8,128)(2,1)}) %all-gather.24.cloned.1.call-update) | async-done | bytes 5242896 | tf_op jit(solution)/shard_map/all_gather | solution.py:79
  158.9 7.7 fusion.7
  168.6 22.2 %psum.14 = f32[2,1280]{1,0:T(2,128)S(1)} all-reduce(f32[2,1280]{1,0:T(2,128)S(1)} %pad_maximum_fusion.10), channel_id=1, replica_groups=mesh['dp'=4,'seq'=8] {'seq'}, use_global_device_ids=true, to_apply=%region_2.3 | all-reduce | flops 2560 | bytes 20480 | tf_op jit(solution)/shard_map/psum | solution.py:155
  194.5 3.5 fusion.83
  200.3 3.1 copy-done
  204.2 3.8 convolution_convert_fusion.4
  211.9 88.8 %all_to_all.127 = bf16[64,8,2048]{2,0,1:T(8,128)(2,1)} all-to-all(bf16[64,8,2048]{2,0,1:T(8,128)(2,1)S(1)} %copy.119), channel_id=1, replica_groups=mesh['dp'=4,'seq'=8] {'seq'}, dimensions={1} | all-to-all | bytes 4194304 | tf_op jit(solution)/shard_map/all_to_all | solution.py:74
  300.8 15.4 %reduce-scatter.9.cloned.1.call-done = bf16[160,2048]{1,0:T(8,128)(2,1)} async-done(((bf16[1280,2048]{1,0:T(8,128)(2,1)}), bf16[160,2048]{1,0:T(8,128)(2,1)}) %reduce-scatter.9.cloned.1.call-update) | async-done | bytes 655376 | tf_op jit(solution)/shard_map/reduce_scatter | solution.py:83
  319.9 27.2 %all_to_all.128 = bf16[64,8,1024]{2,0,1:T(8,128)(2,1)} all-to-all(bf16[64,8,1024]{2,0,1:T(8,128)(2,1)S(1)} %bitcast.187), channel_id=1, replica_groups=mesh['dp'=4,'seq'=8] {'seq'}, dimensions={1} | all-to-all | bytes 2097152 | tf_op jit(solution)/shard_map/all_to_all | solution.py:74
  347.6 57.2 %all-gather.16.cloned.1.call-done = bf16[2048,2048]{1,0:T(8,128)(2,1)} async-done(((bf16[512,2048]{1,0:T(8,128)(2,1)}), bf16[2048,2048]{1,0:T(8,128)(2,1)}) %all-gather.16.cloned.1.call-update) | async-done | bytes 8388624 | tf_op jit(solution)/shard_map/all_gather | solution.py:75
  404.9 56.8 %all-gather.14.cloned.1.call-done = bf16[1280,2048]{1,0:T(8,128)(2,1)} async-done(((bf16[160,2048]{1,0:T(8,128)(2,1)}), bf16[1280,2048]{1,0:T(8,128)(2,1)}) %all-gather.14.cloned.1.call-update) | async-done | bytes 5242896 | tf_op jit(solution)/shard_map/all_gather | solution.py:79
  461.7 15.2 %fusion.85 = f32[1280,2048]{1,0:T(8,128)S(1)} fusion(bf16[1280,2048]{1,0:T(8,128)(2,1)} %all-gather.14.cloned.1.call-done, bf16[2048,2048]{1,0:T(8,128)(2,1)} %all-gather.16.cloned.1.call-done), kind=kOutput, calls=%fused_computation.180 | convolution fusion | flops 10737418240 | bytes 24117248 | tf_op jit(solution)/shard_map/dot_general | solution.py:55
  476.9 3.9 copy-done.5
  480.8 2.7 multiply_convert_fusion.2
  483.5 32.9 %all-gather.18.cloned.1.call-done = bf16[2048,1024]{1,0:T(8,128)(2,1)} async-done(((bf16[512,1024]{1,0:T(8,128)(2,1)}), bf16[2048,1024]{1,0:T(8,128)(2,1)}) %all-gather.18.cloned.1.call-update) | async-done | bytes 4194320 | tf_op jit(solution)/shard_map/all_gather | solution.py:75
  516.4 9.9 convolution_convert_fusion.3
  526.4 58.5 %reduce-scatter.11.cloned.1.call-done = bf16[160,2048]{1,0:T(8,128)(2,1)} async-done(((bf16[1280,2048]{1,0:T(8,128)(2,1)}), bf16[160,2048]{1,0:T(8,128)(2,1)}) %reduce-scatter.11.cloned.1.call-update) | async-done | bytes 655376 | tf_op jit(solution)/shard_map/reduce_scatter | solution.py:83
  589.4 54.5 %all-gather.20.cloned.1.call-done = bf16[1280,2048]{1,0:T(8,128)(2,1)} async-done(((bf16[160,2048]{1,0:T(8,128)(2,1)}), bf16[1280,2048]{1,0:T(8,128)(2,1)}) %all-gather.20.cloned.1.call-update) | async-done | bytes 5242896 | tf_op jit(solution)/shard_map/all_gather | solution.py:79
  643.9 13.1 %multiply_convert_fusion.1 = (bf16[1280,1024]{1,0:T(8,128)(2,1)S(1)}, bf16[1280,1024]{1,0:T(8,128)(2,1)S(1)}) fusion(f32[1280,2048]{1,0:T(8,128)} %copy-done.5, bf16[1280,2048]{1,0:T(8,128)(2,1)} %all-gather.20.cloned.1.call-done, bf16[2048,1024]{1,0:T(8,128)(2,1)} %all-gather.18.cloned.1.call-done), kind=kOutput, calls=%fused_computation.19 | convolution fusion | flops 5385748480 | bytes 25165824 | tf_op jit(solution)/shard_map/dot_general | solution.py:55
  659.3 15.3 %convolution_convert_fusion.2 = bf16[1280,2048]{1,0:T(8,128)(2,1)} fusion(bf16[2048,2048]{1,0:T(8,128)(2,1)} %all-gather.16.cloned.1.call-done, bf16[1280,1024]{1,0:T(8,128)(2,1)S(1)} %get-tuple-element.38, bf16[1280,1024]{1,0:T(8,128)(2,1)S(1)} %get-tuple-element.37), kind=kOutput, calls=%fused_computation.7 | convolution fusion | flops 10750525440 | bytes 18874368 | tf_op jit(solution)/shard_map/dot_general | solution.py:59
  674.7 58.6 %reduce-scatter.13.cloned.1.call-done = bf16[160,2048]{1,0:T(8,128)(2,1)} async-done(((bf16[1280,2048]{1,0:T(8,128)(2,1)}), bf16[160,2048]{1,0:T(8,128)(2,1)}) %reduce-scatter.13.cloned.1.call-update) | async-done | bytes 655376 | tf_op jit(solution)/shard_map/reduce_scatter | solution.py:83
  737.1 10.2 convolution_convert_fusion.5
  747.6 16.7 %convolution_convert_fusion = bf16[2048,2048]{1,0:T(8,128)(2,1)} fusion(bf16[1280,2048]{1,0:T(8,128)(2,1)} %all-gather.14.cloned.1.call-done, bf16[1280,1024]{1,0:T(8,128)(2,1)} %copy-done.42, bf16[1280,1024]{1,0:T(8,128)(2,1)} %copy-done.41), kind=kOutput, calls=%fused_computation.5 | convolution fusion | flops 10752098304 | bytes 18874368 | tf_op jit(solution)/shard_map/dot_general | solution.py:63
  764.4 27.4 %all-gather.22.cloned.1.call-done = bf16[1280,2048]{1,0:T(8,128)(2,1)} async-done(((bf16[160,2048]{1,0:T(8,128)(2,1)}), bf16[1280,2048]{1,0:T(8,128)(2,1)}) %all-gather.22.cloned.1.call-update) | async-done | bytes 5242896 | tf_op jit(solution)/shard_map/all_gather | solution.py:79
  791.8 4.7 multiply_reduce_fusion.2
  796.6 6.3 fusion.1
  810.4 23.1 %psum.15 = f32[2,1280]{1,0:T(2,128)S(1)} all-reduce(f32[2,1280]{1,0:T(2,128)S(1)} %pad_maximum_fusion.11), channel_id=1, replica_groups=mesh['dp'=4,'seq'=8] {'seq'}, use_global_device_ids=true, to_apply=%region_14.15 | all-reduce | flops 2560 | bytes 20480 | tf_op jit(solution)/shard_map/psum | solution.py:221
  833.6 5.3 convolution_convert_fusion.6
  839.0 2.6 multiply_convert_fusion.4
  841.7 7.5 fusion.27
  849.2 5.6 fusion.18
  854.8 2.3 fusion.10
  858.7 8.0 convolution_convert_fusion.1
  866.7 33.6 %all_to_all.129 = bf16[8,64,1024]{2,1,0:T(8,128)(2,1)} all-to-all(bf16[8,64,1024]{2,1,0:T(8,128)(2,1)} %bitcast.201), channel_id=1, replica_groups=mesh['dp'=4,'seq'=8] {'seq'}, dimensions={0} | all-to-all | bytes 2097152 | tf_op jit(solution)/shard_map/all_to_all | solution.py:91
  900.3 36.9 %reduce-scatter.21.cloned.1.call-done = bf16[512,2048]{1,0:T(8,128)(2,1)} async-done(((bf16[2048,2048]{1,0:T(8,128)(2,1)}), bf16[512,2048]{1,0:T(8,128)(2,1)}) %reduce-scatter.21.cloned.1.call-update) | async-done | bytes 2097168 | tf_op jit(solution)/shard_map/reduce_scatter | solution.py:89
  937.2 51.5 %all_to_all.130 = bf16[8,64,2048]{2,1,0:T(8,128)(2,1)S(1)} all-to-all(bf16[8,64,2048]{2,1,0:T(8,128)(2,1)} %bitcast.192), channel_id=1, replica_groups=mesh['dp'=4,'seq'=8] {'seq'}, dimensions={0} | all-to-all | bytes 4194304 | tf_op jit(solution)/shard_map/all_to_all | solution.py:91
  988.7 6.3 all-to-all-start.5
  995.1 24.7 %reduce-scatter.17.cloned.1.call-done = bf16[512,896]{0,1:T(8,128)(2,1)} async-done(((bf16[2048,896]{0,1:T(8,128)(2,1)}), bf16[512,896]{0,1:T(8,128)(2,1)}) %reduce-scatter.17.cloned.1.call-update) | async-done | bytes 917520 | tf_op jit(solution)/shard_map/reduce_scatter | solution.py:89
  1022.0 5.5 all-to-all-start.4
  1034.7 26.6 %all-to-all-done.4 = bf16[8,64,896]{2,1,0:T(8,128)(2,1)} async-done(((bf16[8,64,896]{2,1,0:T(8,128)(2,1)}), bf16[8,64,896]{2,1,0:T(8,128)(2,1)}, u32[]{:S(2)}, u32[]{:S(2)}) %all-to-all-start.4) | async-done | bytes 917536 | tf_op jit(solution)/shard_map/all_to_all | solution.py:91
  1066.8 33.0 %reduce-scatter.15.cloned.1.call-done = bf16[160,2048]{1,0:T(8,128)(2,1)} async-done(((bf16[1280,2048]{1,0:T(8,128)(2,1)}), bf16[160,2048]{1,0:T(8,128)(2,1)}) %reduce-scatter.15.cloned.1.call-update) | async-done | bytes 655376 | tf_op jit(solution)/shard_map/reduce_scatter | solution.py:83
  1099.8 2.2 fusion.64
  (210 shorter events, 60.7 us)
Async XLA Ops:
  7.2 18.0 %copy-start.27 = (bf16[64,2048]{1,0:T(8,128)(2,1)S(1)}, bf16[64,2048]{1,0:T(8,128)(2,1)}, u32[]{:S(2)}) copy-start(bf16[64,2048]{1,0:T(8,128)(2,1)} %param.17) | copy-start | bytes 786436
  7.2 18.1 %copy-start.28 = (bf16[64,2048]{1,0:T(8,128)(2,1)S(1)}, bf16[64,2048]{1,0:T(8,128)(2,1)}, u32[]{:S(2)}) copy-start(bf16[64,2048]{1,0:T(8,128)(2,1)} %param.18) | copy-start | bytes 786436
  7.2 59.6 %all-gather.12.cloned.1.call-start = ((), (), s32[]{:S(2)}) async-start(), calls=%async_computation.17 | async-start | bytes 1966080 | tf_op jit(solution)/shard_map/all_gather | solution.py:75
  8.3 17.0 %copy-start.29 = (bf16[64,2048]{1,0:T(8,128)(2,1)S(1)}, bf16[64,2048]{1,0:T(8,128)(2,1)}, u32[]{:S(2)}) copy-start(bf16[64,2048]{1,0:T(8,128)(2,1)} %param.19) | copy-start | bytes 786436
  25.1 77.4 %all-gather.10.cloned.1.call-start = ((), (), s32[]{:S(2)}) async-start(), calls=%async_computation.16 | async-start | bytes 3932160 | tf_op jit(solution)/shard_map/all_gather | solution.py:75
  25.4 24.9 %copy-start.40 = (u32[32]{0:T(128)S(1)}, u32[32]{0:T(128)}, u32[]{:S(2)}) copy-start(u32[32]{0:T(128)} %constant.93) | copy-start | bytes 388
  25.5 26.1 %copy-start.38 = (s32[1,2]{1,0:T(1,128)S(1)}, s32[1,2]{1,0:T(1,128)}, u32[]{:S(2)}) copy-start(s32[1,2]{1,0:T(1,128)} %param.31) | copy-start | bytes 28
  25.5 26.7 %copy-start.39 = (s32[1,160]{1,0:T(1,128)S(1)}, s32[1,160]{1,0:T(1,128)}, u32[]{:S(2)}) copy-start(s32[1,160]{1,0:T(1,128)} %param.29) | copy-start | bytes 1924
  48.9 109.9 %all-gather.24.cloned.1.call-start = ((), (), s32[]{:S(2)}) async-start(), calls=%async_computation.31 | async-start | bytes 5898240 | tf_op jit(solution)/shard_map/all_gather | solution.py:79
  49.7 266.6 %reduce-scatter.9.cloned.1.call-start = ((), (), s32[]{:S(2)}) async-start(), calls=%async_computation.18 | async-start | bytes 5898240 | tf_op jit(solution)/shard_map/reduce_scatter | solution.py:83
  69.6 121.2 %copy-start.34 = (f32[256]{0:T(256)}, f32[256]{0:T(256)S(1)}, u32[]{:S(2)}) copy-start(f32[256]{0:T(256)S(1)} %get-tuple-element.79) | copy-start | bytes 3076
  69.6 121.2 %copy-start.36 = (f32[256]{0:T(256)}, f32[256]{0:T(256)S(1)}, u32[]{:S(2)}) copy-start(f32[256]{0:T(256)S(1)} %get-tuple-element.80) | copy-start | bytes 3076
  193.7 4.4 copy-start.16
  198.1 5.3 copy-start
  198.1 6.1 copy-start.19
  208.1 196.8 %all-gather.16.cloned.1.call-start = ((), (), s32[]{:S(2)}) async-start(), calls=%async_computation.20 | async-start | bytes 10485760 | tf_op jit(solution)/shard_map/all_gather | solution.py:75
  300.7 16.8 %copy-start.10 = (bf16[1,160,2048]{2,1,0:T(8,128)(2,1)S(1)}, bf16[1,160,2048]{2,1,0:T(8,128)(2,1)}, u32[]{:S(2)}) copy-start(bf16[1,160,2048]{2,1,0:T(8,128)(2,1)} %param.16) | copy-start | bytes 1966084
  300.7 19.1 %copy-start.22 = (bf16[8192,64]{0,1:T(8,128)(2,1)S(1)}, bf16[8192,64]{0,1:T(8,128)(2,1)}, u32[]{:S(2)}) copy-start(bf16[8192,64]{0,1:T(8,128)(2,1)} %param.23) | copy-start | bytes 3145732
  300.7 160.9 %all-gather.14.cloned.1.call-start = ((), (), s32[]{:S(2)}) async-start(), calls=%async_computation.19 | async-start | bytes 5898240 | tf_op jit(solution)/shard_map/all_gather | solution.py:79
  319.8 196.6 %all-gather.18.cloned.1.call-start = ((), (), s32[]{:S(2)}) async-start(), calls=%async_computation.21 | async-start | bytes 5242880 | tf_op jit(solution)/shard_map/all_gather | solution.py:75
  347.2 237.7 %reduce-scatter.11.cloned.1.call-start = ((), (), s32[]{:S(2)}) async-start(), calls=%async_computation.22 | async-start | bytes 5898240 | tf_op jit(solution)/shard_map/reduce_scatter | solution.py:83
  476.9 3.9 copy-start.5
  526.3 60.0 %copy-start.3 = (bf16[1,160,2048]{2,1,0:T(8,128)(2,1)S(1)}, bf16[1,160,2048]{2,1,0:T(8,128)(2,1)}, u32[]{:S(2)}) copy-start(bf16[1,160,2048]{2,1,0:T(8,128)(2,1)} %param.28) | copy-start | bytes 1966084
  526.3 117.6 %all-gather.20.cloned.1.call-start = ((), (), s32[]{:S(2)}) async-start(), calls=%async_computation.23 | async-start | bytes 5898240 | tf_op jit(solution)/shard_map/all_gather | solution.py:79
  584.9 3.1 copy-start.6
  589.2 144.2 %reduce-scatter.13.cloned.1.call-start = ((), (), s32[]{:S(2)}) async-start(), calls=%async_computation.24 | async-start | bytes 5898240 | tf_op jit(solution)/shard_map/reduce_scatter | solution.py:83
  657.1 2.3 copy-start.42
  674.6 58.7 %copy-start.4 = (bf16[160,2048]{1,0:T(8,128)(2,1)S(1)}, bf16[160,2048]{1,0:T(8,128)(2,1)}, u32[]{:S(2)}) copy-start(bf16[160,2048]{1,0:T(8,128)(2,1)} %reduce-scatter.9.cloned.1.call-done) | copy-start | bytes 1966084
  674.7 117.1 %all-gather.22.cloned.1.call-start = ((), (), s32[]{:S(2)}) async-start(), calls=%async_computation.25 | async-start | bytes 5898240 | tf_op jit(solution)/shard_map/all_gather | solution.py:79
  737.1 129.6 %reduce-scatter.23.cloned.1.call-start = ((), (), s32[]{:S(2)}) async-start(), calls=%async_computation.30 | async-start | bytes 5242880 | tf_op jit(solution)/shard_map/reduce_scatter | solution.py:89
  747.3 189.9 %reduce-scatter.21.cloned.1.call-start = ((), (), s32[]{:S(2)}) async-start(), calls=%async_computation.29 | async-start | bytes 10485760 | tf_op jit(solution)/shard_map/reduce_scatter | solution.py:89
  764.3 224.5 %reduce-scatter.19.cloned.1.call-start = ((), (), s32[]{:S(2)}) async-start(), calls=%async_computation.28 | async-start | bytes 1310720 | tf_op jit(solution)/shard_map/reduce_scatter | solution.py:89
  796.5 6.4 copy-start.12
  796.5 6.3 copy-start.17
  802.9 2.2 copy-start.7
  807.5 2.1 copy-start.31
  807.5 2.2 copy-start.33
  807.5 2.2 copy-start.35
  838.9 180.8 %reduce-scatter.17.cloned.1.call-start = ((), (), s32[]{:S(2)}) async-start(), calls=%async_computation.27 | async-start | bytes 4587520 | tf_op jit(solution)/shard_map/reduce_scatter | solution.py:89
  839.0 2.7 copy-start.13
  839.0 10.2 slice-start
  841.6 7.6 copy-start.23
  841.6 7.6 copy-start.25
  841.7 7.5 slice-start.1
  857.1 242.6 %reduce-scatter.15.cloned.1.call-start = ((), (), s32[]{:S(2)}) async-start(), calls=%async_computation.26 | async-start | bytes 5898240 | tf_op jit(solution)/shard_map/reduce_scatter | solution.py:83
  988.7 33.2 %all-to-all-start.5 = ((bf16[8,64,256]{2,1,0:T(8,128)(2,1)}), bf16[8,64,256]{2,1,0:T(8,128)(2,1)S(1)}, u32[]{:S(2)}, u32[]{:S(2)}) async-start(bf16[8,64,256]{2,1,0:T(8,128)(2,1)} %bitcast.218), calls=%async_computation.11 | async-start | bytes 524288 | tf_op jit(solution)/shard_map/all_to_all | solution.py:91
  1022.0 39.3 %all-to-all-start.4 = ((bf16[8,64,896]{2,1,0:T(8,128)(2,1)}), bf16[8,64,896]{2,1,0:T(8,128)(2,1)}, u32[]{:S(2)}, u32[]{:S(2)}) async-start(bf16[8,64,896]{2,1,0:T(8,128)(2,1)} %bitcast.190), calls=%async_computation.9 | async-start | bytes 1835008 | tf_op jit(solution)/shard_map/all_to_all | solution.py:91
  1062.5 37.2 %copy-start.9 = (bf16[160,2048]{1,0:T(8,128)(2,1)S(1)}, bf16[160,2048]{1,0:T(8,128)(2,1)}, u32[]{:S(2)}) copy-start(bf16[160,2048]{1,0:T(8,128)(2,1)} %reduce-scatter.13.cloned.1.call-done) | copy-start | bytes 1966084
  (15 other events, 24.7 us)
Sparse Core Ops, SparseCore 0:
  25.2 31.3 all-gather.11
  58.5 43.9 all-gather.9
  104.1 54.6 all-gather.23
  208.2 107.9 reduce-scatter.8
  317.9 86.8 all-gather.15
  406.9 54.6 all-gather.13
  463.5 52.8 all-gather.17
  526.4 58.3 reduce-scatter.10
  589.3 54.5 all-gather.19
  674.8 58.5 reduce-scatter.12
  737.2 54.5 all-gather.21
  794.6 52.8 reduce-scatter.22
  850.8 86.3 reduce-scatter.20
  940.5 27.7 reduce-scatter.18
  971.4 48.3 reduce-scatter.16
  1022.0 77.6 reduce-scatter.14

commit v2 on v1

v2 whole, which is shorter than its diff:
```python
import functools

import jax
import jax.numpy as jnp
from jax import lax
from jax.experimental import pallas as pl
from jax.experimental.pallas import tpu as pltpu
from jax.sharding import PartitionSpec as P

MESH = pl.DeviceIdType.MESH

HEAD_DIM = 128

rope_base = 500000.0
norm_eps = 1e-06
f32 = jnp.float32
bf16 = jnp.bfloat16


def rms_factor(values):
    return lax.rsqrt(jnp.mean(values * values, axis=-1, keepdims=True) + norm_eps)


def norm_back(grad_normed, raw_values, factor):
    unit_values = raw_values * factor
    return factor * (
        grad_normed - unit_values * jnp.mean(grad_normed * unit_values, axis=-1, keepdims=True)
    )


def rope_tables(positions, head_dim):
    half_dim = head_dim // 2
    steps_f = jnp.arange(half_dim).astype(f32) * (2.0 / head_dim)
    inv_freq = jnp.power(rope_base, -steps_f)
    angle = positions.astype(f32)[:, None] * inv_freq[None, :]
    angle = jnp.concatenate([angle, angle], axis=-1)[:, None, :]
    return (jnp.cos(angle), jnp.sin(angle))


def rotate(values, cosine, sine):
    half_dim = values.shape[-1] // 2
    turned = jnp.concatenate([-values[..., half_dim:], values[..., :half_dim]], axis=-1)
    return values * cosine + turned * sine


def unrotate(grads, cosine, sine):
    half_dim = grads.shape[-1] // 2
    moved = grads * sine
    back_part = jnp.concatenate([moved[..., half_dim:], -moved[..., :half_dim]], axis=-1)
    return grads * cosine + back_part


def allowed_mask(query_pos, key_code):
    key_pos = key_code // 2
    usable = key_code % 2 == 1
    causal = key_pos[None, :] <= query_pos[:, None]
    return causal & (usable[None, :] | (key_pos[None, :] == query_pos[:, None]))


def dot_nn(left, right):
    return jnp.dot(left, right, preferred_element_type=f32)


def dot_nt(left, right):
    return lax.dot_general(left, right, (((1,), (1,)), ((), ())), preferred_element_type=f32)


def dot_tn(left, right):
    return lax.dot_general(left, right, (((0,), (0,)), ((), ())), preferred_element_type=f32)


def across(piece):
    return lax.all_gather(piece, "dp", axis=0, tiled=True)


def dp_sum(grad):
    return lax.psum_scatter(grad, "dp", scatter_dimension=0, tiled=True)


def send_home(summed, ways):
    return lax.all_to_all(summed, "seq", split_axis=0, concat_axis=1, tiled=True)


def split_grads(moved, widths, ways):
    rows = moved.shape[0]
    moved = moved.reshape(rows, ways, sum(widths))
    outs, begin = [], 0
    for width in widths:
        outs.append(moved[:, :, begin : begin + width].reshape(rows, ways * width).astype(f32))
        begin += width
    return outs


class Line:
    def __init__(self, ways):
        self.chips = ways // 2
        self.last = self.chips - 1
        self.me = lax.axis_index("seq")
        self.chip = self.me // 2
        self.core = self.me % 2
        self.sibling = self.me + 1 - 2 * self.core

    def greet(self):
        barrier = pltpu.get_barrier_semaphore()
        has_low = jnp.minimum(self.chip, 1)
        has_high = jnp.minimum(self.last - self.chip, 1)
        pl.semaphore_signal(barrier, inc=1, device_id={"seq": self.sibling}, device_id_type=MESH)

        @pl.when(self.chip > 0)
        def _():
            pl.semaphore_signal(barrier, inc=1, device_id={"seq": self.me - 2}, device_id_type=MESH)

        @pl.when(self.chip < self.last)
        def _():
            pl.semaphore_signal(barrier, inc=1, device_id={"seq": self.me + 2}, device_id_type=MESH)

        pl.semaphore_wait(barrier, 1 + has_low + has_high)


def remote(src, dst, send_sem, recv_sem, device):
    return pltpu.make_async_remote_copy(
        src_ref=src,
        dst_ref=dst,
        send_sem=send_sem,
        recv_sem=recv_sem,
        device_id={"seq": device},
        device_id_type=MESH,
    )


def rows_at(index, count):
    return pl.ds(pl.multiple_of(index * count, count), count)


def each_strip(tok_count, strip, fn):
    def one(i, carry):
        fn(rows_at(i, strip))
        return carry

    lax.fori_loop(0, tok_count // strip, one, 0)


class RowGather:
    def __init__(self, line, tok, row_buf, sems):
        self.line, self.tok, self.buf = line, tok, row_buf
        self.up_send, self.down_send, self.col_recv, self.sib_send, self.sib_recv = sems

    @staticmethod
    def scratch(chips):
        return [pltpu.SemaphoreType.DMA((chips,))] * 5

    def piece(self, src, core):
        return self.buf.at[rows_at(2 * src + core, self.tok)]

    def hop(self, src, device, send):
        piece = self.piece(src, self.line.core)
        return remote(piece, piece, send.at[src], self.col_recv.at[src], device)

    def swap(self, src, core):
        piece = self.piece(src, core)
        return remote(
            piece, piece, self.sib_send.at[src], self.sib_recv.at[src], self.line.sibling
        )

    def start(self):
        line = self.line
        self.forward_up(line.chip)
        self.forward_down(line.chip)
        self.swap(line.chip, line.core).start()

    def forward_up(self, src):
        @pl.when(self.line.chip < self.line.last)
        def _():
            self.hop(src, self.line.me + 2, self.up_send).start()

    def forward_down(self, src):
        @pl.when(self.line.chip > 0)
        def _():
            self.hop(src, self.line.me - 2, self.down_send).start()

    def receive(self, src, up):
        self.hop(src, self.line.sibling, self.up_send).wait_recv()
        if up:
            self.forward_up(src)
        else:
            self.forward_down(src)
        self.swap(src, self.line.core).start()

    def visit(self, use_block):
        line = self.line
        self.swap(line.chip, 1 - line.core).wait_recv()
        use_block(line.chip)
        for away in range(1, line.chips):
            low, high = line.chip - away, line.chip + away

            @pl.when(low >= 0)
            def _():
                self.receive(low, True)

            @pl.when(high <= line.last)
            def _():
                self.receive(high, False)

            for src, there in ((low, low >= 0), (high, high <= line.last)):

                @pl.when(there)
                def _(src=src):
                    self.swap(src, 1 - line.core).wait_recv()
                    use_block(src)

    def finish(self):
        line = self.line
        for src in range(line.chips):
            self.swap(src, line.core).wait_send()

            @pl.when((src <= line.chip) & (line.chip < line.last))
            def _():
                self.hop(src, line.sibling, self.up_send).wait_send()

            @pl.when((src >= line.chip) & (line.chip > 0))
            def _():
                self.hop(src, line.sibling, self.down_send).wait_send()


class RowScatter:
    def __init__(self, line, tok, bufs, sems):
        self.line, self.tok = line, tok
        self.pair, self.sib_in, self.acc = bufs
        self.sib_send, self.sib_recv, self.send, self.recv = sems

    @staticmethod
    def scratch(chips, tok, width):
        return [
            pltpu.VMEM((2 * chips * tok, width), bf16),
            pltpu.VMEM((chips * tok, width), bf16),
            pltpu.VMEM(((chips + 1) * tok, width), bf16),
            pltpu.SemaphoreType.DMA((chips,)),
            pltpu.SemaphoreType.DMA((chips,)),
            pltpu.SemaphoreType.DMA((chips,)),
            pltpu.SemaphoreType.DMA((chips + 1,)),
        ]

    def swap(self, dest):
        tok, line = self.tok, self.line
        return remote(
            self.pair.at[rows_at(2 * dest + 1 - line.core, tok)],
            self.sib_in.at[rows_at(dest, tok)],
            self.sib_send.at[dest],
            self.sib_recv.at[dest],
            line.sibling,
        )

    def hop(self, dest, slot, device):
        tok = self.tok
        return remote(
            self.acc.at[rows_at(dest, tok)],
            self.acc.at[rows_at(slot, tok)],
            self.send.at[dest],
            self.recv.at[slot],
            device,
        )

    def produce(self, dest, left, right, tile):
        rows = rows_at(dest, 2 * self.tok)

        def one(n, carry):
            cols = rows_at(n, tile)
            self.pair[rows, cols] = dot_nt(left[rows, :], right[cols, :]).astype(bf16)
            return carry

        lax.fori_loop(0, right.shape[0] // tile, one, 0)
        self.swap(dest).start()

    def chip_sum(self, dest, strip):
        mine = self.pair[pl.ds((2 * dest + self.line.core) * self.tok + strip.start, strip.size), :]
        other = self.sib_in[pl.ds(dest * self.tok + strip.start, strip.size), :]
        return mine.astype(f32) + other.astype(f32)

    def acc_strip(self, slot, strip):
        return pl.ds(slot * self.tok + strip.start, strip.size)

    def run(self, left, right, tile):
        line, tok = self.line, self.tok
        chips = line.chips
        near_low = 1 - line.chip // (chips // 2)

        def leg(j, first):
            up = near_low if first else 1 - near_low
            dest = up * (chips - j) + (1 - up) * (j - 1)
            step = 2 * up - 1
            return up, dest, step, (dest - line.chip) * step > 0

        def make(j):
            for first in (True, False):
                up, dest, step, there = leg(j, first)

                @pl.when(there)
                def _(dest=dest):
                    self.produce(dest, left, right, tile)

        def pass_on(j):
            for first in (True, False):
                up, dest, step, there = leg(j, first)
                behind = up * line.chip + (1 - up) * (line.last - line.chip)
                target = line.chip + step
                ends = 1 - jnp.minimum((dest - target) * step, 1)
                slot = dest + (1 - up) * ends * (chips - dest)

                @pl.when(there)
                def _(dest=dest, behind=behind, slot=slot, step=step):
                    self.swap(dest).wait_recv()

                    @pl.when(behind > 0)
                    def _():
                        self.hop(dest, dest, line.sibling).wait_recv()

                        def add(strip):
                            at = self.acc_strip(dest, strip)
                            total = self.chip_sum(dest, strip) + self.acc[at, :].astype(f32)
                            self.acc[at, :] = total.astype(bf16)

                        each_strip(tok, 16, add)

                    @pl.when(behind == 0)
                    def _():
                        def put(strip):
                            at = self.acc_strip(dest, strip)
                            self.acc[at, :] = self.chip_sum(dest, strip).astype(bf16)

                        each_strip(tok, 16, put)

                    self.hop(dest, slot, line.me + 2 * step).start()

        make(1)
        for j in range(1, chips):
            if j + 1 < chips:
                make(j + 1)
            else:
                self.produce(line.chip, left, right, tile)
            pass_on(j)
        self.swap(line.chip).wait_recv()

        @pl.when(line.chip > 0)
        def _():
            self.hop(line.chip, line.chip, line.sibling).wait_recv()

        @pl.when(line.chip == 0)
        def _():
            self.acc[rows_at(line.chip, tok), :] = jnp.zeros((tok, self.acc.shape[1]), bf16)

        @pl.when(line.chip < line.last)
        def _():
            self.hop(line.chip, chips, line.sibling).wait_recv()

        @pl.when(line.chip == line.last)
        def _():
            self.acc[rows_at(chips, tok), :] = jnp.zeros((tok, self.acc.shape[1]), bf16)

    def total(self, strip):
        low = self.acc[self.acc_strip(self.line.chip, strip), :].astype(f32)
        high = self.acc[self.acc_strip(self.line.chips, strip), :].astype(f32)
        return self.chip_sum(self.line.chip, strip) + (low + high)

    def finish(self):
        line = self.line
        for dest in range(line.chips):
            self.swap(dest).wait_send()

            @pl.when(line.chip != dest)
            def _():
                self.hop(dest, dest, line.sibling).wait_send()


def mean_rows(values):
    return jnp.sum(values, axis=-1, keepdims=True) * (1.0 / values.shape[-1])


def call(kernel, outs, scratch, args, ident, cost=1):
    return pl.pallas_call(
        kernel,
        out_shape=outs,
        in_specs=[pl.BlockSpec(memory_space=pltpu.VMEM)] * len(args),
        out_specs=[pl.BlockSpec(memory_space=pltpu.VMEM)] * len(outs),
        scratch_shapes=scratch,
        cost_estimate=pl.CostEstimate(
            flops=cost * 10**9, transcendentals=0, bytes_accessed=cost * 3 * 10**6
        ),
        compiler_params=pltpu.CompilerParams(
            collective_id=ident, has_side_effects=True, vmem_limit_bytes=60 * 2**20
        ),
    )(*args)


def shape(dims, kind):
    return jax.ShapeDtypeStruct(dims, kind)


def gather_project(rows, codes, weights, ways, ident):
    tok, width = rows.shape
    cols = weights.shape[1]

    def kernel(rows_ref, code_ref, w_ref, all_ref, codes_ref, prod_ref, code_send, code_recv, *sems):
        line = Line(ways)
        me = line.me
        barrier = pltpu.get_barrier_semaphore()
        for off in range(1, ways):
            pl.semaphore_signal(
                barrier, inc=1, device_id={"seq": (me + off) % ways}, device_id_type=MESH
            )
        pl.semaphore_wait(barrier, ways - 1)
        gather = RowGather(line, tok, all_ref, sems)
        all_ref[rows_at(me, tok), :] = rows_ref[...]
        gather.start()
        codes_ref[me] = code_ref[...]

        def tell(off):
            return remote(
                code_ref, codes_ref.at[me], code_send.at[off], code_recv.at[off], (me + off) % ways
            )

        for off in range(1, ways):
            tell(off).start()

        def use(chip):
            at = rows_at(chip, 2 * tok)

            def one(n, carry):
                here = rows_at(n, 256)
                prod_ref[at, here] = dot_nn(all_ref[at, :], w_ref[:, here])
                return carry

            lax.fori_loop(0, cols // 256, one, 0)

        gather.visit(use)
        gather.finish()
        for off in range(1, ways):
            tell(off).wait()

    return call(
        kernel,
        [
            shape((ways * tok, width), bf16),
            shape((ways,) + codes.shape, jnp.int32),
            shape((ways * tok, cols), f32),
        ],
        [pltpu.SemaphoreType.DMA((ways,))] * 2 + RowGather.scratch(ways // 2),
        [rows, codes, weights],
        ident,
        55,
    )


def attn_out_to_ff(attn_low, m_out, m_gu, token_rows, gain_row, ways, ident):
    tok, width = token_rows.shape
    own_ff = m_gu.shape[1] // 2
    row = ways * tok

    def kernel(left, right, w_ref, x_ref, gain_ref, branch_ref, in_ref, all_ref, gu_ref, mix_ref, *rest):
        line = Line(ways)
        line.greet()
        scatter = RowScatter(line, tok, rest[:3], rest[3:7])
        gather = RowGather(line, tok, all_ref, rest[7:])
        scatter.run(left, right, 256)

        def settle(strip):
            branch = scatter.total(strip)
            factor = lax.rsqrt(mean_rows(branch * branch) + norm_eps)
            hidden = x_ref[strip, :].astype(f32) + branch * factor * gain_ref[...]
            branch_ref[strip, :] = branch
            in_ref[strip, :] = hidden
            all_ref[pl.ds(line.me * tok + strip.start, strip.size), :] = hidden.astype(bf16)

        each_strip(tok, 16, settle)
        gather.start()

        def use(chip):
            at = rows_at(chip, 2 * tok)

            def one(n, carry):
                here, there = rows_at(n, 256), pl.ds(pl.multiple_of(own_ff + n * 256, 256), 256)
                block = all_ref[at, :]
                gate = dot_nn(block, w_ref[:, here])
                up = dot_nn(block, w_ref[:, there])
                gu_ref[at, here] = gate.astype(bf16)
                gu_ref[at, there] = up.astype(bf16)
                mix_ref[at, here] = (gate * jax.nn.sigmoid(gate) * up).astype(bf16)
                return carry

            lax.fori_loop(0, own_ff // 256, one, 0)

        gather.visit(use)
        gather.finish()
        scatter.finish()

    return call(
        kernel,
        [
            shape((tok, width), f32),
            shape((tok, width), f32),
            shape((row, width), bf16),
            shape((row, 2 * own_ff), bf16),
            shape((row, own_ff), bf16),
        ],
        RowScatter.scratch(ways // 2, tok, width) + RowGather.scratch(ways // 2),
        [attn_low, m_out, m_gu, token_rows, gain_row],
        ident,
        105,
    )


def ff_turn(mixed_low, m_down, gate_up, hidden_in, grad_out, gain_row, ways, ident):
    tok, width = hidden_in.shape
    own_ff = m_down.shape[1]
    row = ways * tok

    def kernel(left, w_ref, gu_ref, in_ref, go_ref, gain_ref, out_ref, gg_ref, all_ref, dgu_ref, *rest):
        line = Line(ways)
        line.greet()
        scatter = RowScatter(line, tok, rest[:3], rest[3:7])
        gather = RowGather(line, tok, all_ref, rest[7:])
        scatter.run(left, w_ref, 256)
        gg_ref[...] = jnp.zeros_like(gg_ref)

        def settle(strip):
            mlp = scatter.total(strip)
            factor = lax.rsqrt(mean_rows(mlp * mlp) + norm_eps)
            unit = mlp * factor
            grad = go_ref[strip, :].astype(f32)
            out_ref[strip, :] = (in_ref[strip, :] + unit * gain_ref[...]).astype(bf16)
            terms = grad * unit
            gg_ref[...] += terms[:8] + terms[8:]
            lifted = grad * gain_ref[...]
            back = factor * (lifted - unit * mean_rows(lifted * unit))
            all_ref[pl.ds(line.me * tok + strip.start, strip.size), :] = back.astype(bf16)

        each_strip(tok, 16, settle)
        gather.start()

        def use(chip):
            at = rows_at(chip, 2 * tok)

            def one(n, carry):
                here, there = rows_at(n, 256), pl.ds(pl.multiple_of(own_ff + n * 256, 256), 256)
                grad = dot_nn(all_ref[at, :], w_ref[:, here])
                gate, up = gu_ref[at, here].astype(f32), gu_ref[at, there].astype(f32)
                sigma = jax.nn.sigmoid(gate)
                dgu_ref[at, here] = (grad * up * sigma * (1.0 + gate * (1.0 - sigma))).astype(bf16)
                dgu_ref[at, there] = (grad * gate * sigma).astype(bf16)
                return carry

            lax.fori_loop(0, own_ff // 256, one, 0)

        gather.visit(use)
        gather.finish()
        scatter.finish()

    return call(
        kernel,
        [
            shape((tok, width), bf16),
            shape((8, width), f32),
            shape((row, width), bf16),
            shape((row, 2 * own_ff), bf16),
        ],
        RowScatter.scratch(ways // 2, tok, width) + RowGather.scratch(ways // 2),
        [mixed_low, m_down, gate_up, hidden_in, grad_out, gain_row],
        ident,
        105,
    )


def ff_to_attn_back(grad_gu, m_gu, m_out, branch, grad_out, gain_row, ways, ident):
    tok, width = branch.shape
    own_feat = m_out.shape[1]
    row = ways * tok

    def kernel(left, right, w_ref, br_ref, go_ref, gain_ref, gh_ref, gg_ref, all_ref, ga_ref, *rest):
        line = Line(ways)
        line.greet()
        scatter = RowScatter(line, tok, rest[:3], rest[3:7])
        gather = RowGather(line, tok, all_ref, rest[7:])
        scatter.run(left, right, 256)
        gg_ref[...] = jnp.zeros_like(gg_ref)

        def settle(strip):
            grad = scatter.total(strip) + go_ref[strip, :].astype(f32)
            branch = br_ref[strip, :]
            factor = lax.rsqrt(mean_rows(branch * branch) + norm_eps)
            unit = branch * factor
            gh_ref[strip, :] = grad
            terms = grad * unit
            gg_ref[...] += terms[:8] + terms[8:]
            lifted = grad * gain_ref[...]
            back = factor * (lifted - unit * mean_rows(lifted * unit))
            all_ref[pl.ds(line.me * tok + strip.start, strip.size), :] = back.astype(bf16)

        each_strip(tok, 16, settle)
        gather.start()

        def use(chip):
            at = rows_at(chip, 2 * tok)
            ga_ref[at, :] = dot_nn(all_ref[at, :], w_ref[...])

        gather.visit(use)
        gather.finish()
        scatter.finish()

    return call(
        kernel,
        [
            shape((tok, width), f32),
            shape((8, width), f32),
            shape((row, width), bf16),
            shape((row, own_feat), f32),
        ],
        RowScatter.scratch(ways // 2, tok, width) + RowGather.scratch(ways // 2),
        [grad_gu, m_gu, m_out, branch, grad_out, gain_row],
        ident,
        105,
    )


def project_back(grad_qkv, m_qkv, grad_hidden, ways, ident):
    tok, width = grad_hidden.shape

    def kernel(left, right, gh_ref, out_ref, *rest):
        line = Line(ways)
        line.greet()
        scatter = RowScatter(line, tok, rest[:3], rest[3:7])
        scatter.run(left, right, 256)

        def settle(strip):
            out_ref[strip, :] = (gh_ref[strip, :] + scatter.total(strip)).astype(bf16)

        each_strip(tok, 16, settle)
        scatter.finish()

    return call(
        kernel,
        [shape((tok, width), bf16)],
        RowScatter.scratch(ways // 2, tok, width),
        [grad_qkv, m_qkv, grad_hidden],
        ident,
        55,
    )[0]


def exchange(sources, ways, ident, cost):
    rows = sources[0].shape[0]
    widths = [a.shape[1] // ways for a in sources]
    begins = [sum(widths[:i]) for i in range(len(widths))]
    count = len(sources)

    def kernel(*refs):
        ins, out_ref, send, recv, local = refs[:count], *refs[count:]
        me = lax.axis_index("seq")
        barrier = pltpu.get_barrier_semaphore()

        def greet(off, carry):
            pl.semaphore_signal(
                barrier, inc=1, device_id={"seq": (me + off) % ways}, device_id_type=MESH
            )
            return carry

        def move(off, i):
            dest = (me + off) % ways
            return remote(
                ins[i].at[:, rows_at(dest, widths[i])],
                out_ref.at[rows_at(me, rows), pl.ds(begins[i], widths[i])],
                send.at[off * count + i],
                recv.at[off * count + i],
                dest,
            )

        def keep(i):
            return pltpu.make_async_copy(
                ins[i].at[:, rows_at(me, widths[i])],
                out_ref.at[rows_at(me, rows), pl.ds(begins[i], widths[i])],
                local.at[i],
            )

        def each(what):
            def one(off, carry):
                for i in range(count):
                    what(move(off, i))
                return carry

            lax.fori_loop(1, ways, one, 0)

        for i in range(count):
            keep(i).start()
        lax.fori_loop(1, ways, greet, 0)
        pl.semaphore_wait(barrier, ways - 1)
        each(lambda copy: copy.start())
        for i in range(count):
            keep(i).wait()
        each(lambda copy: copy.wait())

    return pl.pallas_call(
        kernel,
        out_shape=shape((ways * rows, sum(widths)), bf16),
        in_specs=[pl.BlockSpec(memory_space=pl.ANY)] * count,
        out_specs=pl.BlockSpec(memory_space=pl.ANY),
        scratch_shapes=[
            pltpu.SemaphoreType.DMA((ways * count,)),
            pltpu.SemaphoreType.DMA((ways * count,)),
            pltpu.SemaphoreType.DMA((count,)),
        ],
        cost_estimate=pl.CostEstimate(
            flops=cost * 10**9, transcendentals=0, bytes_accessed=cost * 3 * 10**6
        ),
        compiler_params=pltpu.CompilerParams(collective_id=ident, has_side_effects=True),
    )(*sources)


def line_sum(terms, ways, ident):
    def kernel(terms_ref, out_ref, slots, send, recv):
        me = lax.axis_index("seq")
        barrier = pltpu.get_barrier_semaphore()
        for off in range(1, ways):
            pl.semaphore_signal(
                barrier, inc=1, device_id={"seq": (me + off) % ways}, device_id_type=MESH
            )
        pl.semaphore_wait(barrier, ways - 1)
        for off in range(1, ways):
            remote(
                terms_ref, slots.at[off], send.at[off], recv.at[off], (me + off) % ways
            ).start()
        total = terms_ref[...]
        for off in range(1, ways):
            remote(terms_ref, slots.at[off], send.at[off], recv.at[off], (me + off) % ways).wait_recv()
            total = total + slots[off]
        out_ref[...] = total
        for off in range(1, ways):
            remote(terms_ref, slots.at[off], send.at[off], recv.at[off], (me + off) % ways).wait_send()

    return call(
        kernel,
        [shape(terms.shape, f32)],
        [
            pltpu.VMEM((ways,) + terms.shape, f32),
            pltpu.SemaphoreType.DMA((ways,)),
            pltpu.SemaphoreType.DMA((ways,)),
        ],
        [terms],
        ident,
        8,
    )[0]


def body(
    tokens,
    w_query,
    w_key,
    w_value,
    w_out,
    w_gate,
    w_up,
    w_down,
    gain_query,
    gain_key,
    gain_attn,
    gain_mlp,
    cotangent,
    key_mask,
    lengths,
    tract_order,
):
    ways = lax.axis_size("seq")
    me = lax.axis_index("seq")
    token_rows = tokens[0]
    tok_count, feat_width = token_rows.shape
    ff_width = w_gate.shape[1]
    own_feat = feat_width // ways
    own_heads = own_feat // HEAD_DIM
    own_ff = ff_width // ways
    row_len = tok_count * ways
    score_scale = HEAD_DIM ** (-0.5)
    half_len = tok_count // 2
    order_pair = tract_order[0]
    slot_index = jnp.arange(tok_count, dtype=jnp.int32)
    local_pos = (
        jnp.where(slot_index < half_len, order_pair[0], order_pair[1]) * half_len
        + slot_index % half_len
    )
    key_ok = ((key_mask[0] == 1) & (local_pos < lengths[0])).astype(jnp.int32)

    gain_local = jnp.stack([gain_query, gain_key, gain_attn, gain_mlp], axis=1)
    gain_pad = jnp.pad(gain_local, ((0, 0), (0, HEAD_DIM - 4)))
    gain_all = jnp.tile(gain_pad, (1, ways))
    p_qkv = exchange([w_query, w_key, w_value], ways, 8, 20)
    m_qkv = across(p_qkv)
    p_qkv, w_gate, w_up, w_out_t, w_down_t, gain_all = lax.optimization_barrier(
        (p_qkv, w_gate, w_up, jnp.transpose(w_out), jnp.transpose(w_down), gain_all)
    )
    p_out = exchange([w_out_t, gain_all], ways, 9, 8)
    p_gu = exchange([w_gate, w_up], ways, 10, 40)
    p_down = exchange([w_down_t], ways, 11, 20)
    m_out, m_gu, m_down = across(p_out), across(p_gu), across(p_down)
    gains = jnp.transpose(m_out[:, own_feat:])[:8].astype(f32)
    m_out = m_out[:, :own_feat]
    gain_q = lax.dynamic_slice_in_dim(gains[0], me * own_feat, own_feat, 0)
    gain_k = lax.dynamic_slice_in_dim(gains[1], me * own_feat, own_feat, 0)

    code_pad = -tok_count % HEAD_DIM
    local_code = jnp.pad(local_pos * 2 + key_ok, (0, code_pad))[None]
    x_row, codes, qkv = gather_project(token_rows, local_code, m_qkv, ways, 1)
    key_code = codes[:, 0, :tok_count].reshape(row_len)
    pos = key_code // 2
    q_raw, k_raw, v_raw = (qkv[:, i * own_feat : (i + 1) * own_feat] for i in range(3))
    squares = line_sum(
        jnp.stack([jnp.sum(q_raw * q_raw, axis=-1), jnp.sum(k_raw * k_raw, axis=-1)]), ways, 2
    )
    factors = lax.rsqrt(squares / feat_width + norm_eps)
    q_factor, k_factor = factors[0][:, None], factors[1][:, None]
    cosine, sine = rope_tables(pos, HEAD_DIM)
    head_shape = (row_len, own_heads, HEAD_DIM)
    query_low = rotate((q_raw * q_factor * gain_q).reshape(head_shape), cosine, sine).astype(bf16)
    key_low = rotate((k_raw * k_factor * gain_k).reshape(head_shape), cosine, sine).astype(bf16)
    value_low = v_raw.astype(bf16).reshape(head_shape)

    mask = allowed_mask(pos, key_code)[None]
    scores = jnp.einsum("qhd,khd->hqk", query_low, key_low, preferred_element_type=f32) * score_scale
    expo = jnp.where(mask, jnp.exp(scores), 0.0)
    weight_sum = jnp.transpose(jnp.sum(expo, axis=-1))[:, :, None]
    expo_low = expo.astype(bf16)
    attn = jnp.einsum("hqk,khd->qhd", expo_low, value_low, preferred_element_type=f32) / weight_sum
    attn_low = attn.astype(bf16).reshape(row_len, own_feat)

    branch, hidden_in, hidden_low, gate_up, mixed_low = attn_out_to_ff(
        attn_low, m_out, m_gu, token_rows, gains[2:3], ways, 3
    )
    layer_out, grad_gain_mlp, grad_mlp, grad_gu = ff_turn(
        mixed_low, m_down, gate_up, hidden_in, cotangent[0], gains[3:4], ways, 4
    )
    d_down = dot_tn(grad_mlp, mixed_low).astype(bf16)
    d_gu = dot_tn(hidden_low, grad_gu).astype(bf16)
    grad_gu, d_down, d_gu = lax.optimization_barrier((grad_gu, d_down, d_gu))
    d_down = dp_sum(d_down)
    d_gu = dp_sum(d_gu)
    grad_hidden, grad_gain_attn, grad_branch, grad_attn = ff_to_attn_back(
        grad_gu, m_gu, m_out, branch, cotangent[0], gains[2:3], ways, 5
    )
    grad_attn, d_down = lax.optimization_barrier((grad_attn, d_down))
    d_down = send_home(d_down, ways)
    grad_attn = grad_attn.reshape(head_shape)
    grad_num = (grad_attn / weight_sum).astype(bf16)
    drop = jnp.transpose(jnp.sum(grad_attn * attn, axis=-1) / weight_sum[:, :, 0])
    grad_expo = jnp.einsum("qhd,khd->hqk", grad_num, value_low, preferred_element_type=f32)
    grad_scores = (expo * (grad_expo - drop[:, :, None])).astype(bf16)
    grad_q = (
        jnp.einsum("hqk,khd->qhd", grad_scores, key_low, preferred_element_type=f32) * score_scale
    )
    grad_k = (
        jnp.einsum("hqk,qhd->khd", grad_scores, query_low, preferred_element_type=f32) * score_scale
    )
    grad_v = jnp.einsum("hqk,qhd->khd", expo_low, grad_num, preferred_element_type=f32)
    grad_q_norm = unrotate(grad_q, cosine, sine).reshape(row_len, own_feat)
    grad_k_norm = unrotate(grad_k, cosine, sine).reshape(row_len, own_feat)
    q_unit, k_unit = q_raw * q_factor, k_raw * k_factor
    grad_gain_query = jnp.sum(grad_q_norm * q_unit, axis=0)
    grad_gain_key = jnp.sum(grad_k_norm * k_unit, axis=0)
    c_q, c_k = grad_q_norm * gain_q, grad_k_norm * gain_k
    terms = jnp.stack([jnp.sum(c_q * q_unit, axis=-1), jnp.sum(c_k * k_unit, axis=-1)])
    terms, d_down, d_gu = lax.optimization_barrier((terms, d_down, d_gu))
    means = line_sum(terms, ways, 6) / feat_width
    dw_down = split_grads(d_down, [own_ff], ways)
    dw_gu = split_grads(send_home(d_gu, ways), [own_ff, own_ff], ways)
    grad_q_raw = q_factor * (c_q - q_unit * means[0][:, None])
    grad_k_raw = k_factor * (c_k - k_unit * means[1][:, None])
    grad_qkv = jnp.concatenate(
        [grad_q_raw, grad_k_raw, grad_v.reshape(row_len, own_feat)], axis=1
    ).astype(bf16)

    own_slot = jnp.zeros((2, feat_width), f32)
    own_slot = lax.dynamic_update_slice(
        own_slot, jnp.stack([grad_gain_query, grad_gain_key]), (0, me * own_feat)
    )
    gain_terms = jnp.concatenate(
        [
            own_slot,
            jnp.sum(grad_gain_attn, axis=0, keepdims=True),
            jnp.sum(grad_gain_mlp, axis=0, keepdims=True),
        ]
    )
    gain_columns = jnp.pad(jnp.transpose(gain_terms), ((0, 0), (0, HEAD_DIM - 4)))
    d_attn = jnp.concatenate(
        [dot_tn(x_row, grad_qkv), dot_tn(grad_branch, attn_low), gain_columns], axis=1
    ).astype(bf16)
    grad_qkv, d_attn = lax.optimization_barrier((grad_qkv, d_attn))
    dw_qkv = split_grads(
        send_home(dp_sum(d_attn), ways), [own_feat] * 4 + [HEAD_DIM], ways
    )
    grad_tokens = project_back(grad_qkv, m_qkv, grad_hidden, ways, 7)
    gain_grads = jnp.sum(dw_qkv[4].reshape(-1, ways, HEAD_DIM), axis=1)
    gain_grads = jnp.transpose(gain_grads[:, :8])
    return (
        layer_out[None],
        grad_tokens[None],
        dw_qkv[0],
        dw_qkv[1],
        dw_qkv[2],
        jnp.transpose(dw_qkv[3]),
        dw_gu[0],
        dw_gu[1],
        jnp.transpose(dw_down[0]),
        gain_grads[0],
        gain_grads[1],
        gain_grads[2],
        gain_grads[3],
    )


def solution(mesh):
    both = ("dp", "seq")
    in_specs = (
        P("dp", "seq", None),
        P(both, None),
        P(both, None),
        P(both, None),
        P(None, both),
        P(both, None),
        P(both, None),
        P(None, both),
        P(both),
        P(both),
        P(both),
        P(both),
        P("dp", "seq", None),
        P("dp", "seq"),
        P("dp"),
        P("dp", "seq"),
    )
    out_specs = (
        P("dp", "seq", None),
        P("dp", "seq", None),
        P(both, None),
        P(both, None),
        P(both, None),
        P(None, both),
        P(both, None),
        P(both, None),
        P(None, both),
        P(both),
        P(both),
        P(both),
        P(both),
    )
    return jax.shard_map(body, mesh=mesh, in_specs=in_specs, out_specs=out_specs, check_vma=False)
```

time: 1120 us -> 792 us (0.71)
  Pallas kernels: 0 us -> 591 us
  waiting for transfers between devices: 573 us -> 21.2 us
  blocking collectives: 292 us -> 0 us
  matrix products: 138 us -> 65.9 us
    pallas_call x0 -> x11, Pallas kernels: none -> 591 us  [the longest x7 481 us: call(): pl.pallas_call(kernel, out_shape=outs, in_specs=[pl.BlockSpec(memory_spac...]
    all_gather x8 -> x4, waiting for transfers between devices: 318 us -> 0.04 us  [across(): return lax.all_gather(piece, 'dp', axis=0, tiled=True)]
    all_to_all x6 -> x0, blocking collectives: 240 us -> none  [the longest x4 155 us: collect(): lax.all_to_all(matrix, 'seq', split_axis=1, concat_axis=0, tiled=True)]
    reduce_scatter x8 -> x3, waiting for transfers between devices: 227 us -> 0.02 us  [dp_sum(): return lax.psum_scatter(grad, 'dp', scatter_dimension=0, tiled=True)]
    dot_general x8 -> x0, matrix products: 77.8 us -> none  [the longest x4 40.8 us: dot_nn(): return jnp.dot(left, right, preferred_element_type=f32)]
    psum x2 -> x0, blocking collectives: 45.3 us -> none  [the longest x1 23.1 us: body(): lax.psum(jnp.stack([jnp.sum(c_q * q_unit, axis=-1), jnp.sum(c_k * k_unit,...]
    unnamed x99 -> x70, local copies, waits for them, and re-layouts: 21.2 us -> 3.91 us
    all_to_all x2 -> x3, starting transfers between devices: 11.8 us -> 23.3 us  [send_home(): lax.all_to_all(summed, 'seq', split_axis=0, concat_axis=1, tiled=True)]
  transfers between devices with their start and end apart: 18 -> 10, of which waited for: 14 -> 1; matrix products, arithmetic and copies ran while one was open for 11% -> 10% of each run, Pallas kernels for 0% -> 56%
where the time goes in v2:
time: 792 us; the launch traced here: 783 us
  Pallas kernels  591 us (75%)
  matrix products  65.9 us (8%)
  local copies, waits for them, and re-layouts  33.7 us (4%)
  other arithmetic  31.2 us (4%)
  starting transfers between devices  23.8 us (3%)
  waiting for transfers between devices  21.2 us (3%)
  between operations  16 us (2%)
    pallas_call x7, Pallas kernels, call(): pl.pallas_call(kernel, out_shape=outs, in_specs=[pl.BlockSpec(memory_spac...  481 us
    pallas_call x4, Pallas kernels, exchange(): pl.pallas_call(kernel, out_shape=shape((ways * rows, sum(widths)), bf16),...  110 us
    dot_general x4, matrix products, dot_tn(): lax.dot_general(left, right, (((0,), (0,)), ((), ())), preferred_element_...  39 us
    all_to_all x3, starting transfers between devices, send_home(): lax.all_to_all(summed, 'seq', split_axis=0, concat_axis=1, tiled=True)  23.3 us
    all_to_all x3, waiting for transfers between devices, send_home(): lax.all_to_all(summed, 'seq', split_axis=0, concat_axis=1, tiled=True)  19.8 us
  transfers between devices with their start and end apart: 10, of which 1 were waited for; matrix products, arithmetic and copies ran while one was open for 10% of the time, Pallas kernels for 56%

profile of v2, /device:TPU:9, one launch (start us, length us, event | category | flops | bytes accessed | tf_op | source)
XLA Modules:
  0.0 782.6 jit_solution(13986283529508521072)
XLA Ops:
  8.8 21.7 %shard_map.255 = bf16[512,768]{1,0:T(8,128)(2,1)} custom-call(bf16[64,2048]{1,0:T(8,128)(2,1)} %refs_0_.1, bf16[64,2048]{1,0:T(8,128)(2,1)} %refs_1_.1, bf16[64,2048]{1,0:T(8,128)(2,1)} %refs_2_.1), custom_call_target="tpu_custom_call" | custom-call | flops 20000000000 | bytes 60000000 | tf_op jit(solution)/shard_map/pallas_call | solution.py:699
  30.5 12.5 %shard_map.258 = bf16[512,384]{1,0:T(8,128)(2,1)} custom-call(bf16[64,2048]{1,0:T(8,128)(2,1)} %bitcast.155, bf16[64,1024]{1,0:T(8,128)(2,1)} %bitcast.136), custom_call_target="tpu_custom_call" | custom-call | flops 8000000000 | bytes 24000000 | tf_op jit(solution)/shard_map/pallas_call | solution.py:699
  43.0 1.9 copy.161
  45.7 49.3 %shard_map.259 = bf16[512,2048]{1,0:T(8,128)(2,1)} custom-call(bf16[64,8192]{1,0:T(8,128)(2,1)} %refs_0_.2, bf16[64,8192]{1,0:T(8,128)(2,1)} %refs_1_.2), custom_call_target="tpu_custom_call" | custom-call | flops 40000000000 | bytes 120000000 | tf_op jit(solution)/shard_map/pallas_call | solution.py:699
  95.1 26.5 %shard_map.261 = bf16[512,1024]{1,0:T(8,128)(2,1)} custom-call(bf16[64,8192]{1,0:T(8,128)(2,1)} %bitcast.150), custom_call_target="tpu_custom_call" | custom-call | flops 20000000000 | bytes 60000000 | tf_op jit(solution)/shard_map/pallas_call | solution.py:699
  123.1 1.3 fusion.35
  124.9 1.2 slice_bitcast_fusion
  126.8 1.3 copy.173.right.w_ref
  128.1 51.4 %shard_map.256 = (bf16[1280,2048]{1,0:T(8,128)(2,1)}, s32[8,1,256]{2,1,0:T(1,128)}, f32[1280,768]{1,0:T(8,128)}) custom-call(bf16[160,2048]{1,0:T(8,128)(2,1)} %bitcast.151, s32[1,256]{1,0:T(1,128)} %bitcast.145, bf16[2048,768]{1,0:T(8,128)(2,1)} %all-gather.5.cloned.1.call-done.w_ref.right), custom_call_target="tpu_custom_call" | custom-call | flops 54999998464 | bytes 165000000 | tf_op jit(solution)/shard_map/pallas_call | solution.py:379
  180.3 2.1 multiply_reduce_fusion.6
  183.1 13.6 %shard_map.257 = f32[2,1280]{1,0:T(2,128)} custom-call(f32[2,1280]{1,0:T(2,128)} %pad_maximum_fusion.2.terms_ref), custom_call_target="tpu_custom_call" | custom-call | flops 8000000000 | bytes 24000000 | tf_op jit(solution)/shard_map/pallas_call | solution.py:379
  197.4 1.9 fusion.22
  199.3 1.7 copy.207
  202.0 1.7 copy.206
  203.9 3.3 broadcast_multiply_fusion.3
  207.3 2.0 or_and_fusion
  209.7 3.5 fusion.41
  213.3 5.4 fusion.42
  218.6 1.1 copy.202.left
  219.7 102.4 %shard_map.260 = (f32[160,2048]{1,0:T(8,128)}, f32[160,2048]{1,0:T(8,128)}, bf16[1280,2048]{1,0:T(8,128)(2,1)}, bf16[1280,2048]{1,0:T(8,128)(2,1)}, bf16[1280,1024]{1,0:T(8,128)(2,1)}) custom-call(bf16[1280,256]{1,0:T(8,128)(2,1)} %copy.202.left, bf16[2048,256]{1,0:T(8,128)(2,1)} %copy.173.right.w_ref, ...), custom_call_target="tpu_custom_call" | custom-call | flops 105000001536 | bytes 315000000 | tf_op jit(solution)/shard_map/pallas_call | solution.py:379
  322.2 111.8 %shard_map.262 = (bf16[160,2048]{1,0:T(8,128)(2,1)}, f32[8,2048]{1,0:T(8,128)}, bf16[1280,2048]{1,0:T(8,128)(2,1)}, bf16[1280,2048]{1,0:T(8,128)(2,1)}) custom-call(bf16[1280,1024]{1,0:T(8,128)(2,1)} %get-tuple-element.50.left, bf16[2048,1024]{1,0:T(8,128)(2,1)} %all-gather.11.cloned.1.call-done.w_ref, bf16[1280,2048]{1,0:T(8,128)(2,1)} %get-tuple-element.52.gu_ref, ...), custom_call_target="tpu_custom_call" | custom-call | flops 105000001536 | bytes 315000000 | tf_op jit(solution)/shard_map/pallas_call | solution.py:379
  434.0 9.8 %convolution_convert_fusion.1 = bf16[2048,1024]{1,0:T(8,128)(2,1)} fusion(bf16[1280,2048]{1,0:T(8,128)(2,1)} %get-tuple-element.56, bf16[1280,1024]{1,0:T(8,128)(2,1)S(1)} %copy-done.32), kind=kOutput, calls=%fused_computation.10 | convolution fusion | flops 5370806272 | bytes 12058624 | tf_op jit(solution)/shard_map/dot_general | solution.py:69
  443.8 16.7 %convolution_convert_fusion = bf16[2048,2048]{1,0:T(8,128)(2,1)} fusion(bf16[1280,2048]{1,0:T(8,128)(2,1)} %get-tuple-element.57, bf16[1280,2048]{1,0:T(8,128)(2,1)} %get-tuple-element.58.left), kind=kOutput, calls=%fused_computation.7 | convolution fusion | flops 10741612544 | bytes 18874368 | tf_op jit(solution)/shard_map/dot_general | solution.py:69
  461.1 113.4 %shard_map.263 = (f32[160,2048]{1,0:T(8,128)}, f32[8,2048]{1,0:T(8,128)}, bf16[1280,2048]{1,0:T(8,128)(2,1)}, f32[1280,256]{1,0:T(8,128)}) custom-call(bf16[1280,2048]{1,0:T(8,128)(2,1)} %get-tuple-element.58.left, bf16[2048,2048]{1,0:T(8,128)(2,1)} %all-gather.9.cloned.1.call-done.w_ref.right, bf16[2048,256]{1,0:T(8,128)(2,1)} %copy.173.right.w_ref, ...), custom_call_target="tpu_custom_call" | custom-call | flops 105000001536 | bytes 315000000 | tf_op jit(solution)/shard_map/pallas_call | solution.py:379
  575.4 5.1 convolution_convert_fusion.3
  581.0 11.5 %all-to-all-start = ((bf16[8,64,1024]{2,1,0:T(8,128)(2,1)}), bf16[8,64,1024]{2,1,0:T(8,128)(2,1)}, u32[]{:S(2)}, u32[]{:S(2)}) async-start(bf16[8,64,1024]{2,1,0:T(8,128)(2,1)} %bitcast.125), calls=%async_computation.1 | async-start | bytes 2097152 | tf_op jit(solution)/shard_map/all_to_all | solution.py:81
  593.2 7.6 fusion.1
  600.9 2.2 convolution_bitcast_fusion
  603.1 1.2 broadcast_multiply_fusion.1
  605.5 1.9 maximum_add_fusion
  607.4 1.7 copy.203
  609.1 3.2 copy.204
  612.4 2.7 multiply_reduce_fusion.1
  615.2 7.0 fusion.14
  623.9 2.3 copy.211
  626.2 7.0 shard_map.264
  634.0 2.4 multiply_convert_fusion.1
  636.4 1.4 pad_maximum_fusion.left
  637.8 7.5 convolution_convert_fusion.2
  645.3 2.4 fusion.3
  647.7 5.6 all-to-all-start.2
  653.3 81.4 %shard_map.265 = bf16[160,2048]{1,0:T(8,128)(2,1)} custom-call(bf16[1280,768]{1,0:T(8,128)(2,1)} %pad_maximum_fusion.left, bf16[2048,768]{1,0:T(8,128)(2,1)} %all-gather.5.cloned.1.call-done.w_ref.right, f32[160,2048]{1,0:T(8,128)} %get-tuple-element.71.gh_ref), custom_call_target="tpu_custom_call" | custom-call | flops 54999998464 | bytes 165000000 | tf_op jit(solution)/shard_map/pallas_call | solution.py:379
  734.8 2.4 copy.187
  737.2 6.2 all-to-all-start.1
  743.4 2.7 convert_bitcast_fusion
  746.5 1.5 copy.216
  748.0 1.5 copy.217
  749.5 19.8 %all-to-all-done.1 = bf16[8,64,1152]{2,1,0:T(8,128)(2,1)S(1)} async-done(((bf16[8,64,1152]{2,1,0:T(8,128)(2,1)}), bf16[8,64,1152]{2,1,0:T(8,128)(2,1)S(1)}, u32[]{:S(2)}, u32[]{:S(2)}) %all-to-all-start.1) | async-done | bytes 1179680 | tf_op jit(solution)/shard_map/all_to_all | solution.py:81
  (145 shorter events, 21.1 us)
Async XLA Ops:
  7.2 117.8 %all-gather.7.cloned.1.call-start = ((), (), s32[]{:S(2)}) async-start(), calls=%async_computation.7 | async-start | bytes 1966080 | tf_op jit(solution)/shard_map/all_gather | solution.py:73
  44.9 83.2 %all-gather.5.cloned.1.call-start = ((), (), s32[]{:S(2)}) async-start(), calls=%async_computation.6 | async-start | bytes 3932160 | tf_op jit(solution)/shard_map/all_gather | solution.py:73
  45.7 174.1 %all-gather.9.cloned.1.call-start = ((), (), s32[]{:S(2)}) async-start(), calls=%async_computation.8 | async-start | bytes 10485760 | tf_op jit(solution)/shard_map/all_gather | solution.py:73
  95.1 26.7 %copy-start.30 = (s32[1,2]{1,0:T(1,128)S(1)}, s32[1,2]{1,0:T(1,128)}, u32[]{:S(2)}) copy-start(s32[1,2]{1,0:T(1,128)} %param.31) | copy-start | bytes 28
  95.1 28.0 %copy-start.31 = (s32[1,160]{1,0:T(1,128)S(1)}, s32[1,160]{1,0:T(1,128)}, u32[]{:S(2)}) copy-start(s32[1,160]{1,0:T(1,128)} %param.29) | copy-start | bytes 1924
  95.1 227.1 %all-gather.11.cloned.1.call-start = ((), (), s32[]{:S(2)}) async-start(), calls=%async_computation.9 | async-start | bytes 5242880 | tf_op jit(solution)/shard_map/all_gather | solution.py:73
  121.7 458.9 %reduce-scatter.4.cloned.1.call-start = ((), (), s32[]{:S(2)}) async-start(), calls=%async_computation.10 | async-start | bytes 5242880 | tf_op jit(solution)/shard_map/reduce_scatter | solution.py:77
  124.9 1.8 slice-start
  128.1 69.4 %copy-start.26 = (f32[1,256]{1,0:T(1,128)}, f32[1,256]{1,0:T(1,128)S(1)}, u32[]{:S(2)}) copy-start(f32[1,256]{1,0:T(1,128)S(1)} %get-tuple-element.132) | copy-start | bytes 3076
  128.1 69.4 %copy-start.28 = (f32[1,256]{1,0:T(1,128)}, f32[1,256]{1,0:T(1,128)S(1)}, u32[]{:S(2)}) copy-start(f32[1,256]{1,0:T(1,128)S(1)} %get-tuple-element.133) | copy-start | bytes 3076
  183.1 14.4 %copy-start.1 = (f32[1280,768]{1,0:T(8,128)S(1)}, f32[1280,768]{1,0:T(8,128)}, u32[]{:S(2)}) copy-start(f32[1280,768]{1,0:T(8,128)} %get-tuple-element.44) | copy-start | bytes 11796484
  197.4 2.0 copy-start.21
  197.4 1.9 copy-start.23
  203.9 5.3 copy-start.11
  209.7 3.5 copy-start.5
  209.7 3.5 copy-start.9
  213.3 5.4 copy-start
  213.3 5.4 copy-start.19
  218.6 103.5 %copy-start.13 = (bf16[1280,2,128]{0,2,1:T(8,128)(2,1)}, bf16[1280,2,128]{0,2,1:T(8,128)(2,1)S(1)}, u32[]{:S(2)}) copy-start(bf16[1280,2,128]{0,2,1:T(8,128)(2,1)S(1)} %get-tuple-element.129) | copy-start | bytes 1966084
  322.2 111.8 %copy-start.32 = (bf16[1280,1024]{1,0:T(8,128)(2,1)S(1)}, bf16[1280,1024]{1,0:T(8,128)(2,1)}, u32[]{:S(2)}) copy-start(bf16[1280,1024]{1,0:T(8,128)(2,1)} %get-tuple-element.50.left) | copy-start | bytes 7864324
  460.5 165.8 %reduce-scatter.6.cloned.1.call-start = ((), (), s32[]{:S(2)}) async-start(), calls=%async_computation.11 | async-start | bytes 10485760 | tf_op jit(solution)/shard_map/reduce_scatter | solution.py:77
  461.0 114.3 %copy-start.25 = (f32[8,2048]{1,0:T(8,128)S(1)}, f32[8,2048]{1,0:T(8,128)}, u32[]{:S(2)}) copy-start(f32[8,2048]{1,0:T(8,128)} %get-tuple-element.69) | copy-start | bytes 196612
  461.1 114.4 %copy-start.14 = (bf16[1280,2,128]{0,2,1:T(8,128)(2,1)S(1)}, bf16[1280,2,128]{0,2,1:T(8,128)(2,1)}, u32[]{:S(2)}) copy-start(bf16[1280,2,128]{0,2,1:T(8,128)(2,1)} %copy-done.13) | copy-start | bytes 1966084
  575.4 5.1 copy-start.15
  581.0 11.7 %copy-start.7 = (f32[1280,2,128]{0,2,1:T(8,128)S(1)}, f32[1280,2,128]{0,2,1:T(8,128)}, u32[]{:S(2)}) copy-start(f32[1280,2,128]{0,2,1:T(8,128)} %get-tuple-element.130) | copy-start | bytes 3932164
  581.0 42.9 %all-to-all-start = ((bf16[8,64,1024]{2,1,0:T(8,128)(2,1)}), bf16[8,64,1024]{2,1,0:T(8,128)(2,1)}, u32[]{:S(2)}, u32[]{:S(2)}) async-start(bf16[8,64,1024]{2,1,0:T(8,128)(2,1)} %bitcast.125), calls=%async_computation.1 | async-start | bytes 2097152 | tf_op jit(solution)/shard_map/all_to_all | solution.py:81
  592.5 0.7 copy-start.20
  592.5 142.2 %reduce-scatter.8.cloned.1.call-start = ((), (), s32[]{:S(2)}) async-start(), calls=%async_computation.12 | async-start | bytes 5898240 | tf_op jit(solution)/shard_map/reduce_scatter | solution.py:77
  593.2 7.6 copy-start.10
  600.8 2.2 copy-start.4
  600.9 2.2 copy-start.6
  604.4 1.1 copy-start.8
  609.1 6.1 copy-start.3
  609.1 3.3 copy-start.22
  609.1 3.3 copy-start.24
  609.1 3.3 copy-start.27
  609.1 3.3 copy-start.29
  626.2 7.7 copy-start.2
  634.0 2.4 copy-start.12
  637.8 7.5 copy-start.16
  647.7 89.5 %all-to-all-start.2 = ((bf16[8,64,2048]{2,1,0:T(8,128)(2,1)}), bf16[8,64,2048]{2,1,0:T(8,128)(2,1)S(1)}, u32[]{:S(2)}, u32[]{:S(2)}) async-start(bf16[8,64,2048]{2,1,0:T(8,128)(2,1)} %bitcast.122), calls=%async_computation.5 | async-start | bytes 4194304 | tf_op jit(solution)/shard_map/all_to_all | solution.py:81
  737.2 32.1 %all-to-all-start.1 = ((bf16[8,64,1152]{2,1,0:T(8,128)(2,1)}), bf16[8,64,1152]{2,1,0:T(8,128)(2,1)S(1)}, u32[]{:S(2)}, u32[]{:S(2)}) async-start(bf16[8,64,1152]{2,1,0:T(8,128)(2,1)} %bitcast.117), calls=%async_computation.4 | async-start | bytes 2359296 | tf_op jit(solution)/shard_map/all_to_all | solution.py:81
  770.4 3.3 copy-start.17
  771.2 3.3 copy-start.18
Sparse Core Ops, SparseCore 0:
  45.0 31.3 all-gather.6
  78.2 43.9 all-gather.4
  124.1 87.5 all-gather.8
  213.4 52.6 all-gather.10
  460.6 61.7 reduce-scatter.3
  525.6 86.3 reduce-scatter.5
  647.8 58.2 reduce-scatter.7

commit v3 on v2

v3 whole, which is shorter than its diff:
```python
import functools

import jax
import jax.numpy as jnp
from jax import lax
from jax.experimental import pallas as pl
from jax.experimental.pallas import tpu as pltpu
from jax.sharding import PartitionSpec as P

MESH = pl.DeviceIdType.MESH

HEAD_DIM = 128

rope_base = 500000.0
norm_eps = 1e-06
f32 = jnp.float32
bf16 = jnp.bfloat16


def rms_factor(values):
    return lax.rsqrt(jnp.mean(values * values, axis=-1, keepdims=True) + norm_eps)


def norm_back(grad_normed, raw_values, factor):
    unit_values = raw_values * factor
    return factor * (
        grad_normed - unit_values * jnp.mean(grad_normed * unit_values, axis=-1, keepdims=True)
    )


def rope_tables(positions, head_dim):
    half_dim = head_dim // 2
    steps_f = jnp.arange(half_dim).astype(f32) * (2.0 / head_dim)
    inv_freq = jnp.power(rope_base, -steps_f)
    angle = positions.astype(f32)[:, None] * inv_freq[None, :]
    angle = jnp.concatenate([angle, angle], axis=-1)[:, None, :]
    return (jnp.cos(angle), jnp.sin(angle))


def rotate(values, cosine, sine):
    half_dim = values.shape[-1] // 2
    turned = jnp.concatenate([-values[..., half_dim:], values[..., :half_dim]], axis=-1)
    return values * cosine + turned * sine


def unrotate(grads, cosine, sine):
    half_dim = grads.shape[-1] // 2
    moved = grads * sine
    back_part = jnp.concatenate([moved[..., half_dim:], -moved[..., :half_dim]], axis=-1)
    return grads * cosine + back_part


def allowed_mask(query_pos, key_code):
    key_pos = key_code // 2
    usable = key_code % 2 == 1
    causal = key_pos[None, :] <= query_pos[:, None]
    return causal & (usable[None, :] | (key_pos[None, :] == query_pos[:, None]))


def dot_nn(left, right):
    return jnp.dot(left, right, preferred_element_type=f32)


def dot_nt(left, right):
    return lax.dot_general(left, right, (((1,), (1,)), ((), ())), preferred_element_type=f32)


def dot_tn(left, right):
    return lax.dot_general(left, right, (((0,), (0,)), ((), ())), preferred_element_type=f32)


def across(piece):
    return lax.all_gather(piece, "dp", axis=0, tiled=True)


def dp_sum(grad):
    return lax.psum_scatter(grad, "dp", scatter_dimension=0, tiled=True)


def send_home(summed, ways):
    return lax.all_to_all(summed, "seq", split_axis=0, concat_axis=1, tiled=True)


def split_grads(moved, widths, ways):
    rows = moved.shape[0]
    moved = moved.reshape(rows, ways, sum(widths))
    outs, begin = [], 0
    for width in widths:
        outs.append(moved[:, :, begin : begin + width].reshape(rows, ways * width).astype(f32))
        begin += width
    return outs


class Line:
    def __init__(self, ways):
        self.chips = ways // 2
        self.last = self.chips - 1
        self.me = lax.axis_index("seq")
        self.chip = self.me // 2
        self.core = self.me % 2
        self.sibling = self.me + 1 - 2 * self.core

    def greet(self, groups=1):
        barrier = pltpu.get_barrier_semaphore()
        group = lax.axis_index("dp")
        for off in range(1, groups):
            pl.semaphore_signal(
                barrier, inc=1, device_id={"dp": (group + off) % groups}, device_id_type=MESH
            )
        has_low = jnp.minimum(self.chip, 1)
        has_high = jnp.minimum(self.last - self.chip, 1)
        pl.semaphore_signal(barrier, inc=1, device_id={"seq": self.sibling}, device_id_type=MESH)

        @pl.when(self.chip > 0)
        def _():
            pl.semaphore_signal(barrier, inc=1, device_id={"seq": self.me - 2}, device_id_type=MESH)

        @pl.when(self.chip < self.last)
        def _():
            pl.semaphore_signal(barrier, inc=1, device_id={"seq": self.me + 2}, device_id_type=MESH)

        pl.semaphore_wait(barrier, groups + has_low + has_high)


def remote(src, dst, send_sem, recv_sem, device):
    return pltpu.make_async_remote_copy(
        src_ref=src,
        dst_ref=dst,
        send_sem=send_sem,
        recv_sem=recv_sem,
        device_id={"seq": device},
        device_id_type=MESH,
    )


def rows_at(index, count):
    return pl.ds(pl.multiple_of(index * count, count), count)


def each_strip(tok_count, strip, fn):
    def one(i, carry):
        fn(rows_at(i, strip))
        return carry

    lax.fori_loop(0, tok_count // strip, one, 0)


class RowGather:
    def __init__(self, line, half, buf, sems):
        self.line, self.half, self.buf = line, half, buf
        self.up_send, self.down_send, self.col_recv, self.sib_send, self.sib_recv = sems

    @staticmethod
    def scratch(chips):
        return [pltpu.SemaphoreType.DMA((2 * chips,))] * 5

    def piece(self, src, core, h):
        return self.buf.at[rows_at(h * 2 * self.line.chips + 2 * src + core, self.half)]

    def hop(self, src, h, device, send):
        piece, at = self.piece(src, self.line.core, h), h * self.line.chips + src
        return remote(piece, piece, send.at[at], self.col_recv.at[at], device)

    def swap(self, src, core, h):
        piece, at = self.piece(src, core, h), h * self.line.chips + src
        return remote(piece, piece, self.sib_send.at[at], self.sib_recv.at[at], self.line.sibling)

    def start(self, h):
        line = self.line
        self.forward_up(line.chip, h)
        self.forward_down(line.chip, h)
        self.swap(line.chip, line.core, h).start()

    def forward_up(self, src, h):
        @pl.when(self.line.chip < self.line.last)
        def _():
            self.hop(src, h, self.line.me + 2, self.up_send).start()

    def forward_down(self, src, h):
        @pl.when(self.line.chip > 0)
        def _():
            self.hop(src, h, self.line.me - 2, self.down_send).start()

    def receive(self, away, h):
        line = self.line
        low, high = line.chip - away, line.chip + away

        @pl.when(low >= 0)
        def _():
            self.hop(low, h, line.sibling, self.up_send).wait_recv()
            self.forward_up(low, h)
            self.swap(low, line.core, h).start()

        @pl.when(high <= line.last)
        def _():
            self.hop(high, h, line.sibling, self.down_send).wait_recv()
            self.forward_down(high, h)
            self.swap(high, line.core, h).start()

    def use_at(self, away, h, use):
        line = self.line
        low, high = line.chip - away, line.chip + away

        @pl.when(low >= 0)
        def _():
            self.swap(low, 1 - line.core, h).wait_recv()
            use(low, h)

        @pl.when((high <= line.last) & (away > 0))
        def _():
            self.swap(high, 1 - line.core, h).wait_recv()
            use(high, h)

    def finish(self):
        line = self.line
        for h in (0, 1):

            def one(src, carry, h=h):
                self.swap(src, line.core, h).wait_send()

                @pl.when((src <= line.chip) & (line.chip < line.last))
                def _():
                    self.hop(src, h, line.sibling, self.up_send).wait_send()

                @pl.when((src >= line.chip) & (line.chip > 0))
                def _():
                    self.hop(src, h, line.sibling, self.down_send).wait_send()

                return carry

            lax.fori_loop(0, line.chips, one, 0)


class RowScatter:
    def __init__(self, line, half, bufs, sems):
        self.line, self.half = line, half
        self.pair, self.sib_in, self.acc = bufs
        self.sib_send, self.sib_recv, self.send, self.recv = sems

    @staticmethod
    def scratch(chips, tok, width):
        return [
            pltpu.VMEM((2 * chips * tok, width), bf16),
            pltpu.VMEM((chips * tok, width), bf16),
            pltpu.VMEM(((chips + 1) * tok, width), bf16),
            pltpu.SemaphoreType.DMA((2 * chips,)),
            pltpu.SemaphoreType.DMA((2 * chips,)),
            pltpu.SemaphoreType.DMA((2 * chips,)),
            pltpu.SemaphoreType.DMA((2 * (chips + 1),)),
        ]

    def of(self, left, right, tile, joined):
        self.left, self.right, self.tile, self.joined = left, right, tile, joined
        return self

    def swap(self, dest, h):
        half, line = self.half, self.line
        at = h * line.chips + dest
        return remote(
            self.pair.at[rows_at(2 * at + 1 - line.core, half)],
            self.sib_in.at[rows_at(at, half)],
            self.sib_send.at[at],
            self.sib_recv.at[at],
            line.sibling,
        )

    def hop(self, dest, slot, h, device):
        half, slots = self.half, self.line.chips + 1
        return remote(
            self.acc.at[rows_at(h * slots + dest, half)],
            self.acc.at[rows_at(h * slots + slot, half)],
            self.send.at[h * self.line.chips + dest],
            self.recv.at[h * slots + slot],
            device,
        )

    def produce(self, dest, h):
        if self.joined and h:
            return
        spans = [rows_at(h * self.line.chips + dest, 2 * self.half)]
        if self.joined:
            spans.append(rows_at(self.line.chips + dest, 2 * self.half))

        def one(n, carry):
            cols = rows_at(n, self.tile)
            left = [self.left[span, :] for span in spans]
            left = jnp.concatenate(left, axis=0) if self.joined else left[0]
            part = dot_nt(left, self.right[cols, :]).astype(bf16)
            for i, span in enumerate(spans):
                self.pair[span, cols] = part[i * 2 * self.half : (i + 1) * 2 * self.half]
            return carry

        lax.fori_loop(0, self.right.shape[0] // self.tile, one, 0)
        for i in range(len(spans)):
            self.swap(dest, h + i).start()

    def strip_of(self, index, strip):
        return pl.ds(pl.multiple_of(index * self.half + strip.start, 16), strip.size)

    def chip_sum(self, dest, h, strip):
        at = h * self.line.chips + dest
        mine = self.pair[self.strip_of(2 * at + self.line.core, strip), :]
        other = self.sib_in[self.strip_of(at, strip), :]
        return mine.astype(f32) + other.astype(f32)

    def legs(self, s):
        line = self.line
        below, above = line.chip, line.last - line.chip
        return (
            (line.last - s + below, 1, below, (s >= below) & (s < line.last)),
            (s - above, -1, above, (s >= above) & (s < line.last)),
        )

    def make(self, s, h):
        for dest, _, _, there in self.legs(s):

            @pl.when(there)
            def _(dest=dest):
                self.produce(dest, h)

    def pass_on(self, s, h):
        line = self.line
        chips, slots = line.chips, line.chips + 1
        for dest, step, behind, there in self.legs(s):
            if step > 0:
                slot = dest
            else:
                ends = 1 - jnp.minimum(line.chip - 1 - dest, 1)
                slot = dest + ends * (chips - dest)

            @pl.when(there)
            def _(dest=dest, behind=behind, slot=slot, step=step):
                self.swap(dest, h).wait_recv()

                @pl.when(behind > 0)
                def _():
                    self.hop(dest, dest, h, line.sibling).wait_recv()

                    def add(strip):
                        at = self.strip_of(h * slots + dest, strip)
                        total = self.chip_sum(dest, h, strip) + self.acc[at, :].astype(f32)
                        self.acc[at, :] = total.astype(bf16)

                    each_strip(self.half, 16, add)

                @pl.when(behind == 0)
                def _():
                    def put(strip):
                        at = self.strip_of(h * slots + dest, strip)
                        self.acc[at, :] = self.chip_sum(dest, h, strip).astype(bf16)

                    each_strip(self.half, 16, put)

                self.hop(dest, slot, h, line.me + 2 * step).start()

    def close(self, h):
        line = self.line
        chips, slots = line.chips, line.chips + 1
        empty = jnp.zeros((self.half, self.acc.shape[1]), bf16)
        self.swap(line.chip, h).wait_recv()

        @pl.when(line.chip > 0)
        def _():
            self.hop(line.chip, line.chip, h, line.sibling).wait_recv()

        @pl.when(line.chip == 0)
        def _():
            self.acc[rows_at(h * slots + line.chip, self.half), :] = empty

        @pl.when(line.chip < line.last)
        def _():
            self.hop(line.chip, chips, h, line.sibling).wait_recv()

        @pl.when(line.chip == line.last)
        def _():
            self.acc[rows_at(h * slots + chips, self.half), :] = empty

    def total(self, h, strip):
        line = self.line
        slots = line.chips + 1
        low = self.acc[self.strip_of(h * slots + line.chip, strip), :].astype(f32)
        high = self.acc[self.strip_of(h * slots + line.chips, strip), :].astype(f32)
        return self.chip_sum(line.chip, h, strip) + (low + high)

    def finish(self, h):
        line = self.line

        def one(dest, carry):
            self.swap(dest, h).wait_send()

            @pl.when(line.chip != dest)
            def _():
                self.hop(dest, dest, h, line.sibling).wait_send()

            return carry

        lax.fori_loop(0, line.chips, one, 0)


def advance(scatter=None, sh=0, gather=None, gh=0, use=None):
    line = (scatter or gather).line
    if scatter:
        scatter.make(0, sh)

    def slot(s, carry):
        if gather:

            @pl.when(s > 0)
            def _():
                gather.receive(s, gh)

        if scatter:
            scatter.pass_on(s, sh)
            scatter.make(s + 1, sh)

            @pl.when(s == line.last - 1)
            def _():
                scatter.produce(line.chip, sh)

        if gather:

            @pl.when(s > 0)
            def _():
                gather.use_at(s - 1, gh, use)

        return carry

    lax.fori_loop(0, line.chips, slot, 0)


def mean_rows(values):
    return jnp.sum(values, axis=-1, keepdims=True) * (1.0 / values.shape[-1])


class Blocks:
    def __init__(self, line, count, pairs, sems):
        self.line, self.count, self.pairs, self.sems = line, count, pairs, sems

    def copy(self, i, index):
        src, dst = self.pairs[i]
        at = rows_at(index, self.count)
        return pltpu.make_async_copy(src.at[at], dst.at[at], self.sems.at[i, index])

    def send(self, i, chip, h):
        self.copy(i, h * self.line.chips + chip).start()

    def finish(self):
        def one(index, carry):
            for i in range(len(self.pairs)):
                self.copy(i, index).wait()
            return carry

        lax.fori_loop(0, 2 * self.line.chips, one, 0)


def call(kernel, outs, scratch, args, ident, cost=1, far_in=(), far_out=()):
    def space(i, far):
        return pl.BlockSpec(memory_space=pl.ANY if i in far else pltpu.VMEM)

    return pl.pallas_call(
        kernel,
        out_shape=outs,
        in_specs=[space(i, far_in) for i in range(len(args))],
        out_specs=[space(i, far_out) for i in range(len(outs))],
        scratch_shapes=scratch,
        cost_estimate=pl.CostEstimate(
            flops=cost * 10**9, transcendentals=0, bytes_accessed=cost * 3 * 10**6
        ),
        compiler_params=pltpu.CompilerParams(
            collective_id=ident, has_side_effects=True, vmem_limit_bytes=63 * 2**20
        ),
    )(*args)


def shape(dims, kind):
    return jax.ShapeDtypeStruct(dims, kind)


def gather_project(rows, codes, weights, ways, ident):
    tok, width = rows.shape
    cols = weights.shape[1] - HEAD_DIM
    half = tok // 2

    def kernel(
        rows_ref, code_ref, w_far, all_far, codes_ref, prod_far,
        w_ref, all_ref, prod_ref, w_sem, out_sem, code_send, code_recv, *sems
    ):
        line = Line(ways)
        w_copy = pltpu.make_async_copy(w_far.at[:, pl.ds(0, cols)], w_ref, w_sem)
        w_copy.start()
        outs = Blocks(line, 2 * half, [(all_ref, all_far), (prod_ref, prod_far)], out_sem)
        me = line.me
        barrier = pltpu.get_barrier_semaphore()
        for off in range(1, ways):
            pl.semaphore_signal(
                barrier, inc=1, device_id={"seq": (me + off) % ways}, device_id_type=MESH
            )
        pl.semaphore_wait(barrier, ways - 1)
        gather = RowGather(line, half, all_ref, sems)
        for h in (0, 1):
            all_ref[rows_at(h * ways + me, half), :] = rows_ref[pl.ds(h * half, half), :]
            gather.start(h)
        codes_ref[me] = code_ref[...]

        def tell(off):
            return remote(
                code_ref, codes_ref.at[me], code_send.at[off], code_recv.at[off], (me + off) % ways
            )

        for off in range(1, ways):
            tell(off).start()

        def use(chip, h):
            at = rows_at(h * line.chips + chip, 2 * half)

            prod_ref[at, :] = dot_nn(all_ref[at, :], w_ref[...])
            outs.send(0, chip, h)
            outs.send(1, chip, h)

        def step(j, carry):
            for h in (0, 1):
                gather.receive(j, h)
                gather.use_at(j - 1, h, use)
            return carry

        w_copy.wait()
        lax.fori_loop(1, line.chips, step, 0)
        for h in (0, 1):
            gather.use_at(line.last, h, use)
        gather.finish()
        outs.finish()
        for off in range(1, ways):
            tell(off).wait()

    return call(
        kernel,
        [
            shape((ways * tok, width), bf16),
            shape((ways,) + codes.shape, jnp.int32),
            shape((ways * tok, cols), f32),
        ],
        [
            pltpu.VMEM((width, cols), bf16),
            pltpu.VMEM((ways * tok, width), bf16),
            pltpu.VMEM((ways * tok, cols), f32),
            pltpu.SemaphoreType.DMA,
            pltpu.SemaphoreType.DMA((2, ways)),
            pltpu.SemaphoreType.DMA((ways,)),
            pltpu.SemaphoreType.DMA((ways,)),
        ]
        + RowGather.scratch(ways // 2),
        [rows, codes, weights],
        ident,
        55,
        (2,),
        (0, 2),
    )


def attn_out_and_ff(attn_low, m_mid, p_down, token_rows, grad_out, gains, groups, ways, ident):
    tok, width = token_rows.shape
    half = tok // 2
    own_feat, own_ff = attn_low.shape[1], p_down.shape[1]
    part = p_down.shape[0]
    row = ways * tok
    tile = min(own_ff, 1024)

    def kernel(
        left_far, mid_far, down_far, x_far, go_far, gains_ref,
        branch_far, out_ref, gg_ref, hid_far, mix_far, gm_far, dgu_far,
        left, mid_ref, down_ref, x_ref, go_ref, branch_ref, hid_ref, mix_ref, gm_ref, dgu_ref,
        in_sem, out_sem, branch_sem, down_send, down_recv, *rest
    ):
        line = Line(ways)
        group = lax.axis_index("dp")
        gu_cols, out_cols = pl.ds(0, 2 * own_ff), pl.ds(2 * own_ff, own_feat)
        fetch = [
            pltpu.make_async_copy(src, dst, in_sem.at[i])
            for i, (src, dst) in enumerate(
                [
                    (left_far, left),
                    (mid_far.at[:, out_cols], mid_ref.at[:, out_cols]),
                    (x_far, x_ref),
                    (mid_far.at[:, gu_cols], mid_ref.at[:, gu_cols]),
                    (down_far, down_ref.at[rows_at(group, part)]),
                    (go_far, go_ref),
                ]
            )
        ]
        for copy in fetch:
            copy.start()
        outs = Blocks(
            line,
            2 * half,
            [(hid_ref, hid_far), (mix_ref, mix_far), (gm_ref, gm_far), (dgu_ref, dgu_far)],
            out_sem,
        )
        keep_branch = pltpu.make_async_copy(branch_ref, branch_far, branch_sem)
        line.greet(groups)

        def spread(off):
            return pltpu.make_async_remote_copy(
                src_ref=down_far,
                dst_ref=down_ref.at[rows_at(group, part)],
                send_sem=down_send.at[off],
                recv_sem=down_recv.at[off],
                device_id={"dp": (group + off) % groups},
                device_id_type=MESH,
            )

        for off in range(1, groups):
            spread(off).start()
        scatter = RowScatter(line, half, rest[:3], rest[3:7])
        hidden = RowGather(line, half, hid_ref, rest[7:12])
        back = RowGather(line, half, gm_ref, rest[12:17])
        gg_ref[...] = jnp.zeros_like(gg_ref)
        gain_attn, gain_mlp = gains_ref[2:3, :], gains_ref[3:4, :]

        def own(h, strip):
            return pl.ds(pl.multiple_of((h * ways + line.me) * half + strip.start, 16), strip.size)

        def residual(at):
            branch = branch_ref[at, :]
            factor = lax.rsqrt(mean_rows(branch * branch) + norm_eps)
            return x_ref[at, :].astype(f32) + branch * factor * gain_attn

        def settle_attn(h):
            def one(strip):
                at = pl.ds(pl.multiple_of(h * half + strip.start, 16), strip.size)
                branch_ref[at, :] = scatter.total(h, strip)
                hid_ref[own(h, strip), :] = residual(at).astype(bf16)

            scatter.close(h)
            each_strip(half, 16, one)
            hidden.start(h)
            scatter.finish(h)

        def settle_mlp(h):
            def one(strip):
                at = pl.ds(pl.multiple_of(h * half + strip.start, 16), strip.size)
                mlp = scatter.total(h, strip)
                factor = lax.rsqrt(mean_rows(mlp * mlp) + norm_eps)
                unit = mlp * factor
                grad = go_ref[at, :].astype(f32)
                out_ref[at, :] = (residual(at) + unit * gain_mlp).astype(bf16)
                terms = grad * unit
                gg_ref[...] += terms[:8] + terms[8:]
                lifted = grad * gain_mlp
                turned = factor * (lifted - unit * mean_rows(lifted * unit))
                gm_ref[own(h, strip), :] = turned.astype(bf16)

            scatter.close(h)
            each_strip(half, 16, one)
            back.start(h)
            scatter.finish(h)

        def gate_up(chip, h):
            at = rows_at(h * line.chips + chip, 2 * half)

            outs.send(0, chip, h)

            def one(n, carry):
                here, there = rows_at(n, tile), pl.ds(pl.multiple_of(own_ff + n * tile, tile), tile)
                block = hid_ref[at, :]
                gate = dot_nn(block, mid_ref[:, here])
                up = dot_nn(block, mid_ref[:, there])
                dgu_ref[at, here] = gate.astype(bf16)
                dgu_ref[at, there] = up.astype(bf16)
                mix_ref[at, here] = (gate * jax.nn.sigmoid(gate) * up).astype(bf16)
                return carry

            lax.fori_loop(0, own_ff // tile, one, 0)
            outs.send(1, chip, h)

        def gate_up_back(chip, h):
            at = rows_at(h * line.chips + chip, 2 * half)

            outs.send(2, chip, h)

            def one(n, carry):
                here, there = rows_at(n, tile), pl.ds(pl.multiple_of(own_ff + n * tile, tile), tile)
                grad = dot_nn(gm_ref[at, :], down_ref[:, here])
                gate, up = dgu_ref[at, here].astype(f32), dgu_ref[at, there].astype(f32)
                sigma = jax.nn.sigmoid(gate)
                dgu_ref[at, here] = (grad * up * sigma * (1.0 + gate * (1.0 - sigma))).astype(bf16)
                dgu_ref[at, there] = (grad * gate * sigma).astype(bf16)
                return carry

            lax.fori_loop(0, own_ff // tile, one, 0)
            outs.send(3, chip, h)

        for copy in fetch[:3]:
            copy.wait()
        scatter.of(left, mid_ref.at[:, out_cols], 1024, True)
        advance(scatter, 0)
        fetch[3].wait()
        settle_attn(0)
        advance(scatter, 1, hidden, 0, gate_up)
        settle_attn(1)
        hidden.use_at(line.last, 0, gate_up)
        keep_branch.start()
        for copy in fetch[4:]:
            copy.wait()
        for off in range(1, groups):
            spread(off).wait()
        scatter.of(mix_ref, down_ref, 1024, False)
        advance(scatter, 0, hidden, 1, gate_up)
        settle_mlp(0)
        hidden.use_at(line.last, 1, gate_up)
        advance(scatter, 1, back, 0, gate_up_back)
        settle_mlp(1)
        back.use_at(line.last, 0, gate_up_back)
        advance(None, 0, back, 1, gate_up_back)
        back.use_at(line.last, 1, gate_up_back)
        hidden.finish()
        back.finish()
        keep_branch.wait()
        outs.finish()

    return call(
        kernel,
        [
            shape((tok, width), f32),
            shape((tok, width), bf16),
            shape((8, width), f32),
            shape((row, width), bf16),
            shape((row, own_ff), bf16),
            shape((row, width), bf16),
            shape((row, 2 * own_ff), bf16),
        ],
        [
            pltpu.VMEM((row, own_feat), bf16),
            pltpu.VMEM(m_mid.shape, bf16),
            pltpu.VMEM((groups * part, own_ff), bf16),
            pltpu.VMEM((tok, width), bf16),
            pltpu.VMEM((tok, width), bf16),
            pltpu.VMEM((tok, width), f32),
            pltpu.VMEM((row, width), bf16),
            pltpu.VMEM((row, own_ff), bf16),
            pltpu.VMEM((row, width), bf16),
            pltpu.VMEM((row, 2 * own_ff), bf16),
            pltpu.SemaphoreType.DMA((6,)),
            pltpu.SemaphoreType.DMA((4, ways)),
            pltpu.SemaphoreType.DMA,
            pltpu.SemaphoreType.DMA((groups,)),
            pltpu.SemaphoreType.DMA((groups,)),
        ]
        + RowScatter.scratch(ways // 2, tok, width)
        + RowGather.scratch(ways // 2)
        + RowGather.scratch(ways // 2),
        [attn_low, m_mid, p_down, token_rows, grad_out, gains],
        ident,
        150,
        range(5),
        (0, 3, 4, 5, 6),
    )


def ff_to_attn_back(grad_gu, m_mid, branch, grad_out, gain_row, ways, ident):
    tok, width = branch.shape
    half = tok // 2
    own_ff = grad_gu.shape[1] // 2
    own_feat = m_mid.shape[1] - 2 * own_ff
    row = ways * tok

    def kernel(
        left, w_ref, br_ref, go_ref, gain_ref, gh_ref, gg_ref, all_far, ga_ref,
        all_ref, out_sem, *rest
    ):
        line = Line(ways)
        outs = Blocks(line, 2 * half, [(all_ref, all_far)], out_sem)
        line.greet()
        scatter = RowScatter(line, half, rest[:3], rest[3:7])
        gather = RowGather(line, half, all_ref, rest[7:])
        gg_ref[...] = jnp.zeros_like(gg_ref)

        def settle(h):
            def one(strip):
                at = pl.ds(pl.multiple_of(h * half + strip.start, 16), strip.size)
                mine = pl.ds(
                    pl.multiple_of((h * ways + line.me) * half + strip.start, 16), strip.size
                )
                grad = scatter.total(h, strip) + go_ref[at, :].astype(f32)
                branch = br_ref[at, :]
                factor = lax.rsqrt(mean_rows(branch * branch) + norm_eps)
                unit = branch * factor
                gh_ref[at, :] = grad
                terms = grad * unit
                gg_ref[...] += terms[:8] + terms[8:]
                lifted = grad * gain_ref[...]
                turned = factor * (lifted - unit * mean_rows(lifted * unit))
                all_ref[mine, :] = turned.astype(bf16)

            scatter.close(h)
            each_strip(half, 16, one)
            gather.start(h)

        def use(chip, h):
            at = rows_at(h * line.chips + chip, 2 * half)
            outs.send(0, chip, h)
            ga_ref[at, :] = dot_nn(all_ref[at, :], w_ref[:, pl.ds(2 * own_ff, own_feat)])

        scatter.of(left, w_ref.at[:, pl.ds(0, 2 * own_ff)], 512, True)
        advance(scatter, 0)
        settle(0)
        advance(scatter, 1, gather, 0, use)
        settle(1)
        gather.use_at(line.last, 0, use)
        advance(None, 0, gather, 1, use)
        gather.use_at(line.last, 1, use)
        gather.finish()
        outs.finish()
        for h in (0, 1):
            scatter.finish(h)

    return call(
        kernel,
        [
            shape((tok, width), f32),
            shape((8, width), f32),
            shape((row, width), bf16),
            shape((row, own_feat), f32),
        ],
        [pltpu.VMEM((row, width), bf16), pltpu.SemaphoreType.DMA((1, ways))]
        + RowScatter.scratch(ways // 2, tok, width)
        + RowGather.scratch(ways // 2),
        [grad_gu, m_mid, branch, grad_out, gain_row],
        ident,
        100,
        (),
        (2,),
    )


def project_back(grad_qkv, m_qkv, grad_hidden, ways, ident):
    tok, width = grad_hidden.shape
    half = tok // 2

    def kernel(left, w_ref, gh_ref, out_ref, *rest):
        line = Line(ways)
        line.greet()
        scatter = RowScatter(line, half, rest[:3], rest[3:7])
        scatter.of(left, w_ref.at[:, pl.ds(0, left.shape[1])], 1024, True)
        for h in (0, 1):
            advance(scatter, h)
        for h in (0, 1):

            def one(strip, h=h):
                at = pl.ds(pl.multiple_of(h * half + strip.start, 16), strip.size)
                out_ref[at, :] = (gh_ref[at, :] + scatter.total(h, strip)).astype(bf16)

            scatter.close(h)
            each_strip(half, 16, one)
        for h in (0, 1):
            scatter.finish(h)

    return call(
        kernel,
        [shape((tok, width), bf16)],
        RowScatter.scratch(ways // 2, tok, width),
        [grad_qkv, m_qkv, grad_hidden],
        ident,
        55,
    )[0]


def exchange(sources, ways, ident, cost):
    rows = sources[0].shape[0]
    widths = [a.shape[1] // ways for a in sources]
    begins = [sum(widths[:i]) for i in range(len(widths))]
    count = len(sources)

    def kernel(*refs):
        ins, out_ref, send, recv, local = refs[:count], *refs[count:]
        me = lax.axis_index("seq")
        barrier = pltpu.get_barrier_semaphore()

        def greet(off, carry):
            pl.semaphore_signal(
                barrier, inc=1, device_id={"seq": (me + off) % ways}, device_id_type=MESH
            )
            return carry

        def move(off, i):
            dest = (me + off) % ways
            return remote(
                ins[i].at[:, rows_at(dest, widths[i])],
                out_ref.at[rows_at(me, rows), pl.ds(begins[i], widths[i])],
                send.at[off * count + i],
                recv.at[off * count + i],
                dest,
            )

        def keep(i):
            return pltpu.make_async_copy(
                ins[i].at[:, rows_at(me, widths[i])],
                out_ref.at[rows_at(me, rows), pl.ds(begins[i], widths[i])],
                local.at[i],
            )

        def each(what):
            def one(off, carry):
                for i in range(count):
                    what(move(off, i))
                return carry

            lax.fori_loop(1, ways, one, 0)

        for i in range(count):
            keep(i).start()
        lax.fori_loop(1, ways, greet, 0)
        pl.semaphore_wait(barrier, ways - 1)
        each(lambda copy: copy.start())
        for i in range(count):
            keep(i).wait()
        each(lambda copy: copy.wait())

    return pl.pallas_call(
        kernel,
        out_shape=shape((ways * rows, sum(widths)), bf16),
        in_specs=[pl.BlockSpec(memory_space=pl.ANY)] * count,
        out_specs=pl.BlockSpec(memory_space=pl.ANY),
        scratch_shapes=[
            pltpu.SemaphoreType.DMA((ways * count,)),
            pltpu.SemaphoreType.DMA((ways * count,)),
            pltpu.SemaphoreType.DMA((count,)),
        ],
        cost_estimate=pl.CostEstimate(
            flops=cost * 10**9, transcendentals=0, bytes_accessed=cost * 3 * 10**6
        ),
        compiler_params=pltpu.CompilerParams(collective_id=ident, has_side_effects=True),
    )(*sources)


def line_sum(terms, ways, ident):
    def kernel(terms_ref, out_ref, slots, send, recv):
        me = lax.axis_index("seq")
        barrier = pltpu.get_barrier_semaphore()
        for off in range(1, ways):
            pl.semaphore_signal(
                barrier, inc=1, device_id={"seq": (me + off) % ways}, device_id_type=MESH
            )
        pl.semaphore_wait(barrier, ways - 1)
        for off in range(1, ways):
            remote(
                terms_ref, slots.at[off], send.at[off], recv.at[off], (me + off) % ways
            ).start()
        total = terms_ref[...]
        for off in range(1, ways):
            remote(terms_ref, slots.at[off], send.at[off], recv.at[off], (me + off) % ways).wait_recv()
            total = total + slots[off]
        out_ref[...] = total
        for off in range(1, ways):
            remote(terms_ref, slots.at[off], send.at[off], recv.at[off], (me + off) % ways).wait_send()

    return call(
        kernel,
        [shape(terms.shape, f32)],
        [
            pltpu.VMEM((ways,) + terms.shape, f32),
            pltpu.SemaphoreType.DMA((ways,)),
            pltpu.SemaphoreType.DMA((ways,)),
        ],
        [terms],
        ident,
        8,
    )[0]


def body(
    tokens,
    w_query,
    w_key,
    w_value,
    w_out,
    w_gate,
    w_up,
    w_down,
    gain_query,
    gain_key,
    gain_attn,
    gain_mlp,
    cotangent,
    key_mask,
    lengths,
    tract_order,
):
    ways, groups = lax.axis_size("seq"), lax.axis_size("dp")
    me = lax.axis_index("seq")
    token_rows = tokens[0]
    tok_count, feat_width = token_rows.shape
    ff_width = w_gate.shape[1]
    own_feat = feat_width // ways
    own_heads = own_feat // HEAD_DIM
    own_ff = ff_width // ways
    row_len = tok_count * ways
    score_scale = HEAD_DIM ** (-0.5)
    half_len = tok_count // 2
    order_pair = tract_order[0]
    slot_index = jnp.arange(tok_count, dtype=jnp.int32)
    local_pos = (
        jnp.where(slot_index < half_len, order_pair[0], order_pair[1]) * half_len
        + slot_index % half_len
    )
    key_ok = ((key_mask[0] == 1) & (local_pos < lengths[0])).astype(jnp.int32)

    gain_local = jnp.stack([gain_query, gain_key, gain_attn, gain_mlp], axis=1)
    gain_pad = jnp.pad(gain_local, ((0, 0), (0, HEAD_DIM - 4)))
    gain_all = jnp.tile(gain_pad, (1, ways))
    p_qkv = exchange([w_query, w_key, w_value, gain_all], ways, 8, 20)
    m_qkv = across(p_qkv)
    p_qkv, w_gate, w_up, w_out_t = lax.optimization_barrier(
        (p_qkv, w_gate, w_up, jnp.transpose(w_out))
    )
    p_mid = exchange([w_gate, w_up, w_out_t], ways, 10, 50)
    m_mid = across(p_mid)
    gains = dot_nt(jnp.eye(8, HEAD_DIM, dtype=bf16), m_qkv[:, 3 * own_feat :])
    gain_q = lax.dynamic_slice_in_dim(gains[0], me * own_feat, own_feat, 0)
    gain_k = lax.dynamic_slice_in_dim(gains[1], me * own_feat, own_feat, 0)

    code_pad = -tok_count % HEAD_DIM
    local_code = jnp.pad(local_pos * 2 + key_ok, (0, code_pad))[None]
    local_code, p_mid = lax.optimization_barrier((local_code, p_mid))
    x_row, codes, qkv = gather_project(token_rows, local_code, m_qkv, ways, 1)
    key_code = codes[:, 0, :tok_count].reshape(ways, 2, half_len)
    key_code = jnp.transpose(key_code, (1, 0, 2)).reshape(row_len)
    pos = key_code // 2
    q_raw, k_raw, v_raw = (qkv[:, i * own_feat : (i + 1) * own_feat] for i in range(3))
    squares = line_sum(
        jnp.stack([jnp.sum(q_raw * q_raw, axis=-1), jnp.sum(k_raw * k_raw, axis=-1)]), ways, 2
    )
    squares, w_down_t = lax.optimization_barrier((squares, jnp.transpose(w_down)))
    p_down = lax.all_to_all(w_down_t, "seq", split_axis=1, concat_axis=0, tiled=True)
    factors = lax.rsqrt(squares / feat_width + norm_eps)
    q_factor, k_factor = factors[0][:, None], factors[1][:, None]
    cosine, sine = rope_tables(pos, HEAD_DIM)
    head_shape = (row_len, own_heads, HEAD_DIM)
    query_low = rotate((q_raw * q_factor * gain_q).reshape(head_shape), cosine, sine).astype(bf16)
    key_low = rotate((k_raw * k_factor * gain_k).reshape(head_shape), cosine, sine).astype(bf16)
    value_low = v_raw.astype(bf16).reshape(head_shape)

    mask = allowed_mask(pos, key_code)[None]
    scores = jnp.einsum("qhd,khd->hqk", query_low, key_low, preferred_element_type=f32) * score_scale
    expo = jnp.where(mask, jnp.exp(scores), 0.0)
    weight_sum = jnp.transpose(jnp.sum(expo, axis=-1))[:, :, None]
    expo_low = expo.astype(bf16)
    attn = jnp.einsum("hqk,khd->qhd", expo_low, value_low, preferred_element_type=f32) / weight_sum
    attn_low = attn.astype(bf16).reshape(row_len, own_feat)

    branch, layer_out, grad_gain_mlp, hidden_low, mixed_low, grad_mlp, grad_gu = attn_out_and_ff(
        attn_low, m_mid, p_down, token_rows, cotangent[0], gains, groups, ways, 3
    )
    d_down = dot_tn(grad_mlp, mixed_low).astype(bf16)
    d_gu = dot_tn(hidden_low, grad_gu).astype(bf16)
    grad_gu, d_down, d_gu = lax.optimization_barrier((grad_gu, d_down, d_gu))
    d_gu = dp_sum(d_gu)
    d_down = dp_sum(d_down)
    grad_hidden, grad_gain_attn, grad_branch, grad_attn = ff_to_attn_back(
        grad_gu, m_mid, branch, cotangent[0], gains[2:3], ways, 5
    )
    grad_attn, d_gu = lax.optimization_barrier((grad_attn, d_gu))
    d_gu = send_home(d_gu, ways)
    grad_attn = grad_attn.reshape(head_shape)
    grad_num = (grad_attn / weight_sum).astype(bf16)
    drop = jnp.transpose(jnp.sum(grad_attn * attn, axis=-1) / weight_sum[:, :, 0])
    grad_expo = jnp.einsum("qhd,khd->hqk", grad_num, value_low, preferred_element_type=f32)
    grad_scores = (expo * (grad_expo - drop[:, :, None])).astype(bf16)
    grad_q = (
        jnp.einsum("hqk,khd->qhd", grad_scores, key_low, preferred_element_type=f32) * score_scale
    )
    grad_k = (
        jnp.einsum("hqk,qhd->khd", grad_scores, query_low, preferred_element_type=f32) * score_scale
    )
    grad_v = jnp.einsum("hqk,qhd->khd", expo_low, grad_num, preferred_element_type=f32)
    grad_q_norm = unrotate(grad_q, cosine, sine).reshape(row_len, own_feat)
    grad_k_norm = unrotate(grad_k, cosine, sine).reshape(row_len, own_feat)
    q_unit, k_unit = q_raw * q_factor, k_raw * k_factor
    grad_gain_query = jnp.sum(grad_q_norm * q_unit, axis=0)
    grad_gain_key = jnp.sum(grad_k_norm * k_unit, axis=0)
    c_q, c_k = grad_q_norm * gain_q, grad_k_norm * gain_k
    terms = jnp.stack([jnp.sum(c_q * q_unit, axis=-1), jnp.sum(c_k * k_unit, axis=-1)])
    terms, d_down, d_gu = lax.optimization_barrier((terms, d_down, d_gu))
    means = line_sum(terms, ways, 6) / feat_width
    d_down = send_home(d_down, ways)
    dw_gu = split_grads(d_gu, [own_ff, own_ff], ways)
    grad_q_raw = q_factor * (c_q - q_unit * means[0][:, None])
    grad_k_raw = k_factor * (c_k - k_unit * means[1][:, None])
    grad_qkv = jnp.concatenate(
        [grad_q_raw, grad_k_raw, grad_v.reshape(row_len, own_feat)], axis=1
    ).astype(bf16)

    own_slot = jnp.zeros((2, feat_width), f32)
    own_slot = lax.dynamic_update_slice(
        own_slot, jnp.stack([grad_gain_query, grad_gain_key]), (0, me * own_feat)
    )
    gain_terms = jnp.concatenate(
        [
            own_slot,
            jnp.sum(grad_gain_attn, axis=0, keepdims=True),
            jnp.sum(grad_gain_mlp, axis=0, keepdims=True),
        ]
    )
    gain_columns = jnp.pad(jnp.transpose(gain_terms), ((0, 0), (0, HEAD_DIM - 4)))
    d_attn = jnp.concatenate(
        [dot_tn(x_row, grad_qkv), dot_tn(grad_branch, attn_low), gain_columns], axis=1
    ).astype(bf16)
    grad_qkv, d_attn, d_down = lax.optimization_barrier((grad_qkv, d_attn, d_down))
    dw_down = split_grads(d_down, [own_ff], ways)
    grad_tokens = project_back(grad_qkv, m_qkv, grad_hidden, ways, 7)
    grad_tokens, d_attn = lax.optimization_barrier((grad_tokens, dp_sum(d_attn)))
    dw_qkv = split_grads(send_home(d_attn, ways), [own_feat] * 4 + [HEAD_DIM], ways)
    gain_grads = jnp.sum(dw_qkv[4].reshape(-1, ways, HEAD_DIM), axis=1)
    gain_grads = jnp.transpose(gain_grads[:, :8])
    return (
        layer_out[None],
        grad_tokens[None],
        dw_qkv[0],
        dw_qkv[1],
        dw_qkv[2],
        jnp.transpose(dw_qkv[3]),
        dw_gu[0],
        dw_gu[1],
        jnp.transpose(dw_down[0]),
        gain_grads[0],
        gain_grads[1],
        gain_grads[2],
        gain_grads[3],
    )


def solution(mesh):
    both = ("dp", "seq")
    in_specs = (
        P("dp", "seq", None),
        P(both, None),
        P(both, None),
        P(both, None),
        P(None, both),
        P(both, None),
        P(both, None),
        P(None, both),
        P(both),
        P(both),
        P(both),
        P(both),
        P("dp", "seq", None),
        P("dp", "seq"),
        P("dp"),
        P("dp", "seq"),
    )
    out_specs = (
        P("dp", "seq", None),
        P("dp", "seq", None),
        P(both, None),
        P(both, None),
        P(both, None),
        P(None, both),
        P(both, None),
        P(both, None),
        P(None, both),
        P(both),
        P(both),
        P(both),
        P(both),
    )
    return jax.shard_map(body, mesh=mesh, in_specs=in_specs, out_specs=out_specs, check_vma=False)
```

time: 792 us -> 698 us (0.88)
  Pallas kernels: 591 us -> 462 us
  waiting for transfers between devices: 21.2 us -> 40.7 us
    pallas_call x7 -> x6, Pallas kernels: 481 us -> 383 us  [call(): pl.pallas_call(kernel, out_shape=outs, in_specs=[space(i, far_in) for i i...]
    pallas_call x4 -> x2, Pallas kernels: 110 us -> 79.5 us  [exchange(): pl.pallas_call(kernel, out_shape=shape((ways * rows, sum(widths)), bf16),...]
    all_to_all x3, waiting for transfers between devices: 19.8 us -> 39.1 us  [send_home(): lax.all_to_all(summed, 'seq', split_axis=0, concat_axis=1, tiled=True)]
    unnamed x70 -> x77, local copies, waits for them, and re-layouts: 3.91 us -> 14.9 us
  transfers between devices with their start and end apart: 10 -> 9, of which waited for: 1 -> 4; matrix products, arithmetic and copies ran while one was open for 10% -> 14% of each run, Pallas kernels for 56% -> 39%
where the time goes in v3:
time: 698 us; the launch traced here: 687 us
  Pallas kernels  462 us (66%)
  matrix products  72.6 us (10%)
  waiting for transfers between devices  40.7 us (6%)
  local copies, waits for them, and re-layouts  38.5 us (6%)
  other arithmetic  29.9 us (4%)
  starting transfers between devices  28 us (4%)
  between operations  15.4 us (2%)
    pallas_call x6, Pallas kernels, call(): pl.pallas_call(kernel, out_shape=outs, in_specs=[space(i, far_in) for i i...  383 us
    pallas_call x2, Pallas kernels, exchange(): pl.pallas_call(kernel, out_shape=shape((ways * rows, sum(widths)), bf16),...  79.5 us
    dot_general x4, matrix products, dot_tn(): lax.dot_general(left, right, (((0,), (0,)), ((), ())), preferred_element_...  39.3 us
    all_to_all x3, waiting for transfers between devices, send_home(): lax.all_to_all(summed, 'seq', split_axis=0, concat_axis=1, tiled=True)  39.1 us
    all_to_all x3, starting transfers between devices, send_home(): lax.all_to_all(summed, 'seq', split_axis=0, concat_axis=1, tiled=True)  21.7 us
    unnamed x77, local copies, waits for them, and re-layouts  14.9 us
  transfers between devices with their start and end apart: 9, of which 4 were waited for; matrix products, arithmetic and copies ran while one was open for 14% of the time, Pallas kernels for 39%

profile of v3, /device:TPU:9, one launch (start us, length us, event | category | flops | bytes accessed | tf_op | source)
XLA Modules:
  0.0 687.3 jit_solution(14608827584992243426)
XLA Ops:
  8.8 24.7 %shard_map.255 = bf16[512,896]{1,0:T(8,128)(2,1)} custom-call(bf16[64,2048]{1,0:T(8,128)(2,1)} %refs_0_.1, bf16[64,2048]{1,0:T(8,128)(2,1)} %refs_1_.1, bf16[64,2048]{1,0:T(8,128)(2,1)} %refs_2_.1, bf16[64,1024]{1,0:T(8,128)(2,1)} %bitcast.151), custom_call_target="tpu_custom_call" | custom-call | flops 20000000000 | bytes 60000000 | tf_op jit(solution)/shard_map/pallas_call | solution.py:918
  33.5 54.8 %shard_map.256 = bf16[512,2304]{1,0:T(8,128)(2,1)} custom-call(bf16[64,8192]{1,0:T(8,128)(2,1)} %refs_0_.2, bf16[64,8192]{1,0:T(8,128)(2,1)} %refs_1_.2, bf16[64,2048]{1,0:T(8,128)(2,1)} %bitcast.170), custom_call_target="tpu_custom_call" | custom-call | flops 49999998976 | bytes 150000000 | tf_op jit(solution)/shard_map/pallas_call | solution.py:918
  89.6 1.3 fusion.37
  91.5 46.9 %shard_map.257 = (bf16[1280,2048]{1,0:T(8,128)(2,1)}, s32[8,1,256]{2,1,0:T(1,128)}, f32[1280,768]{1,0:T(8,128)}) custom-call(bf16[160,2048]{1,0:T(8,128)(2,1)} %bitcast.166, s32[1,256]{1,0:T(1,128)} %bitcast.161, bf16[2048,896]{1,0:T(8,128)(2,1)} %all-gather.3.cloned.1.call-done.w_far.w_ref), custom_call_target="tpu_custom_call" | custom-call | flops 54999998464 | bytes 165000000 | tf_op jit(solution)/shard_map/pallas_call | solution.py:460
  139.3 2.1 multiply_reduce_fusion.6
  142.1 11.6 %shard_map.258 = f32[2,1280]{1,0:T(2,128)} custom-call(f32[2,1280]{1,0:T(2,128)} %pad_maximum_fusion.2.terms_ref), custom_call_target="tpu_custom_call" | custom-call | flops 8000000000 | bytes 24000000 | tf_op jit(solution)/shard_map/pallas_call | solution.py:460
  153.7 2.3 copy.223
  156.0 5.5 all-to-all-start
  161.9 1.3 fusion.30.gains_ref
  163.9 3.2 fusion.22
  167.5 1.7 copy.194
  169.4 3.3 broadcast_multiply_fusion.3
  172.9 2.0 or_and_fusion
  175.4 3.5 fusion.43
  179.0 5.4 fusion.44
  186.3 162.6 %shard_map.259 = (f32[160,2048]{1,0:T(8,128)}, bf16[160,2048]{1,0:T(8,128)(2,1)}, f32[8,2048]{1,0:T(8,128)}, bf16[1280,2048]{1,0:T(8,128)(2,1)}, bf16[1280,1024]...) custom-call(bf16[1280,256]{1,0:T(8,128)(2,1)} %copy.190.left_far, ...), custom_call_target="tpu_custom_call" | custom-call | flops 149999992832 | bytes 450000000 | tf_op jit(solution)/shard_map/pallas_call | solution.py:460
  348.9 10.1 %convolution_convert_fusion.1 = bf16[2048,1024]{1,0:T(8,128)(2,1)} fusion(bf16[1280,2048]{1,0:T(8,128)(2,1)} %get-tuple-element.56, bf16[1280,1024]{1,0:T(8,128)(2,1)} %get-tuple-element.57), kind=kOutput, calls=%fused_computation.10 | convolution fusion | flops 5370806272 | bytes 12058624 | tf_op jit(solution)/shard_map/dot_general | solution.py:69
  359.1 16.7 %convolution_convert_fusion = bf16[2048,2048]{1,0:T(8,128)(2,1)} fusion(bf16[1280,2048]{1,0:T(8,128)(2,1)} %get-tuple-element.58, bf16[1280,2048]{1,0:T(8,128)(2,1)} %get-tuple-element.59.left), kind=kOutput, calls=%fused_computation.7 | convolution fusion | flops 10741612544 | bytes 18874368 | tf_op jit(solution)/shard_map/dot_general | solution.py:69
  376.4 97.8 %shard_map.260 = (f32[160,2048]{1,0:T(8,128)}, f32[8,2048]{1,0:T(8,128)}, bf16[1280,2048]{1,0:T(8,128)(2,1)}, f32[1280,256]{1,0:T(8,128)}) custom-call(bf16[1280,2048]{1,0:T(8,128)(2,1)} %get-tuple-element.59.left, bf16[2048,2304]{1,0:T(8,128)(2,1)} %all-gather.5.cloned.1.call-done.mid_far.w_ref, f32[160,2048]{1,0:T(8,128)} %get-tuple-element.60.br_ref, ...), custom_call_target="tpu_custom_call" | custom-call | flops 99999997952 | bytes 300000000 | tf_op jit(solution)/shard_map/pallas_call | solution.py:460
  475.1 5.0 convolution_convert_fusion.3
  480.0 1.7 copy.196
  481.8 11.2 %all-to-all-start.1 = ((bf16[8,64,2048]{2,1,0:T(8,128)(2,1)}), bf16[8,64,2048]{2,1,0:T(8,128)(2,1)}, u32[]{:S(2)}, u32[]{:S(2)}) async-start(bf16[8,64,2048]{2,1,0:T(8,128)(2,1)} %bitcast.136), calls=%async_computation.3 | async-start | bytes 4194304 | tf_op jit(solution)/shard_map/all_to_all | solution.py:81
  493.7 9.9 %fusion.1 = bf16[2,1280,1280]{1,2,0:T(8,128)(2,1)} fusion(f32[2,1280,1280]{1,2,0:T(8,128)} %copy-done, f32[2,1280]{1,0:T(2,128)S(1)} %bitcast_divide_fusion, f32[1280,2,128]{0,2,1:T(8,128)S(1)} %bitcast.116, f32[1280,2]{0,1:T(2,128)S(1)} %bitcast.149, f32[1280,768]{1,0:T(8,128)} %get-tuple-element.50), kind=kOutput, calls=%fused_computation.4 | convolution fusion | flops 849346560 | bytes 21647360 | tf_op jit(solution)/shard_map/qhd,khd->hqk/dot_general | solution.py:1066
  503.6 7.0 %fusion.14 = bf16[2,128,1280]{2,1,0:T(8,128)(2,1)S(1)} fusion(f32[2,1280,1280]{1,2,0:T(8,128)} %copy-done, f32[1280,2,128]{0,2,1:T(8,128)S(1)} %bitcast.117, f32[1280,2]{0,1:T(2,128)S(1)} %bitcast.150), kind=kOutput, calls=%fused_computation.20 | convolution fusion | flops 843120640 | bytes 15083520 | tf_op jit(solution)/shard_map/hqk,qhd->khd/dot_general | solution.py:1074
  511.7 5.2 convolution_bitcast_fusion
  516.9 1.2 broadcast_multiply_fusion.1
  519.3 1.4 maximum_add_fusion
  521.2 2.2 copy.192
  523.4 3.0 multiply_reduce_fusion.1
  527.2 11.4 %all-to-all-done.1 = bf16[8,64,2048]{2,1,0:T(8,128)(2,1)} async-done(((bf16[8,64,2048]{2,1,0:T(8,128)(2,1)}), bf16[8,64,2048]{2,1,0:T(8,128)(2,1)}, u32[]{:S(2)}, u32[]{:S(2)}) %all-to-all-start.1) | async-done | bytes 2097184 | tf_op jit(solution)/shard_map/all_to_all | solution.py:81
  538.5 3.2 copy.200
  541.7 9.3 %shard_map.261 = f32[2,1280]{1,0:T(2,128)} custom-call(f32[2,1280]{1,0:T(2,128)} %pad_maximum_fusion.3.terms_ref), custom_call_target="tpu_custom_call" | custom-call | flops 8000000000 | bytes 24000000 | tf_op jit(solution)/shard_map/pallas_call | solution.py:460
  551.9 4.7 all-to-all-start.2
  556.8 2.6 multiply_convert_fusion.1
  559.5 1.4 pad_maximum_fusion.left
  560.9 7.5 %convolution_convert_fusion.2 = bf16[2048,768]{0,1:T(8,128)(2,1)S(1)} fusion(bf16[1280,2048]{1,0:T(8,128)(2,1)} %get-tuple-element.67, bf16[1280,256]{1,0:T(8,128)(2,1)S(1)} %copy.193, bf16[1280,256]{1,0:T(8,128)(2,1)S(1)} %get-tuple-element.98, bf16[1280,256]{1,0:T(8,128)(2,1)S(1)} %get-tuple-element.97), kind=kOutput, calls=%fused_computation.11 | convolution fusion | flops 4034002944 | bytes 10354688 | tf_op jit(solution)/shard_map/dot_general | solution.py:69
  568.4 2.4 fusion.3
  570.8 8.8 %all-to-all-done.2 = bf16[8,64,1024]{2,1,0:T(8,128)(2,1)S(1)} async-done(((bf16[8,64,1024]{2,1,0:T(8,128)(2,1)}), bf16[8,64,1024]{2,1,0:T(8,128)(2,1)S(1)}, u32[]{:S(2)}, u32[]{:S(2)}) %all-to-all-start.2) | async-done | bytes 1048608 | tf_op jit(solution)/shard_map/all_to_all | solution.py:81
  579.6 1.1 copy.201
  580.7 1.6 copy-done.6
  582.3 2.5 copy.207
  584.8 54.5 %shard_map.262 = bf16[160,2048]{1,0:T(8,128)(2,1)} custom-call(bf16[1280,768]{1,0:T(8,128)(2,1)} %pad_maximum_fusion.left, bf16[2048,896]{1,0:T(8,128)(2,1)} %all-gather.3.cloned.1.call-done.w_far.w_ref, f32[160,2048]{1,0:T(8,128)} %get-tuple-element.73.gh_ref), custom_call_target="tpu_custom_call" | custom-call | flops 54999998464 | bytes 165000000 | tf_op jit(solution)/shard_map/pallas_call | solution.py:460
  640.3 2.4 copy.177
  642.7 5.9 all-to-all-start.3
  649.0 2.5 copy.209
  651.5 2.5 copy.208
  654.0 1.5 convert_bitcast_fusion
  655.5 18.9 %all-to-all-done.3 = bf16[8,64,1152]{2,1,0:T(8,128)(2,1)S(1)} async-done(((bf16[8,64,1152]{2,1,0:T(8,128)(2,1)}), bf16[8,64,1152]{2,1,0:T(8,128)(2,1)S(1)}, u32[]{:S(2)}, u32[]{:S(2)}) %all-to-all-start.3) | async-done | bytes 1179680 | tf_op jit(solution)/shard_map/all_to_all | solution.py:81
  (142 shorter events, 22.8 us)
Async XLA Ops:
  7.2 84.4 %all-gather.3.cloned.1.call-start = ((), (), s32[]{:S(2)}) async-start(), calls=%async_computation.7 | async-start | bytes 4587520 | tf_op jit(solution)/shard_map/all_gather | solution.py:73
  33.5 152.8 %all-gather.5.cloned.1.call-start = ((), (), s32[]{:S(2)}) async-start(), calls=%async_computation.8 | async-start | bytes 11796480 | tf_op jit(solution)/shard_map/all_gather | solution.py:73
  88.3 0.7 copy-start.34
  88.3 0.7 copy-start.33
  156.0 7.9 %copy-start.32 = (f32[2,1280]{1,0:T(2,128)S(1)}, f32[2,1280]{1,0:T(2,128)}, u32[]{:S(2)}) copy-start(f32[2,1280]{1,0:T(2,128)} %shard_map.258) | copy-start | bytes 30724
  156.0 30.3 %all-to-all-start = ((bf16[64,8,1024]{2,0,1:T(8,128)(2,1)}), bf16[64,8,1024]{2,0,1:T(8,128)(2,1)}, u32[]{:S(2)}, u32[]{:S(2)}) async-start(bf16[64,8,1024]{2,0,1:T(8,128)(2,1)} %bitcast.112), calls=%async_computation | async-start | bytes 2097152 | tf_op jit(solution)/shard_map/all_to_all | solution.py:1033
  161.5 318.6 %reduce-scatter.4.cloned.1.call-start = ((), (), s32[]{:S(2)}) async-start(), calls=%async_computation.9 | async-start | bytes 10485760 | tf_op jit(solution)/shard_map/reduce_scatter | solution.py:77
  163.2 3.9 copy-start.26
  163.8 3.3 copy-start.28
  163.8 3.3 copy-start.30
  163.9 3.2 copy-start.22
  163.9 3.2 copy-start.24
  175.4 3.5 copy-start.8
  175.4 3.5 copy-start.13
  179.0 5.4 copy-start
  179.0 5.4 copy-start.20
  184.3 0.8 copy-start.15
  375.8 165.9 %reduce-scatter.6.cloned.1.call-start = ((), (), s32[]{:S(2)}) async-start(), calls=%async_computation.10 | async-start | bytes 5242880 | tf_op jit(solution)/shard_map/reduce_scatter | solution.py:77
  376.3 97.8 %copy-start.27 = (f32[8,2048]{1,0:T(8,128)S(1)}, f32[8,2048]{1,0:T(8,128)}, u32[]{:S(2)}) copy-start(f32[8,2048]{1,0:T(8,128)} %get-tuple-element.70) | copy-start | bytes 196612
  376.4 98.7 %copy-start.16 = (bf16[1280,2,128]{0,2,1:T(8,128)(2,1)S(1)}, bf16[1280,2,128]{0,2,1:T(8,128)(2,1)}, u32[]{:S(2)}) copy-start(bf16[1280,2,128]{0,2,1:T(8,128)(2,1)} %copy-done.15) | copy-start | bytes 1966084
  481.8 11.2 %copy-start.10 = (f32[1280,2,128]{0,2,1:T(8,128)S(1)}, f32[1280,2,128]{0,2,1:T(8,128)}, u32[]{:S(2)}) copy-start(f32[1280,2,128]{0,2,1:T(8,128)} %get-tuple-element.133) | copy-start | bytes 3932164
  481.8 56.8 %all-to-all-start.1 = ((bf16[8,64,2048]{2,1,0:T(8,128)(2,1)}), bf16[8,64,2048]{2,1,0:T(8,128)(2,1)}, u32[]{:S(2)}, u32[]{:S(2)}) async-start(bf16[8,64,2048]{2,1,0:T(8,128)(2,1)} %bitcast.136), calls=%async_computation.3 | async-start | bytes 4194304 | tf_op jit(solution)/shard_map/all_to_all | solution.py:81
  493.0 0.7 copy-start.21
  510.6 1.1 copy-start.14
  511.6 5.2 copy-start.1
  511.6 5.2 copy-start.7
  511.6 5.2 copy-start.9
  518.2 1.1 copy-start.12
  521.1 5.3 copy-start.2
  521.1 2.2 copy-start.23
  521.1 2.2 copy-start.25
  521.1 2.2 copy-start.29
  521.2 2.2 copy-start.31
  523.4 3.0 copy-start.4
  551.0 5.8 copy-start.3
  551.9 27.7 %all-to-all-start.2 = ((bf16[8,64,1024]{2,1,0:T(8,128)(2,1)}), bf16[8,64,1024]{2,1,0:T(8,128)(2,1)S(1)}, u32[]{:S(2)}, u32[]{:S(2)}) async-start(bf16[8,64,1024]{2,1,0:T(8,128)(2,1)} %bitcast.140), calls=%async_computation.4 | async-start | bytes 2097152 | tf_op jit(solution)/shard_map/all_to_all | solution.py:81
  556.6 83.7 %reduce-scatter.8.cloned.1.call-start = ((), (), s32[]{:S(2)}) async-start(), calls=%async_computation.11 | async-start | bytes 5898240 | tf_op jit(solution)/shard_map/reduce_scatter | solution.py:77
  560.9 7.5 %copy-start.17 = (bf16[2048,256]{0,1:T(8,128)(2,1)S(1)}, bf16[2048,256]{0,1:T(8,128)(2,1)}, u32[]{:S(2)}) copy-start(bf16[2048,256]{0,1:T(8,128)(2,1)} %convolution_convert_fusion.3) | copy-start | bytes 3145732
  580.7 1.6 copy-start.6
  642.7 5.9 copy-start.5
  642.7 31.7 %all-to-all-start.3 = ((bf16[8,64,1152]{2,1,0:T(8,128)(2,1)}), bf16[8,64,1152]{2,1,0:T(8,128)(2,1)S(1)}, u32[]{:S(2)}, u32[]{:S(2)}) async-start(bf16[8,64,1152]{2,1,0:T(8,128)(2,1)} %bitcast.130), calls=%async_computation.6 | async-start | bytes 2359296 | tf_op jit(solution)/shard_map/all_to_all | solution.py:81
  651.5 2.5 copy-start.11
  676.3 2.5 copy-start.18
  677.1 2.5 copy-start.19
Sparse Core Ops, SparseCore 0:
  33.6 48.8 all-gather.2
  88.5 96.8 all-gather.4
  375.9 91.6 reduce-scatter.3
  470.7 52.7 reduce-scatter.5
  580.8 59.4 reduce-scatter.7

commit v4 on v3

--- a/solution.py
+++ b/solution.py
@@ -13,6 +13,7 @@
 
 rope_base = 500000.0
 norm_eps = 1e-06
+LOG2_E = 1.4426950408889634
 f32 = jnp.float32
 bf16 = jnp.bfloat16
 
@@ -33,7 +34,7 @@
     steps_f = jnp.arange(half_dim).astype(f32) * (2.0 / head_dim)
     inv_freq = jnp.power(rope_base, -steps_f)
     angle = positions.astype(f32)[:, None] * inv_freq[None, :]
-    angle = jnp.concatenate([angle, angle], axis=-1)[:, None, :]
+    angle = jnp.concatenate([angle, angle], axis=-1)
     return (jnp.cos(angle), jnp.sin(angle))
 
 
@@ -75,20 +76,6 @@
 
 def dp_sum(grad):
     return lax.psum_scatter(grad, "dp", scatter_dimension=0, tiled=True)
-
-
-def send_home(summed, ways):
-    return lax.all_to_all(summed, "seq", split_axis=0, concat_axis=1, tiled=True)
-
-
-def split_grads(moved, widths, ways):
-    rows = moved.shape[0]
-    moved = moved.reshape(rows, ways, sum(widths))
-    outs, begin = [], 0
-    for width in widths:
-        outs.append(moved[:, :, begin : begin + width].reshape(rows, ways * width).astype(f32))
-        begin += width
-    return outs
 
 
 class Line:
@@ -249,8 +236,9 @@
             pltpu.SemaphoreType.DMA((2 * (chips + 1),)),
         ]
 
-    def of(self, left, right, tile, joined):
-        self.left, self.right, self.tile, self.joined = left, right, tile, joined
+    def of(self, left, right, tile, joined, turned=False):
+        self.left, self.right, self.tile = left, right, tile
+        self.joined, self.turned = joined, turned
         return self
 
     def swap(self, dest, h):
@@ -285,12 +273,15 @@
             cols = rows_at(n, self.tile)
             left = [self.left[span, :] for span in spans]
             left = jnp.concatenate(left, axis=0) if self.joined else left[0]
-            part = dot_nt(left, self.right[cols, :]).astype(bf16)
+            if self.turned:
+                part = dot_nn(left, self.right[:, cols]).astype(bf16)
+            else:
+                part = dot_nt(left, self.right[cols, :]).astype(bf16)
             for i, span in enumerate(spans):
                 self.pair[span, cols] = part[i * 2 * self.half : (i + 1) * 2 * self.half]
             return carry
 
-        lax.fori_loop(0, self.right.shape[0] // self.tile, one, 0)
+        lax.fori_loop(0, self.right.shape[1 if self.turned else 0] // self.tile, one, 0)
         for i in range(len(spans)):
             self.swap(dest, h + i).start()
 
@@ -397,7 +388,7 @@
         lax.fori_loop(0, line.chips, one, 0)
 
 
-def advance(scatter=None, sh=0, gather=None, gh=0, use=None):
+def advance(scatter=None, sh=0, gather=None, gh=0, use=None, fill=None):
     line = (scatter or gather).line
     if scatter:
         scatter.make(0, sh)
@@ -423,6 +414,8 @@
             def _():
                 gather.use_at(s - 1, gh, use)
 
+        if fill:
+            fill(s)
         return carry
 
     lax.fori_loop(0, line.chips, slot, 0)
@@ -564,12 +557,15 @@
     part = p_down.shape[0]
     row = ways * tok
     tile = min(own_ff, 1024)
+    square = width == 2 * own_ff
+    square_tile = 256
+    squares = width // square_tile
 
     def kernel(
         left_far, mid_far, down_far, x_far, go_far, gains_ref,
-        branch_far, out_ref, gg_ref, hid_far, mix_far, gm_far, dgu_far,
+        branch_far, out_ref, gg_ref, hid_far, mix_far, gm_far, dgu_far, first_ref,
         left, mid_ref, down_ref, x_ref, go_ref, branch_ref, hid_ref, mix_ref, gm_ref, dgu_ref,
-        in_sem, out_sem, branch_sem, down_send, down_recv, *rest
+        down_turned, in_sem, out_sem, branch_sem, down_send, down_recv, *rest
     ):
         line = Line(ways)
         group = lax.axis_index("dp")
@@ -659,17 +655,10 @@
 
             outs.send(0, chip, h)
 
-            def one(n, carry):
-                here, there = rows_at(n, tile), pl.ds(pl.multiple_of(own_ff + n * tile, tile), tile)
-                block = hid_ref[at, :]
-                gate = dot_nn(block, mid_ref[:, here])
-                up = dot_nn(block, mid_ref[:, there])
-                dgu_ref[at, here] = gate.astype(bf16)
-                dgu_ref[at, there] = up.astype(bf16)
-                mix_ref[at, here] = (gate * jax.nn.sigmoid(gate) * up).astype(bf16)
-                return carry
-
-            lax.fori_loop(0, own_ff // tile, one, 0)
+            both = dot_nn(hid_ref[at, :], mid_ref[:, gu_cols])
+            gate, up = both[:, :own_ff], both[:, own_ff:]
+            dgu_ref[at, :] = both.astype(bf16)
+            mix_ref[at, :] = (gate * jax.nn.sigmoid(gate) * up).astype(bf16)
             outs.send(1, chip, h)
 
         def gate_up_back(chip, h):
@@ -698,20 +687,50 @@
         advance(scatter, 1, hidden, 0, gate_up)
         settle_attn(1)
         hidden.use_at(line.last, 0, gate_up)
+        def turn_down(i, carry):
+            rows = rows_at(i, square_tile)
+            down_turned[:, rows] = down_ref[rows, :].T
+            return carry
+
+        def turn_square(s):
+            def one(i, carry):
+                def two(j, carry):
+                    rows, cols = rows_at(i, square_tile), rows_at(j, square_tile)
+                    block, other = mid_ref[rows, cols], mid_ref[cols, rows]
+                    mid_ref[cols, rows] = block.T
+                    mid_ref[rows, cols] = other.T
+                    return carry
+
+                return lax.fori_loop(i, squares, two, carry)
+
+            lax.fori_loop(s * squares // line.chips, (s + 1) * squares // line.chips, one, 0)
+
         keep_branch.start()
         for copy in fetch[4:]:
             copy.wait()
         for off in range(1, groups):
             spread(off).wait()
-        scatter.of(mix_ref, down_ref, 1024, False)
+        if square:
+            lax.fori_loop(0, squares, turn_down, 0)
+            scatter.of(mix_ref, down_turned, 2048, False, True)
+        else:
+            scatter.of(mix_ref, down_ref, 2048, False)
         advance(scatter, 0, hidden, 1, gate_up)
         settle_mlp(0)
         hidden.use_at(line.last, 1, gate_up)
-        advance(scatter, 1, back, 0, gate_up_back)
+        advance(scatter, 1, back, 0, gate_up_back, turn_square if square else None)
         settle_mlp(1)
         back.use_at(line.last, 0, gate_up_back)
-        advance(None, 0, back, 1, gate_up_back)
+        scatter.of(dgu_ref, mid_ref.at[:, gu_cols], 1024, False, square)
+        advance(scatter, 0, back, 1, gate_up_back)
         back.use_at(line.last, 1, gate_up_back)
+
+        def put(strip):
+            first_ref[strip, :] = scatter.total(0, strip)
+
+        scatter.close(0)
+        each_strip(half, 16, put)
+        scatter.finish(0)
         hidden.finish()
         back.finish()
         keep_branch.wait()
@@ -727,6 +746,7 @@
             shape((row, own_ff), bf16),
             shape((row, width), bf16),
             shape((row, 2 * own_ff), bf16),
+            shape((half, width), f32),
         ],
         [
             pltpu.VMEM((row, own_feat), bf16),
@@ -739,6 +759,7 @@
             pltpu.VMEM((row, own_ff), bf16),
             pltpu.VMEM((row, width), bf16),
             pltpu.VMEM((row, 2 * own_ff), bf16),
+            pltpu.VMEM((own_ff, width) if square else (16, HEAD_DIM), bf16),
             pltpu.SemaphoreType.DMA((6,)),
             pltpu.SemaphoreType.DMA((4, ways)),
             pltpu.SemaphoreType.DMA,
@@ -756,18 +777,47 @@
     )
 
 
-def ff_to_attn_back(grad_gu, m_mid, branch, grad_out, gain_row, ways, ident):
+def ff_to_attn_back(
+    grad_gu, first_half, m_mid, branch, grad_out, gain_row, grad_mlp, mixed_low, ways, ident
+):
     tok, width = branch.shape
     half = tok // 2
     own_ff = grad_gu.shape[1] // 2
     own_feat = m_mid.shape[1] - 2 * own_ff
     row = ways * tok
+    tiles = width // 256
 
     def kernel(
-        left, w_ref, br_ref, go_ref, gain_ref, gh_ref, gg_ref, all_far, ga_ref,
-        all_ref, out_sem, *rest
+        left, first_ref, w_ref, br_ref, go_ref, gain_ref, gm_far, mix_far,
+        gh_ref, gg_ref, all_far, ga_ref, dd_far,
+        all_ref, out_sem, gm_ref, mix_ref, dd_ref, gm_sem, mix_sem, dd_sem, *rest
     ):
         line = Line(ways)
+        mix_copy = pltpu.make_async_copy(mix_far, mix_ref, mix_sem)
+
+        def fetch(i):
+            return pltpu.make_async_copy(
+                gm_far.at[:, pl.ds(i * 256, 256)], gm_ref.at[i % 2], gm_sem.at[i % 2]
+            )
+
+        def keep(i):
+            rows = pl.ds(i * 256, 256)
+            return pltpu.make_async_copy(dd_ref.at[rows], dd_far.at[rows], dd_sem.at[i])
+
+        def down_grad(i):
+            fetch(i).wait()
+            if i + 1 < tiles:
+                fetch(i + 1).start()
+            dd_ref[pl.ds(i * 256, 256), :] = dot_tn(gm_ref[i % 2], mix_ref[...]).astype(bf16)
+            keep(i).start()
+
+        def fill(s):
+            for i in range(tiles):
+
+                @pl.when(s == i * line.chips // tiles)
+                def _(i=i):
+                    down_grad(i)
+
         outs = Blocks(line, 2 * half, [(all_ref, all_far)], out_sem)
         line.greet()
         scatter = RowScatter(line, half, rest[:3], rest[3:7])
@@ -780,7 +830,8 @@
                 mine = pl.ds(
                     pl.multiple_of((h * ways + line.me) * half + strip.start, 16), strip.size
                 )
-                grad = scatter.total(h, strip) + go_ref[at, :].astype(f32)
+                total = scatter.total(h, strip) if h else first_ref[strip, :]
+                grad = total + go_ref[at, :].astype(f32)
                 branch = br_ref[at, :]
                 factor = lax.rsqrt(mean_rows(branch * branch) + norm_eps)
                 unit = branch * factor
@@ -791,7 +842,8 @@
                 turned = factor * (lifted - unit * mean_rows(lifted * unit))
                 all_ref[mine, :] = turned.astype(bf16)
 
-            scatter.close(h)
+            if h:
+                scatter.close(h)
             each_strip(half, 16, one)
             gather.start(h)
 
@@ -800,18 +852,21 @@
             outs.send(0, chip, h)
             ga_ref[at, :] = dot_nn(all_ref[at, :], w_ref[:, pl.ds(2 * own_ff, own_feat)])
 
-        scatter.of(left, w_ref.at[:, pl.ds(0, 2 * own_ff)], 512, True)
-        advance(scatter, 0)
+        scatter.of(left, w_ref.at[:, pl.ds(0, 2 * own_ff)], 1024, False)
         settle(0)
         advance(scatter, 1, gather, 0, use)
         settle(1)
         gather.use_at(line.last, 0, use)
-        advance(None, 0, gather, 1, use)
+        mix_copy.start()
+        fetch(0).start()
+        mix_copy.wait()
+        advance(None, 0, gather, 1, use, fill)
         gather.use_at(line.last, 1, use)
         gather.finish()
         outs.finish()
-        for h in (0, 1):
-            scatter.finish(h)
+        for i in range(tiles):
+            keep(i).wait()
+        scatter.finish(1)
 
     return call(
         kernel,
@@ -820,25 +875,114 @@
             shape((8, width), f32),
             shape((row, width), bf16),
             shape((row, own_feat), f32),
+            shape((width, own_ff), bf16),
         ],
-        [pltpu.VMEM((row, width), bf16), pltpu.SemaphoreType.DMA((1, ways))]
+        [
+            pltpu.VMEM((row, width), bf16),
+            pltpu.SemaphoreType.DMA((1, ways)),
+            pltpu.VMEM((2, row, 256), bf16),
+            pltpu.VMEM((row, own_ff), bf16),
+            pltpu.VMEM((width, own_ff), bf16),
+            pltpu.SemaphoreType.DMA((2,)),
+            pltpu.SemaphoreType.DMA,
+            pltpu.SemaphoreType.DMA((tiles,)),
+        ]
         + RowScatter.scratch(ways // 2, tok, width)
         + RowGather.scratch(ways // 2),
-        [grad_gu, m_mid, branch, grad_out, gain_row],
+        [grad_gu, first_half, m_mid, branch, grad_out, gain_row, grad_mlp, mixed_low],
         ident,
-        100,
-        (),
-        (2,),
-    )
-
-
-def project_back(grad_qkv, m_qkv, grad_hidden, ways, ident):
+        70,
+        (6, 7),
+        (2, 4),
+    )
+
+
+def home_copies(me, ways, source, targets, widths, send, recv):
+    rows = source.shape[0] // ways
+    begins = [sum(widths[:i]) for i in range(len(widths))]
+    count = len(widths)
+
+    def part(i, dest):
+        return (
+            source.at[rows_at(dest, rows), pl.ds(begins[i], widths[i])],
+            targets[i].at[:, rows_at(me, widths[i])],
+        )
+
+    def move(off, i):
+        dest = (me + off) % ways
+        return remote(*part(i, dest), send.at[off * count + i], recv.at[off * count + i], dest)
+
+    def keep(i):
+        return pltpu.make_async_copy(*part(i, me), send.at[i])
+
+    def each(what):
+        def one(off, carry):
+            for i in range(count):
+                what(move(off, i))
+            return carry
+
+        lax.fori_loop(1, ways, one, 0)
+
+    def start():
+        for i in range(count):
+            keep(i).start()
+        each(lambda copy: copy.start())
+
+    def wait():
+        for i in range(count):
+            keep(i).wait()
+        each(lambda copy: copy.wait())
+
+    return start, wait
+
+
+def greet_line(me, ways):
+    barrier = pltpu.get_barrier_semaphore()
+
+    def greet(off, carry):
+        pl.semaphore_signal(
+            barrier, inc=1, device_id={"seq": (me + off) % ways}, device_id_type=MESH
+        )
+        return carry
+
+    lax.fori_loop(1, ways, greet, 0)
+    pl.semaphore_wait(barrier, ways - 1)
+
+
+def bring_home(summed, widths, ways, ident):
+    rows = summed.shape[0] // ways
+    count = len(widths)
+
+    def kernel(*refs):
+        source, targets, (send, recv) = refs[0], refs[1 : 1 + count], refs[1 + count :]
+        me = lax.axis_index("seq")
+        greet_line(me, ways)
+        start, wait = home_copies(me, ways, source, targets, widths, send, recv)
+        start()
+        wait()
+
+    return call(
+        kernel,
+        [shape((rows, ways * width), bf16) for width in widths],
+        [pltpu.SemaphoreType.DMA((ways * count,))] * 2,
+        [summed],
+        ident,
+        30,
+        (0,),
+        range(count),
+    )
+
+
+def project_back(grad_qkv, m_qkv, grad_hidden, d_down, ways, ident):
     tok, width = grad_hidden.shape
     half = tok // 2
-
-    def kernel(left, w_ref, gh_ref, out_ref, *rest):
+    own_ff = d_down.shape[1]
+
+    def kernel(left, w_ref, gh_ref, dd_ref, out_ref, home_ref, dd_send, dd_recv, *rest):
         line = Line(ways)
-        line.greet()
+        greet_line(line.me, ways)
+        start, wait = home_copies(line.me, ways, dd_ref, [home_ref], [own_ff], dd_send, dd_recv)
+        start()
         scatter = RowScatter(line, half, rest[:3], rest[3:7])
         scatter.of(left, w_ref.at[:, pl.ds(0, left.shape[1])], 1024, True)
         for h in (0, 1):
@@ -853,15 +997,238 @@
             each_strip(half, 16, one)
         for h in (0, 1):
             scatter.finish(h)
+        wait()
 
     return call(
         kernel,
-        [shape((tok, width), bf16)],
-        RowScatter.scratch(ways // 2, tok, width),
-        [grad_qkv, m_qkv, grad_hidden],
+        [
+            shape((tok, width), bf16),
+            shape((d_down.shape[0] // ways, ways * own_ff), bf16),
+        ],
+        [pltpu.SemaphoreType.DMA((ways,))] * 2 + RowScatter.scratch(ways // 2, tok, width),
+        [grad_qkv, m_qkv, grad_hidden, d_down],
         ident,
-        55,
-    )[0]
+        65,
+        (3,),
+        (1,),
+    )
+
+
+def half_turn(values, sign):
+    half_dim = HEAD_DIM // 2
+    lane = lax.broadcasted_iota(jnp.int32, values.shape, 1)
+    swapped = pltpu.roll(values, half_dim, 1)
+    return jnp.where(lane < half_dim, -sign * swapped, sign * swapped)
+
+
+def attend(parts, block):
+    row = parts[0].shape[0]
+    width = parts[0].shape[1] // 3
+    heads = width // HEAD_DIM
+    scale = HEAD_DIM ** (-0.5)
+
+    def kernel(
+        qkv_ref, factor_ref, cos_ref, sin_ref, gain_ref, qpos_ref, kpos_ref, kmax_ref,
+        q_ref, k_ref, v_ref, at_ref, low_ref, ws_ref
+    ):
+        def turn(i, carry):
+            rows = rows_at(i, block)
+            cosine, sine = cos_ref[rows, :], sin_ref[rows, :]
+            for which, out_ref in ((0, q_ref), (1, k_ref)):
+                factor = factor_ref[rows, pl.ds(which, 1)]
+                for head in range(heads):
+                    lanes = pl.ds(head * HEAD_DIM, HEAD_DIM)
+                    raw = qkv_ref[rows, pl.ds(which * width + head * HEAD_DIM, HEAD_DIM)]
+                    normed = raw * factor * gain_ref[which : which + 1, lanes]
+                    out_ref[rows, lanes] = (
+                        normed * cosine + half_turn(normed, 1.0) * sine
+                    ).astype(bf16)
+            v_ref[rows, :] = qkv_ref[rows, pl.ds(2 * width, width)].astype(bf16)
+            return carry
+
+        lax.fori_loop(0, row // block, turn, 0)
+
+        def one(i, carry):
+            rows = rows_at(i, block)
+            qpos = qpos_ref[rows, :]
+            mask = (kpos_ref[...] <= qpos) & (qpos <= kmax_ref[...])
+            for head in range(heads):
+                lanes = pl.ds(head * HEAD_DIM, HEAD_DIM)
+                scores = dot_nt(q_ref[rows, lanes], k_ref[:, lanes]) * (scale * LOG2_E)
+                expo = jnp.where(mask, jnp.exp2(scores), 0.0)
+                total = jnp.sum(expo, axis=-1, keepdims=True)
+                result = dot_nn(expo.astype(bf16), v_ref[:, lanes]) / total
+                ws_ref[rows, pl.ds(head, 1)] = total
+                at_ref[rows, lanes] = result
+                low_ref[rows, lanes] = result.astype(bf16)
+            return carry
+
+        lax.fori_loop(0, row // block, one, 0)
+
+    return pl.pallas_call(
+        kernel,
+        out_shape=[shape((row, width), bf16)] * 3
+        + [shape((row, width), f32), shape((row, width), bf16), shape((row, heads), f32)],
+        in_specs=[pl.BlockSpec(memory_space=pltpu.VMEM)] * len(parts),
+        out_specs=[pl.BlockSpec(memory_space=pltpu.VMEM)] * 6,
+        cost_estimate=pl.CostEstimate(
+            flops=4 * row * row * width, transcendentals=row * row * heads, bytes_accessed=60 * 10**6
+        ),
+        compiler_params=pltpu.CompilerParams(vmem_limit_bytes=60 * 2**20),
+    )(*parts)
+
+
+def attend_back(parts, summed, block, ways, ident):
+    row, width = parts[0].shape
+    heads = width // HEAD_DIM
+    scale = HEAD_DIM ** (-0.5)
+
+    def kernel(
+        q_ref, k_ref, v_ref, ga_ref, at_ref, ws_ref, cos_ref, sin_ref, qkv_ref, factor_ref,
+        gain_ref, qpos_ref, kpos_ref, kmax_ref, sum_ref,
+        cq_ref, ck_ref, dv_ref, terms_ref, gg_ref, home_ref, dk_acc, dv_acc, send, recv
+    ):
+        me = lax.axis_index("seq")
+        greet_line(me, ways)
+        start, wait = home_copies(me, ways, sum_ref, [home_ref], [summed.shape[1]], send, recv)
+        start()
+        gg_ref[...] = jnp.zeros_like(gg_ref)
+        dk_acc[...] = jnp.zeros_like(dk_acc)
+        dv_acc[...] = jnp.zeros_like(dv_acc)
+
+        def turn_back(grad, rows, which, out_ref, head):
+            lanes = pl.ds(head * HEAD_DIM, HEAD_DIM)
+            cosine, sine = cos_ref[rows, :], sin_ref[rows, :]
+            normed = grad * cosine + half_turn(grad * sine, -1.0)
+            raw = qkv_ref[rows, pl.ds(which * width + head * HEAD_DIM, HEAD_DIM)]
+            unit = raw * factor_ref[rows, pl.ds(which, 1)]
+            gg_ref[which : which + 1, lanes] += jnp.sum(normed * unit, axis=0, keepdims=True)
+            lifted = normed * gain_ref[which : which + 1, lanes]
+            out_ref[rows, lanes] = lifted
+            term = jnp.sum(lifted * unit, axis=-1, keepdims=True)
+            column = pl.ds(which, 1)
+            if head == 0:
+                terms_ref[rows, column] = term
+            else:
+                terms_ref[rows, column] += term
+
+        def one(i, carry):
+            rows = rows_at(i, block)
+            qpos = qpos_ref[rows, :]
+            mask = (kpos_ref[...] <= qpos) & (qpos <= kmax_ref[...])
+            for head in range(heads):
+                lanes = pl.ds(head * HEAD_DIM, HEAD_DIM)
+                grad = ga_ref[rows, lanes]
+                inverse = 1.0 / ws_ref[rows, pl.ds(head, 1)]
+                drop = jnp.sum(grad * at_ref[rows, lanes], axis=-1, keepdims=True) * inverse
+                grad_num = (grad * inverse).astype(bf16)
+                query, keys = q_ref[rows, lanes], k_ref[:, lanes]
+                scores = dot_nt(query, keys) * (scale * LOG2_E)
+                expo = jnp.where(mask, jnp.exp2(scores), 0.0)
+                grad_expo = dot_nt(grad_num, v_ref[:, lanes])
+                grad_scores = (expo * (grad_expo - drop)).astype(bf16)
+                turn_back(dot_nn(grad_scores, keys) * scale, rows, 0, cq_ref, head)
+                dk_acc[:, lanes] += dot_tn(grad_scores, query)
+                dv_acc[:, lanes] += dot_tn(expo.astype(bf16), grad_num)
+            return carry
+
+        lax.fori_loop(0, row // block, one, 0)
+
+        def last(i, carry):
+            rows = rows_at(i, block)
+            for head in range(heads):
+                lanes = pl.ds(head * HEAD_DIM, HEAD_DIM)
+                turn_back(dk_acc[rows, lanes] * scale, rows, 1, ck_ref, head)
+                dv_ref[rows, lanes] = dv_acc[rows, lanes].astype(bf16)
+            return carry
+
+        lax.fori_loop(0, row // block, last, 0)
+        wait()
+
+    return call(
+        kernel,
+        [
+            shape((row, width), f32),
+            shape((row, width), f32),
+            shape((row, width), bf16),
+            shape((row, 2), f32),
+            shape((2, width), f32),
+            shape((summed.shape[0] // ways, ways * summed.shape[1]), bf16),
+        ],
+        [pltpu.VMEM((row, width), f32)] * 2 + [pltpu.SemaphoreType.DMA((ways,))] * 2,
+        list(parts) + [summed],
+        ident,
+        25,
+        (len(parts),),
+        (5,),
+    )
+
+
+def attn_grads(x_row, grad_qkv, grad_branch, attn_low, gain_columns, summed, ways, ident):
+    row, width = x_row.shape
+    first, second = grad_qkv.shape[1], attn_low.shape[1]
+    cols = first + second + gain_columns.shape[1]
+
+    def kernel(
+        x_far, dq_ref, gb_far, low_ref, gain_ref, sum_ref, out_far, home_ref,
+        x_ref, gb_ref, out_ref, in_sem, out_sem, send, recv
+    ):
+        me = lax.axis_index("seq")
+        fetch = [
+            pltpu.make_async_copy(x_far, x_ref, in_sem.at[0]),
+            pltpu.make_async_copy(gb_far, gb_ref, in_sem.at[1]),
+        ]
+        for copy in fetch:
+            copy.start()
+        greet_line(me, ways)
+        start, wait = home_copies(me, ways, sum_ref, [home_ref], [summed.shape[1]], send, recv)
+        start()
+        for copy in fetch:
+            copy.wait()
+        tile = 256
+
+        def keep(i):
+            rows = rows_at(i, tile)
+            return pltpu.make_async_copy(out_ref.at[rows], out_far.at[rows], out_sem.at[i])
+
+        def one(i, carry):
+            rows = rows_at(i, tile)
+            out_ref[rows, pl.ds(0, first)] = dot_tn(x_ref[:, rows], dq_ref[...]).astype(bf16)
+            out_ref[rows, pl.ds(first, second)] = dot_tn(gb_ref[:, rows], low_ref[...]).astype(bf16)
+            out_ref[rows, pl.ds(first + second, gain_columns.shape[1])] = gain_ref[rows, :]
+            keep(i).start()
+            return carry
+
+        lax.fori_loop(0, width // tile, one, 0)
+
+        def kept(i, carry):
+            keep(i).wait()
+            return carry
+
+        lax.fori_loop(0, width // tile, kept, 0)
+        wait()
+
+    return call(
+        kernel,
+        [
+            shape((width, cols), bf16),
+            shape((summed.shape[0] // ways, ways * summed.shape[1]), bf16),
+        ],
+        [
+            pltpu.VMEM((row, width), bf16),
+            pltpu.VMEM((row, width), bf16),
+            pltpu.VMEM((width, cols), bf16),
+            pltpu.SemaphoreType.DMA((2,)),
+            pltpu.SemaphoreType.DMA((width // 256,)),
+            pltpu.SemaphoreType.DMA((ways,)),
+            pltpu.SemaphoreType.DMA((ways,)),
+        ],
+        [x_row, grad_qkv, grad_branch, attn_low, gain_columns, summed],
+        ident,
+        25,
+        (0, 2, 5),
+        (0, 1),
+    )
 
 
 def exchange(sources, ways, ident, cost):
@@ -1031,68 +1398,49 @@
     )
     squares, w_down_t = lax.optimization_barrier((squares, jnp.transpose(w_down)))
     p_down = lax.all_to_all(w_down_t, "seq", split_axis=1, concat_axis=0, tiled=True)
-    factors = lax.rsqrt(squares / feat_width + norm_eps)
-    q_factor, k_factor = factors[0][:, None], factors[1][:, None]
+    factors = jnp.transpose(lax.rsqrt(squares / feat_width + norm_eps))
     cosine, sine = rope_tables(pos, HEAD_DIM)
-    head_shape = (row_len, own_heads, HEAD_DIM)
-    query_low = rotate((q_raw * q_factor * gain_q).reshape(head_shape), cosine, sine).astype(bf16)
-    key_low = rotate((k_raw * k_factor * gain_k).reshape(head_shape), cosine, sine).astype(bf16)
-    value_low = v_raw.astype(bf16).reshape(head_shape)
-
-    mask = allowed_mask(pos, key_code)[None]
-    scores = jnp.einsum("qhd,khd->hqk", query_low, key_low, preferred_element_type=f32) * score_scale
-    expo = jnp.where(mask, jnp.exp(scores), 0.0)
-    weight_sum = jnp.transpose(jnp.sum(expo, axis=-1))[:, :, None]
-    expo_low = expo.astype(bf16)
-    attn = jnp.einsum("hqk,khd->qhd", expo_low, value_low, preferred_element_type=f32) / weight_sum
-    attn_low = attn.astype(bf16).reshape(row_len, own_feat)
-
-    branch, layer_out, grad_gain_mlp, hidden_low, mixed_low, grad_mlp, grad_gu = attn_out_and_ff(
-        attn_low, m_mid, p_down, token_rows, cotangent[0], gains, groups, ways, 3
-    )
-    d_down = dot_tn(grad_mlp, mixed_low).astype(bf16)
-    d_gu = dot_tn(hidden_low, grad_gu).astype(bf16)
-    grad_gu, d_down, d_gu = lax.optimization_barrier((grad_gu, d_down, d_gu))
-    d_gu = dp_sum(d_gu)
+    key_most = jnp.where(key_code % 2 == 1, jnp.int32(2**30), pos)
+    places = [pos[:, None], pos[None], key_most[None]]
+    gain_qk = jnp.stack([gain_q, gain_k])
+    query_low, key_low, value_low, attn, attn_low, weight_sum = attend(
+        [qkv, factors, cosine, sine, gain_qk] + places, min(row_len, 320)
+    )
+
+    branch, layer_out, grad_gain_mlp, hidden_low, mixed_low, grad_mlp, grad_gu, first_half = (
+        attn_out_and_ff(
+            attn_low, m_mid, p_down, token_rows, cotangent[0], gains, groups, ways, 3
+        )
+    )
+    d_gate = dot_tn(hidden_low, grad_gu[:, :own_ff]).astype(bf16)
+    grad_gu, d_gate = lax.optimization_barrier((grad_gu, d_gate))
+    d_up = dot_tn(hidden_low, grad_gu[:, own_ff:]).astype(bf16)
+    grad_gu, d_up = lax.optimization_barrier((grad_gu, d_up))
+    d_gate, d_up = dp_sum(d_gate), dp_sum(d_up)
+    grad_hidden, grad_gain_attn, grad_branch, grad_attn, d_down = ff_to_attn_back(
+        grad_gu, first_half, m_mid, branch, cotangent[0], gains[2:3], grad_mlp, mixed_low, ways, 5
+    )
     d_down = dp_sum(d_down)
-    grad_hidden, grad_gain_attn, grad_branch, grad_attn = ff_to_attn_back(
-        grad_gu, m_mid, branch, cotangent[0], gains[2:3], ways, 5
-    )
-    grad_attn, d_gu = lax.optimization_barrier((grad_attn, d_gu))
-    d_gu = send_home(d_gu, ways)
-    grad_attn = grad_attn.reshape(head_shape)
-    grad_num = (grad_attn / weight_sum).astype(bf16)
-    drop = jnp.transpose(jnp.sum(grad_attn * attn, axis=-1) / weight_sum[:, :, 0])
-    grad_expo = jnp.einsum("qhd,khd->hqk", grad_num, value_low, preferred_element_type=f32)
-    grad_scores = (expo * (grad_expo - drop[:, :, None])).astype(bf16)
-    grad_q = (
-        jnp.einsum("hqk,khd->qhd", grad_scores, key_low, preferred_element_type=f32) * score_scale
-    )
-    grad_k = (
-        jnp.einsum("hqk,qhd->khd", grad_scores, query_low, preferred_element_type=f32) * score_scale
-    )
-    grad_v = jnp.einsum("hqk,qhd->khd", expo_low, grad_num, preferred_element_type=f32)
-    grad_q_norm = unrotate(grad_q, cosine, sine).reshape(row_len, own_feat)
-    grad_k_norm = unrotate(grad_k, cosine, sine).reshape(row_len, own_feat)
-    q_unit, k_unit = q_raw * q_factor, k_raw * k_factor
-    grad_gain_query = jnp.sum(grad_q_norm * q_unit, axis=0)
-    grad_gain_key = jnp.sum(grad_k_norm * k_unit, axis=0)
-    c_q, c_k = grad_q_norm * gain_q, grad_k_norm * gain_k
-    terms = jnp.stack([jnp.sum(c_q * q_unit, axis=-1), jnp.sum(c_k * k_unit, axis=-1)])
-    terms, d_down, d_gu = lax.optimization_barrier((terms, d_down, d_gu))
+    c_q, c_k, grad_v, terms, gain_part, dw_gate = attend_back(
+        [query_low, key_low, value_low, grad_attn, attn, weight_sum]
+        + [cosine, sine, qkv, factors, gain_qk]
+        + places,
+        d_gate,
+        min(row_len, 320),
+        ways,
+        13,
+    )
+    terms = jnp.transpose(terms)
     means = line_sum(terms, ways, 6) / feat_width
-    d_down = send_home(d_down, ways)
-    dw_gu = split_grads(d_gu, [own_ff, own_ff], ways)
-    grad_q_raw = q_factor * (c_q - q_unit * means[0][:, None])
-    grad_k_raw = k_factor * (c_k - k_unit * means[1][:, None])
+    q_factor, k_factor = factors[:, :1], factors[:, 1:]
+    grad_q_raw = q_factor * (c_q - q_raw * q_factor * means[0][:, None])
+    grad_k_raw = k_factor * (c_k - k_raw * k_factor * means[1][:, None])
     grad_qkv = jnp.concatenate(
-        [grad_q_raw, grad_k_raw, grad_v.reshape(row_len, own_feat)], axis=1
-    ).astype(bf16)
+        [grad_q_raw.astype(bf16), grad_k_raw.astype(bf16), grad_v], axis=1
+    )
 
     own_slot = jnp.zeros((2, feat_width), f32)
-    own_slot = lax.dynamic_update_slice(
-        own_slot, jnp.stack([grad_gain_query, grad_gain_key]), (0, me * own_feat)
-    )
+    own_slot = lax.dynamic_update_slice(own_slot, gain_part, (0, me * own_feat))
     gain_terms = jnp.concatenate(
         [
             own_slot,
@@ -1101,14 +1449,17 @@
         ]
     )
     gain_columns = jnp.pad(jnp.transpose(gain_terms), ((0, 0), (0, HEAD_DIM - 4)))
-    d_attn = jnp.concatenate(
-        [dot_tn(x_row, grad_qkv), dot_tn(grad_branch, attn_low), gain_columns], axis=1
-    ).astype(bf16)
-    grad_qkv, d_attn, d_down = lax.optimization_barrier((grad_qkv, d_attn, d_down))
-    dw_down = split_grads(d_down, [own_ff], ways)
-    grad_tokens = project_back(grad_qkv, m_qkv, grad_hidden, ways, 7)
+    d_attn, dw_up = attn_grads(
+        x_row, grad_qkv, grad_branch, attn_low, gain_columns.astype(bf16), d_up, ways, 14
+    )
+    grad_qkv, d_attn = lax.optimization_barrier((grad_qkv, d_attn))
+    grad_tokens, dw_down = project_back(grad_qkv, m_qkv, grad_hidden, d_down, ways, 7)
     grad_tokens, d_attn = lax.optimization_barrier((grad_tokens, dp_sum(d_attn)))
-    dw_qkv = split_grads(send_home(d_attn, ways), [own_feat] * 4 + [HEAD_DIM], ways)
+    dw_gu = [dw_gate.astype(f32), dw_up.astype(f32)]
+    dw_qkv = bring_home(d_attn, [own_feat] * 4 + [HEAD_DIM], ways, 12)
+    dw_qkv = [part.astype(f32) for part in dw_qkv]
+    dw_gu = [dw_gate.astype(f32), dw_up.astype(f32)]
+    dw_down = [dw_down.astype(f32)]
     gain_grads = jnp.sum(dw_qkv[4].reshape(-1, ways, HEAD_DIM), axis=1)
     gain_grads = jnp.transpose(gain_grads[:, :8])
     return (

time: 698 us -> 673 us (0.964)
  Pallas kernels: 462 us -> 572 us
  matrix products: 72.6 us -> 21.7 us
  waiting for transfers between devices: 40.7 us -> 4.47 us
  local copies, waits for them, and re-layouts: 38.5 us -> 15.3 us
  starting transfers between devices: 28 us -> 5.99 us
    pallas_call x6 -> x9, Pallas kernels: 383 us -> 482 us  [call(): pl.pallas_call(kernel, out_shape=outs, in_specs=[space(i, far_in) for i i...]
    all_to_all x3 -> x0, waiting for transfers between devices: 39.1 us -> none  [send_home(): lax.all_to_all(summed, 'seq', split_axis=0, concat_axis=1, tiled=True)]
    dot_general x6 -> x0, matrix products: 32.1 us -> none  [the longest x1 9.89 us: body(): jnp.einsum('qhd,khd->hqk', grad_num, value_low, preferred_element_type=f32)]
    all_to_all x3 -> x0, starting transfers between devices: 21.7 us -> none  [send_home(): lax.all_to_all(summed, 'seq', split_axis=0, concat_axis=1, tiled=True)]
    dot_general x4 -> x2, matrix products: 39.3 us -> 20.4 us  [dot_tn(): lax.dot_general(left, right, (((0,), (0,)), ((), ())), preferred_element_...]
    unnamed x77 -> x33, local copies, waits for them, and re-layouts: 14.9 us -> 4.22 us
    pallas_call x0 -> x1, Pallas kernels: none -> 10.6 us  [attend(): pl.pallas_call(kernel, out_shape=[shape((row, width), bf16)] * 3 + [shape...]
    convert_element_type x2 -> x6, other arithmetic: 0.91 us -> 10.7 us  [the longest x3 4.48 us: body(): dw_qkv = [part.astype(f32) for part in dw_qkv]]
  transfers between devices with their start and end apart: 9 -> 7, of which waited for: 4 -> 1; matrix products, arithmetic and copies ran while one was open for 14% -> 7% of each run, Pallas kernels for 39% -> 51%
where the time goes in v4:
time: 673 us; the launch traced here: 664 us
  Pallas kernels  572 us (85%)
  other arithmetic  29.1 us (4%)
  matrix products  21.7 us (3%)
  between operations  15.6 us (2%)
  local copies, waits for them, and re-layouts  15.3 us (2%)
    pallas_call x9, Pallas kernels, call(): pl.pallas_call(kernel, out_shape=outs, in_specs=[space(i, far_in) for i i...  482 us
    pallas_call x2, Pallas kernels, exchange(): pl.pallas_call(kernel, out_shape=shape((ways * rows, sum(widths)), bf16),...  79.5 us
    dot_general x2, matrix products, dot_tn(): lax.dot_general(left, right, (((0,), (0,)), ((), ())), preferred_element_...  20.4 us
  transfers between devices with their start and end apart: 7, of which 1 were waited for; matrix products, arithmetic and copies ran while one was open for 7% of the time, Pallas kernels for 51%

profile of v4, /device:TPU:9, one launch (start us, length us, event | category | flops | bytes accessed | tf_op | source)
XLA Modules:
  0.0 664.2 jit_solution(526800196923680413)
XLA Ops:
  7.2 0.7 pad_maximum_fusion.5
  8.1 0.7 copy.79
  8.8 24.7 %shard_map.255 = bf16[512,896]{1,0:T(8,128)(2,1)} custom-call(bf16[64,2048]{1,0:T(8,128)(2,1)} %refs_0_.1, bf16[64,2048]{1,0:T(8,128)(2,1)} %refs_1_.1, bf16[64,2048]{1,0:T(8,128)(2,1)} %refs_2_.1, bf16[64,1024]{1,0:T(8,128)(2,1)} %bitcast.50), custom_call_target="tpu_custom_call" | custom-call | flops 20000000000 | bytes 60000000 | tf_op jit(solution)/shard_map/pallas_call | solution.py:1285
  33.5 54.8 %shard_map.256 = bf16[512,2304]{1,0:T(8,128)(2,1)} custom-call(bf16[64,8192]{1,0:T(8,128)(2,1)} %refs_0_.2, bf16[64,8192]{1,0:T(8,128)(2,1)} %refs_1_.2, bf16[64,2048]{1,0:T(8,128)(2,1)} %bitcast.64), custom_call_target="tpu_custom_call" | custom-call | flops 49999998976 | bytes 150000000 | tf_op jit(solution)/shard_map/pallas_call | solution.py:1285
  89.6 1.3 fusion.13
  91.5 46.9 %shard_map.257 = (bf16[1280,2048]{1,0:T(8,128)(2,1)}, s32[8,1,256]{2,1,0:T(1,128)}, f32[1280,768]{1,0:T(8,128)}) custom-call(bf16[160,2048]{1,0:T(8,128)(2,1)} %bitcast.60, s32[1,256]{1,0:T(1,128)} %bitcast.55, bf16[2048,896]{1,0:T(8,128)(2,1)} %all-gather.3.cloned.1.call-done.w_far.w_ref), custom_call_target="tpu_custom_call" | custom-call | flops 54999998464 | bytes 165000000 | tf_op jit(solution)/shard_map/pallas_call | solution.py:453
  138.4 0.7 slice_reduce_fusion.4
  139.7 2.1 multiply_reduce_fusion.1
  141.8 0.6 pad_maximum_fusion.3.terms_ref
  142.4 11.6 %shard_map.258 = f32[2,1280]{1,0:T(2,128)} custom-call(f32[2,1280]{1,0:T(2,128)} %pad_maximum_fusion.3.terms_ref), custom_call_target="tpu_custom_call" | custom-call | flops 8000000000 | bytes 24000000 | tf_op jit(solution)/shard_map/pallas_call | solution.py:453
  154.0 0.7 rsqrt_bitcast_fusion
  154.8 1.1 copy.66.factor_ref
  155.9 2.3 copy.78
  158.1 5.3 all-to-all-start
  163.5 1.3 fusion.6.gains_ref
  164.7 0.6 fusion.14
  166.2 3.4 fusion.4
  169.7 0.6 compare_select_fusion
  170.3 1.2 add_select_fusion.qpos_ref
  171.5 10.6 %shard_map.259 = (bf16[1280,256]{1,0:T(8,128)(2,1)}, bf16[1280,256]{1,0:T(8,128)(2,1)}, bf16[1280,256]{1,0:T(8,128)(2,1)}, f32[1280,256]{1,0:T(8,128)}, bf16[1280,256]{1,0:T(8,128)(2,1)}, /*index=5*/f32[1280,2]{1,0:T(8,128)}) custom-call(f32[1280,768]{1,0:T(8,128)} %get-tuple-element.68.qkv_ref, f32[1280,2]{1,0:T(8,128)} %copy.66.factor_ref, ...), custom_call_target="tpu_custom_call" | custom-call | flops 1677721600 | bytes 60000000 | tf_op jit(solution)/shard_map/pallas_call | solution.py:1068
  182.2 4.3 all-to-all-done
  186.5 177.3 %shard_map.260 = (f32[160,2048]{1,0:T(8,128)}, bf16[160,2048]{1,0:T(8,128)(2,1)}, f32[8,2048]{1,0:T(8,128)}, bf16[1280,2048]{1,0:T(8,128)(2,1)}, bf16[1280,1024]...) custom-call(bf16[1280,256]{1,0:T(8,128)(2,1)} %get-tuple-element.71.left_far.low_ref,, ...), custom_call_target="tpu_custom_call" | custom-call | flops 149999992832 | bytes 450000000 | tf_op jit(solution)/shard_map/pallas_call | solution.py:453
  363.8 10.2 %convolution_convert_fusion.1 = bf16[2048,1024]{1,0:T(8,128)(2,1)} fusion(bf16[1280,2048]{1,0:T(8,128)(2,1)} %get-tuple-element.78, bf16[1280,2048]{1,0:T(8,128)(2,1)} %get-tuple-element.80.left), kind=kOutput, calls=%fused_computation.1 | convolution fusion | flops 5370806272 | bytes 12058624 | tf_op jit(solution)/shard_map/dot_general | solution.py:70
  374.4 10.2 %convolution_convert_fusion = bf16[2048,1024]{1,0:T(8,128)(2,1)} fusion(bf16[1280,2048]{1,0:T(8,128)(2,1)} %get-tuple-element.78, bf16[1280,2048]{1,0:T(8,128)(2,1)} %get-tuple-element.80.left), kind=kOutput, calls=%fused_computation | convolution fusion | flops 5370806272 | bytes 12058624 | tf_op jit(solution)/shard_map/dot_general | solution.py:70
  384.6 73.9 %shard_map.261 = (f32[160,2048]{1,0:T(8,128)}, f32[8,2048]{1,0:T(8,128)}, bf16[1280,2048]{1,0:T(8,128)(2,1)}, f32[1280,256]{1,0:T(8,128)}, bf16[2048,1024]{1,0:T(8,128)(2,1)}) custom-call(bf16[1280,2048]{1,0:T(8,128)(2,1)} %get-tuple-element.80.left, f32[80,2048]{1,0:T(8,128)} %get-tuple-element.81.first_ref, ...), custom_call_target="tpu_custom_call" | custom-call | flops 70000001024 | bytes 210000000 | tf_op jit(solution)/shard_map/pallas_call | solution.py:453
  459.5 37.4 %shard_map.262 = (f32[1280,256]{1,0:T(8,128)}, f32[1280,256]{1,0:T(8,128)}, bf16[1280,256]{1,0:T(8,128)(2,1)}, f32[1280,2]{1,0:T(8,128)}, f32[2,256]{1,0:T(2,128)}, /*index=5*/bf16[64,8192]{1,0:T(8,128)(2,1)}) custom-call(bf16[1280,256]{1,0:T(8,128)(2,1)} %get-tuple-element.74.q_ref, bf16[1280,256]{1,0:T(8,128)(2,1)} %get-tuple-element.75.k_ref, ...), custom_call_target="tpu_custom_call" | custom-call | flops 24999999488 | bytes 75000000 | tf_op jit(solution)/shard_map/pallas_call | solution.py:453
  497.0 1.9 copy.69
  498.9 0.7 constant_dynamic-update-slice_fusion
  499.9 0.9 pad.15.gain_ref
  500.8 6.1 shard_map.263
  506.9 0.7 broadcast_multiply_fusion.1
  507.7 3.3 multiply_convert_fusion.1
  511.0 1.4 pad_maximum_fusion.dq_ref.left
  512.4 28.6 %shard_map.264 = (bf16[2048,1152]{1,0:T(8,128)(2,1)}, bf16[64,8192]{1,0:T(8,128)(2,1)}) custom-call(bf16[1280,2048]{1,0:T(8,128)(2,1)} %get-tuple-element.93.x_far, bf16[1280,768]{1,0:T(8,128)(2,1)} %pad_maximum_fusion.dq_ref.left, bf16[1280,2048]{1,0:T(8,128)(2,1)} %get-tuple-element.94.gb_far, bf16[1280,256]{1,0:T(8,128)(2,1)} %get-tuple-element.71.left_far.low_ref, ...), custom_call_target="tpu_custom_call" | custom-call | flops 24999999488 | bytes 75000000 | tf_op jit(solution)/shard_map/pallas_call | solution.py:453
  541.1 1.2 copy-done.1
  542.3 1.5 convert_element_type.64
  543.7 1.5 convert_element_type.63
  545.2 68.9 %shard_map.265 = (bf16[160,2048]{1,0:T(8,128)(2,1)}, bf16[64,8192]{1,0:T(8,128)(2,1)}) custom-call(bf16[1280,768]{1,0:T(8,128)(2,1)} %pad_maximum_fusion.dq_ref.left, bf16[2048,896]{1,0:T(8,128)(2,1)} %all-gather.3.cloned.1.call-done.w_far.w_ref, f32[160,2048]{1,0:T(8,128)} %get-tuple-element.101.gh_ref, ...), custom_call_target="tpu_custom_call" | custom-call | flops 65000001536 | bytes 195000000 | tf_op jit(solution)/shard_map/pallas_call | solution.py:453
  614.1 2.7 convert_bitcast_fusion
  616.7 31.2 %shard_map.266 = (bf16[64,2048]{1,0:T(8,128)(2,1)}, bf16[64,2048]{1,0:T(8,128)(2,1)}, bf16[64,2048]{1,0:T(8,128)(2,1)}, bf16[64,2048]{1,0:T(8,128)(2,1)}, bf16[64,1024]{1,0:T(8,128)(2,1)}) custom-call(bf16[512,1152]{1,0:T(8,128)(2,1)} %reduce-scatter.11.cloned.1.call-done.refs_0_), custom_call_target="tpu_custom_call" | custom-call | flops 30000001024 | bytes 90000000 | tf_op jit(solution)/shard_map/pallas_call | solution.py:453
  648.0 1.9 convert_element_type.60
  649.9 1.0 convert_bitcast_fusion.2
  651.0 0.7 slice_reduce_fusion
  651.8 1.8 convert_element_type.61
  653.6 0.8 convert_element_type.62
  654.4 0.8 convert_bitcast_fusion.1
  655.2 0.8 copy.85
  656.1 0.8 copy.86
  (75 shorter events, 4.6 us)
Async XLA Ops:
  7.2 84.3 %all-gather.3.cloned.1.call-start = ((), (), s32[]{:S(2)}) async-start(), calls=%async_computation.5 | async-start | bytes 4587520 | tf_op jit(solution)/shard_map/all_gather | solution.py:74
  33.5 153.0 %all-gather.5.cloned.1.call-start = ((), (), s32[]{:S(2)}) async-start(), calls=%async_computation.6 | async-start | bytes 11796480 | tf_op jit(solution)/shard_map/all_gather | solution.py:74
  33.5 55.5 %copy-start.12 = (s32[1,2]{1,0:T(1,128)S(1)}, s32[1,2]{1,0:T(1,128)}, u32[]{:S(2)}) copy-start(s32[1,2]{1,0:T(1,128)} %param.31) | copy-start | bytes 28
  33.5 56.1 %copy-start.13 = (s32[1,160]{1,0:T(1,128)S(1)}, s32[1,160]{1,0:T(1,128)}, u32[]{:S(2)}) copy-start(s32[1,160]{1,0:T(1,128)} %param.29) | copy-start | bytes 1924
  154.7 10.0 %copy-start.8 = (f32[1280,2]{0,1:T(2,128)}, f32[1280,2]{0,1:T(2,128)S(1)}, u32[]{:S(2)}) copy-start(f32[1280,2]{0,1:T(2,128)S(1)} %rsqrt_bitcast_fusion) | copy-start | bytes 30724
  158.1 28.4 %all-to-all-start = ((bf16[64,8,1024]{2,0,1:T(8,128)(2,1)}), bf16[64,8,1024]{2,0,1:T(8,128)(2,1)}, u32[]{:S(2)}, u32[]{:S(2)}) async-start(bf16[64,8,1024]{2,0,1:T(8,128)(2,1)} %bitcast.41), calls=%async_computation | async-start | bytes 2097152 | tf_op jit(solution)/shard_map/all_to_all | solution.py:1400
  163.5 296.1 %reduce-scatter.5.cloned.1.call-start = ((), (), s32[]{:S(2)}) async-start(), calls=%async_computation.7 | async-start | bytes 5242880 | tf_op jit(solution)/shard_map/reduce_scatter | solution.py:78
  164.7 17.4 %copy-start.7 = (f32[8,2048]{1,0:T(8,128)}, f32[8,2048]{1,0:T(8,128)S(1)}, u32[]{:S(2)}) copy-start(f32[8,2048]{1,0:T(8,128)S(1)} %fusion.6.gains_ref) | copy-start | bytes 196612
  374.1 138.3 %reduce-scatter.7.cloned.1.call-start = ((), (), s32[]{:S(2)}) async-start(), calls=%async_computation.8 | async-start | bytes 5242880 | tf_op jit(solution)/shard_map/reduce_scatter | solution.py:78
  384.6 160.6 %reduce-scatter.9.cloned.1.call-start = ((), (), s32[]{:S(2)}) async-start(), calls=%async_computation.9 | async-start | bytes 5242880 | tf_op jit(solution)/shard_map/reduce_scatter | solution.py:78
  458.5 0.7 copy-start.9
  458.6 0.8 copy-start.10
  458.6 0.9 copy-start.11
  458.6 158.1 %reduce-scatter.11.cloned.1.call-start = ((), (), s32[]{:S(2)}) async-start(), calls=%async_computation.10 | async-start | bytes 5898240 | tf_op jit(solution)/shard_map/reduce_scatter | solution.py:78
  507.7 3.3 copy-start.4
  541.0 1.2 copy-start.1
  541.1 2.7 copy-start
  648.0 5.6 copy-start.6
  648.0 6.4 copy-start.5
  648.0 7.2 %copy-start.2 = (bf16[160,2048]{1,0:T(8,128)(2,1)S(1)}, bf16[160,2048]{1,0:T(8,128)(2,1)}, u32[]{:S(2)}) copy-start(bf16[160,2048]{1,0:T(8,128)(2,1)} %get-tuple-element.73) | copy-start | bytes 1966084
  649.9 6.2 copy-start.3
Sparse Core Ops, SparseCore 0:
  33.6 48.8 all-gather.2
  88.5 96.8 all-gather.4
  374.2 55.4 reduce-scatter.4
  432.8 52.7 reduce-scatter.6
  488.4 52.7 reduce-scatter.8
  544.3 57.0 reduce-scatter.10

commit v5 on v4

--- a/solution.py
+++ b/solution.py
@@ -16,17 +16,6 @@
 LOG2_E = 1.4426950408889634
 f32 = jnp.float32
 bf16 = jnp.bfloat16
-
-
-def rms_factor(values):
-    return lax.rsqrt(jnp.mean(values * values, axis=-1, keepdims=True) + norm_eps)
-
-
-def norm_back(grad_normed, raw_values, factor):
-    unit_values = raw_values * factor
-    return factor * (
-        grad_normed - unit_values * jnp.mean(grad_normed * unit_values, axis=-1, keepdims=True)
-    )
 
 
 def rope_tables(positions, head_dim):
@@ -36,26 +25,6 @@
     angle = positions.astype(f32)[:, None] * inv_freq[None, :]
     angle = jnp.concatenate([angle, angle], axis=-1)
     return (jnp.cos(angle), jnp.sin(angle))
-
-
-def rotate(values, cosine, sine):
-    half_dim = values.shape[-1] // 2
-    turned = jnp.concatenate([-values[..., half_dim:], values[..., :half_dim]], axis=-1)
-    return values * cosine + turned * sine
-
-
-def unrotate(grads, cosine, sine):
-    half_dim = grads.shape[-1] // 2
-    moved = grads * sine
-    back_part = jnp.concatenate([moved[..., half_dim:], -moved[..., :half_dim]], axis=-1)
-    return grads * cosine + back_part
-
-
-def allowed_mask(query_pos, key_code):
-    key_pos = key_code // 2
-    usable = key_code % 2 == 1
-    causal = key_pos[None, :] <= query_pos[:, None]
-    return causal & (usable[None, :] | (key_pos[None, :] == query_pos[:, None]))
 
 
 def dot_nn(left, right):
@@ -186,17 +155,18 @@
 
     def use_at(self, away, h, use):
         line = self.line
-        low, high = line.chip - away, line.chip + away
-
-        @pl.when(low >= 0)
-        def _():
-            self.swap(low, 1 - line.core, h).wait_recv()
-            use(low, h)
-
-        @pl.when((high <= line.last) & (away > 0))
-        def _():
-            self.swap(high, 1 - line.core, h).wait_recv()
-            use(high, h)
+
+        def one(side, carry):
+            src = line.chip + (2 * side - 1) * away
+
+            @pl.when((src >= 0) & (src <= line.last) & (away + 1 > side))
+            def _():
+                self.swap(src, 1 - line.core, h).wait_recv()
+                use(src, h)
+
+            return carry
+
+        lax.fori_loop(0, 2, one, 0)
 
     def finish(self):
         line = self.line
@@ -303,11 +273,23 @@
         )
 
     def make(self, s, h):
-        for dest, _, _, there in self.legs(s):
+        line = self.line
+        if self.joined and h:
+            return
+        (up, _, _, has_up), (down, _, _, has_down) = self.legs(s)
+
+        def one(k, carry):
+            own, low = k // 2, k % 2
+            dest = own * line.chip + (1 - own) * ((1 - low) * up + low * down)
+            there = ((k == 0) & has_up) | ((k == 1) & has_down) | ((k == 2) & (s == line.last))
 
             @pl.when(there)
-            def _(dest=dest):
+            def _():
                 self.produce(dest, h)
+
+            return carry
+
+        lax.fori_loop(0, 3, one, 0)
 
     def pass_on(self, s, h):
         line = self.line
@@ -388,25 +370,25 @@
         lax.fori_loop(0, line.chips, one, 0)
 
 
-def advance(scatter=None, sh=0, gather=None, gh=0, use=None, fill=None):
+def advance(scatter=None, sh=0, gather=None, gh=0, use=None, fill=None, settle=None):
     line = (scatter or gather).line
-    if scatter:
-        scatter.make(0, sh)
-
-    def slot(s, carry):
+
+    def slot(i, carry):
+        s = i - 1
         if gather:
 
-            @pl.when(s > 0)
+            @pl.when((s > 0) & (s < line.chips))
             def _():
                 gather.receive(s, gh)
 
         if scatter:
             scatter.pass_on(s, sh)
             scatter.make(s + 1, sh)
-
-            @pl.when(s == line.last - 1)
+        if settle:
+
+            @pl.when(s == line.chips)
             def _():
-                scatter.produce(line.chip, sh)
+                settle()
 
         if gather:
 
@@ -415,10 +397,14 @@
                 gather.use_at(s - 1, gh, use)
 
         if fill:
-            fill(s)
+
+            @pl.when((s >= 0) & (s < line.chips))
+            def _():
+                fill(s)
+
         return carry
 
-    lax.fori_loop(0, line.chips, slot, 0)
+    lax.fori_loop(0, line.chips + 2, slot, 0)
 
 
 def mean_rows(values):
@@ -511,15 +497,18 @@
             outs.send(1, chip, h)
 
         def step(j, carry):
-            for h in (0, 1):
-                gather.receive(j, h)
+            def one(h, carry):
+                @pl.when(j < line.chips)
+                def _():
+                    gather.receive(j, h)
+
                 gather.use_at(j - 1, h, use)
-            return carry
+                return carry
+
+            return lax.fori_loop(0, 2, one, carry)
 
         w_copy.wait()
-        lax.fori_loop(1, line.chips, step, 0)
-        for h in (0, 1):
-            gather.use_at(line.last, h, use)
+        lax.fori_loop(1, line.chips + 1, step, 0)
         gather.finish()
         outs.finish()
         for off in range(1, ways):
@@ -637,17 +626,22 @@
                 mlp = scatter.total(h, strip)
                 factor = lax.rsqrt(mean_rows(mlp * mlp) + norm_eps)
                 unit = mlp * factor
-                grad = go_ref[at, :].astype(f32)
-                out_ref[at, :] = (residual(at) + unit * gain_mlp).astype(bf16)
-                terms = grad * unit
-                gg_ref[...] += terms[:8] + terms[8:]
-                lifted = grad * gain_mlp
+                lifted = go_ref[at, :].astype(f32) * gain_mlp
                 turned = factor * (lifted - unit * mean_rows(lifted * unit))
                 gm_ref[own(h, strip), :] = turned.astype(bf16)
+
+            def rest_of(strip):
+                at = pl.ds(pl.multiple_of(h * half + strip.start, 16), strip.size)
+                mlp = scatter.total(h, strip)
+                unit = mlp * lax.rsqrt(mean_rows(mlp * mlp) + norm_eps)
+                out_ref[at, :] = (residual(at) + unit * gain_mlp).astype(bf16)
+                terms = go_ref[at, :].astype(f32) * unit
+                gg_ref[...] += terms[:8] + terms[8:]
 
             scatter.close(h)
             each_strip(half, 16, one)
             back.start(h)
+            each_strip(half, 16, rest_of)
             scatter.finish(h)
 
         def gate_up(chip, h):
@@ -681,12 +675,10 @@
         for copy in fetch[:3]:
             copy.wait()
         scatter.of(left, mid_ref.at[:, out_cols], 1024, True)
-        advance(scatter, 0)
+        advance(scatter, 0, settle=lambda: settle_attn(0))
         fetch[3].wait()
-        settle_attn(0)
-        advance(scatter, 1, hidden, 0, gate_up)
-        settle_attn(1)
-        hidden.use_at(line.last, 0, gate_up)
+        advance(scatter, 1, hidden, 0, gate_up, settle=lambda: settle_attn(1))
+
         def turn_down(i, carry):
             rows = rows_at(i, square_tile)
             down_turned[:, rows] = down_ref[rows, :].T
@@ -715,22 +707,21 @@
             scatter.of(mix_ref, down_turned, 2048, False, True)
         else:
             scatter.of(mix_ref, down_ref, 2048, False)
-        advance(scatter, 0, hidden, 1, gate_up)
-        settle_mlp(0)
-        hidden.use_at(line.last, 1, gate_up)
-        advance(scatter, 1, back, 0, gate_up_back, turn_square if square else None)
-        settle_mlp(1)
-        back.use_at(line.last, 0, gate_up_back)
+        advance(scatter, 0, hidden, 1, gate_up, settle=lambda: settle_mlp(0))
+        advance(
+            scatter, 1, back, 0, gate_up_back, turn_square if square else None, lambda: settle_mlp(1)
+        )
         scatter.of(dgu_ref, mid_ref.at[:, gu_cols], 1024, False, square)
-        advance(scatter, 0, back, 1, gate_up_back)
-        back.use_at(line.last, 1, gate_up_back)
-
-        def put(strip):
-            first_ref[strip, :] = scatter.total(0, strip)
-
-        scatter.close(0)
-        each_strip(half, 16, put)
-        scatter.finish(0)
+
+        def keep_first():
+            def put(strip):
+                first_ref[strip, :] = scatter.total(0, strip)
+
+            scatter.close(0)
+            each_strip(half, 16, put)
+            scatter.finish(0)
+
+        advance(scatter, 0, back, 1, gate_up_back, settle=keep_first)
         hidden.finish()
         back.finish()
         keep_branch.wait()
@@ -797,26 +788,26 @@
 
         def fetch(i):
             return pltpu.make_async_copy(
-                gm_far.at[:, pl.ds(i * 256, 256)], gm_ref.at[i % 2], gm_sem.at[i % 2]
+                gm_far.at[:, rows_at(i, 256)], gm_ref.at[i % 2], gm_sem.at[i % 2]
             )
 
         def keep(i):
-            rows = pl.ds(i * 256, 256)
+            rows = rows_at(i, 256)
             return pltpu.make_async_copy(dd_ref.at[rows], dd_far.at[rows], dd_sem.at[i])
 
-        def down_grad(i):
+        def down_grad(i, carry):
             fetch(i).wait()
-            if i + 1 < tiles:
+
+            @pl.when(i + 1 < tiles)
+            def _():
                 fetch(i + 1).start()
-            dd_ref[pl.ds(i * 256, 256), :] = dot_tn(gm_ref[i % 2], mix_ref[...]).astype(bf16)
+
+            dd_ref[rows_at(i, 256), :] = dot_tn(gm_ref[i % 2], mix_ref[...]).astype(bf16)
             keep(i).start()
+            return carry
 
         def fill(s):
-            for i in range(tiles):
-
-                @pl.when(s == i * line.chips // tiles)
-                def _(i=i):
-                    down_grad(i)
+            lax.fori_loop(s * tiles // line.chips, (s + 1) * tiles // line.chips, down_grad, 0)
 
         outs = Blocks(line, 2 * half, [(all_ref, all_far)], out_sem)
         line.greet()
@@ -854,14 +845,11 @@
 
         scatter.of(left, w_ref.at[:, pl.ds(0, 2 * own_ff)], 1024, False)
         settle(0)
-        advance(scatter, 1, gather, 0, use)
-        settle(1)
-        gather.use_at(line.last, 0, use)
+        advance(scatter, 1, gather, 0, use, settle=lambda: settle(1))
         mix_copy.start()
         fetch(0).start()
         mix_copy.wait()
         advance(None, 0, gather, 1, use, fill)
-        gather.use_at(line.last, 1, use)
         gather.finish()
         outs.finish()
         for i in range(tiles):
@@ -1297,6 +1285,30 @@
         ),
         compiler_params=pltpu.CompilerParams(collective_id=ident, has_side_effects=True),
     )(*sources)
+
+
+def finish_grads(grads, kept, gains, ways):
+    rows, count = gains.shape[0], len(grads)
+    parts = list(grads) + list(kept) + [gains]
+
+    def kernel(*refs):
+        ins, outs = refs[: len(parts)], refs[len(parts) :]
+        for i in range(len(parts) - 1):
+            outs[i][...] = ins[i][...].astype(outs[i].dtype)
+        total = ins[-1][:, pl.ds(0, HEAD_DIM)].astype(f32)
+        for off in range(1, ways):
+            total = total + ins[-1][:, pl.ds(off * HEAD_DIM, HEAD_DIM)].astype(f32)
+        outs[-1][...] = total.T[:8, :]
+
+    return pl.pallas_call(
+        kernel,
+        out_shape=[shape(part.shape, f32 if i < count else part.dtype) for i, part in enumerate(parts[:-1])]
+        + [shape((8, rows), f32)],
+        in_specs=[pl.BlockSpec(memory_space=pltpu.VMEM)] * len(parts),
+        out_specs=[pl.BlockSpec(memory_space=pltpu.VMEM)] * len(parts),
+        cost_estimate=pl.CostEstimate(flops=10**6, transcendentals=0, bytes_accessed=10**7),
+        compiler_params=pltpu.CompilerParams(vmem_limit_bytes=60 * 2**20),
+    )(*parts)
 
 
 def line_sum(terms, ways, ident):
@@ -1404,7 +1416,7 @@
     places = [pos[:, None], pos[None], key_most[None]]
     gain_qk = jnp.stack([gain_q, gain_k])
     query_low, key_low, value_low, attn, attn_low, weight_sum = attend(
-        [qkv, factors, cosine, sine, gain_qk] + places, min(row_len, 320)
+        [qkv, factors, cosine, sine, gain_qk] + places, min(row_len, 160)
     )
 
     branch, layer_out, grad_gain_mlp, hidden_low, mixed_low, grad_mlp, grad_gu, first_half = (
@@ -1426,7 +1438,7 @@
         + [cosine, sine, qkv, factors, gain_qk]
         + places,
         d_gate,
-        min(row_len, 320),
+        min(row_len, 160),
         ways,
         13,
     )
@@ -1452,26 +1464,25 @@
     d_attn, dw_up = attn_grads(
         x_row, grad_qkv, grad_branch, attn_low, gain_columns.astype(bf16), d_up, ways, 14
     )
-    grad_qkv, d_attn = lax.optimization_barrier((grad_qkv, d_attn))
+    dw_gu = [dw_gate.astype(f32), dw_up.astype(f32)]
+    grad_qkv, d_attn, dw_gu = lax.optimization_barrier((grad_qkv, d_attn, dw_gu))
     grad_tokens, dw_down = project_back(grad_qkv, m_qkv, grad_hidden, d_down, ways, 7)
     grad_tokens, d_attn = lax.optimization_barrier((grad_tokens, dp_sum(d_attn)))
     dw_gu = [dw_gate.astype(f32), dw_up.astype(f32)]
     dw_qkv = bring_home(d_attn, [own_feat] * 4 + [HEAD_DIM], ways, 12)
-    dw_qkv = [part.astype(f32) for part in dw_qkv]
-    dw_gu = [dw_gate.astype(f32), dw_up.astype(f32)]
-    dw_down = [dw_down.astype(f32)]
-    gain_grads = jnp.sum(dw_qkv[4].reshape(-1, ways, HEAD_DIM), axis=1)
-    gain_grads = jnp.transpose(gain_grads[:, :8])
+    d_query, d_key, d_value, d_out, d_down, layer_out, grad_tokens, gain_grads = finish_grads(
+        list(dw_qkv[:4]) + [dw_down], [layer_out, grad_tokens], dw_qkv[4], ways
+    )
     return (
         layer_out[None],
         grad_tokens[None],
-        dw_qkv[0],
-        dw_qkv[1],
-        dw_qkv[2],
-        jnp.transpose(dw_qkv[3]),
+        d_query,
+        d_key,
+        d_value,
+        jnp.transpose(d_out),
         dw_gu[0],
         dw_gu[1],
-        jnp.transpose(dw_down[0]),
+        jnp.transpose(d_down),
         gain_grads[0],
         gain_grads[1],
         gain_grads[2],

time: 673 us -> 660 us (0.981); the launches traced: 664 us -> 659 us
  Pallas kernels: 572 us -> 580 us
  other arithmetic: 29.1 us -> 21.4 us
  transfers between devices with their start and end apart: 7 -> 7, of which waited for: 1 -> 1; matrix products, arithmetic and copies ran while one was open for 7% -> 6% of each run, Pallas kernels for 51% -> 52%
where the time goes in v5:
time: 660 us; the launch traced here: 659 us
  Pallas kernels  580 us (88%)
  matrix products  21.9 us (3%)
  other arithmetic  21.4 us (3%)
  between operations  15.1 us (2%)
  local copies, waits for them, and re-layouts  13.2 us (2%)
    pallas_call x9, Pallas kernels, call(): pl.pallas_call(kernel, out_shape=outs, in_specs=[space(i, far_in) for i i...  483 us
    pallas_call x2, Pallas kernels, exchange(): pl.pallas_call(kernel, out_shape=shape((ways * rows, sum(widths)), bf16),...  79.5 us
    dot_general x2, matrix products, dot_tn(): lax.dot_general(left, right, (((0,), (0,)), ((), ())), preferred_element_...  20.6 us
  transfers between devices with their start and end apart: 7, of which 1 were waited for; matrix products, arithmetic and copies ran while one was open for 6% of the time, Pallas kernels for 52%

profile of v5, /device:TPU:9, one launch (start us, length us, event | category | flops | bytes accessed | tf_op | source)
XLA Modules:
  0.0 658.9 jit_solution(8486678847312472778)
XLA Ops:
  7.2 0.7 pad_maximum_fusion.5
  8.1 0.7 copy.67
  8.8 24.7 %shard_map.255 = bf16[512,896]{1,0:T(8,128)(2,1)} custom-call(bf16[64,2048]{1,0:T(8,128)(2,1)} %refs_0_.1, bf16[64,2048]{1,0:T(8,128)(2,1)} %refs_1_.1, bf16[64,2048]{1,0:T(8,128)(2,1)} %refs_2_.1, bf16[64,1024]{1,0:T(8,128)(2,1)} %bitcast.48), custom_call_target="tpu_custom_call" | custom-call | flops 20000000000 | bytes 60000000 | tf_op jit(solution)/shard_map/pallas_call | solution.py:1273
  33.5 54.8 %shard_map.256 = bf16[512,2304]{1,0:T(8,128)(2,1)} custom-call(bf16[64,8192]{1,0:T(8,128)(2,1)} %refs_0_.2, bf16[64,8192]{1,0:T(8,128)(2,1)} %refs_1_.2, bf16[64,2048]{1,0:T(8,128)(2,1)} %bitcast.66), custom_call_target="tpu_custom_call" | custom-call | flops 49999998976 | bytes 150000000 | tf_op jit(solution)/shard_map/pallas_call | solution.py:1273
  89.0 0.6 fusion.15
  89.6 1.3 fusion.13
  90.9 0.6 pad.13
  91.5 46.9 %shard_map.257 = (bf16[1280,2048]{1,0:T(8,128)(2,1)}, s32[8,1,256]{2,1,0:T(1,128)}, f32[1280,768]{1,0:T(8,128)}) custom-call(bf16[160,2048]{1,0:T(8,128)(2,1)} %bitcast.59, s32[1,256]{1,0:T(1,128)} %bitcast.53, bf16[2048,896]{1,0:T(8,128)(2,1)} %all-gather.3.cloned.1.call-done.w_far.w_ref), custom_call_target="tpu_custom_call" | custom-call | flops 54999998464 | bytes 165000000 | tf_op jit(solution)/shard_map/pallas_call | solution.py:439
  138.4 0.7 slice_reduce_fusion
  139.4 0.2 reshape.256
  139.6 2.1 multiply_reduce_fusion.1
  141.8 0.6 pad_maximum_fusion.3.terms_ref
  142.4 11.7 %shard_map.258 = f32[2,1280]{1,0:T(2,128)} custom-call(f32[2,1280]{1,0:T(2,128)} %pad_maximum_fusion.3.terms_ref), custom_call_target="tpu_custom_call" | custom-call | flops 8000000000 | bytes 24000000 | tf_op jit(solution)/shard_map/pallas_call | solution.py:439
  154.1 0.7 rsqrt_bitcast_fusion
  154.9 1.1 copy.55.factor_ref
  156.0 2.3 copy.66
  158.2 5.3 all-to-all-start
  163.6 1.3 fusion.6.gains_ref
  164.9 0.6 fusion.14
  165.5 0.6 pad_maximum_fusion.4.gain_ref
  166.1 0.2 broadcast_multiply_fusion
  166.4 3.4 fusion.4
  169.8 0.6 compare_select_fusion
  170.4 1.2 add_select_fusion.qpos_ref
  171.6 12.8 %shard_map.259 = (bf16[1280,256]{1,0:T(8,128)(2,1)}, bf16[1280,256]{1,0:T(8,128)(2,1)}, bf16[1280,256]{1,0:T(8,128)(2,1)}, f32[1280,256]{1,0:T(8,128)}, bf16[1280,256]{1,0:T(8,128)(2,1)}, /*index=5*/f32[1280,2]{1,0:T(8,128)}) custom-call(f32[1280,768]{1,0:T(8,128)} %get-tuple-element.76.qkv_ref, f32[1280,2]{1,0:T(8,128)} %copy.55.factor_ref, ...), custom_call_target="tpu_custom_call" | custom-call | flops 1677721600 | bytes 60000000 | tf_op jit(solution)/shard_map/pallas_call | solution.py:1056
  184.5 2.2 all-to-all-done
  186.6 174.6 %shard_map.260 = (f32[160,2048]{1,0:T(8,128)}, bf16[160,2048]{1,0:T(8,128)(2,1)}, f32[8,2048]{1,0:T(8,128)}, bf16[1280,2048]{1,0:T(8,128)(2,1)}, bf16[1280,1024]...) custom-call(bf16[1280,256]{1,0:T(8,128)(2,1)} %get-tuple-element.82.left_far.low_ref,, ...), custom_call_target="tpu_custom_call" | custom-call | flops 149999992832 | bytes 450000000 | tf_op jit(solution)/shard_map/pallas_call | solution.py:439
  361.3 10.4 %convolution_convert_fusion.1 = bf16[2048,1024]{1,0:T(8,128)(2,1)} fusion(bf16[1280,2048]{1,0:T(8,128)(2,1)} %get-tuple-element.85, bf16[1280,2048]{1,0:T(8,128)(2,1)} %get-tuple-element.87.left), kind=kOutput, calls=%fused_computation.1 | convolution fusion | flops 5370806272 | bytes 12058624 | tf_op jit(solution)/shard_map/dot_general | solution.py:39
  371.8 10.2 %convolution_convert_fusion = bf16[2048,1024]{1,0:T(8,128)(2,1)} fusion(bf16[1280,2048]{1,0:T(8,128)(2,1)} %get-tuple-element.85, bf16[1280,2048]{1,0:T(8,128)(2,1)} %get-tuple-element.87.left), kind=kOutput, calls=%fused_computation | convolution fusion | flops 5370806272 | bytes 12058624 | tf_op jit(solution)/shard_map/dot_general | solution.py:39
  382.0 77.2 %shard_map.261 = (f32[160,2048]{1,0:T(8,128)}, f32[8,2048]{1,0:T(8,128)}, bf16[1280,2048]{1,0:T(8,128)(2,1)}, f32[1280,256]{1,0:T(8,128)}, bf16[2048,1024]{1,0:T(8,128)(2,1)}) custom-call(bf16[1280,2048]{1,0:T(8,128)(2,1)} %get-tuple-element.87.left, f32[80,2048]{1,0:T(8,128)} %get-tuple-element.88.first_ref, ...), custom_call_target="tpu_custom_call" | custom-call | flops 70000001024 | bytes 210000000 | tf_op jit(solution)/shard_map/pallas_call | solution.py:439
  459.3 0.6 copy-done.4
  459.9 0.1 copy-done.5
  460.2 37.5 %shard_map.262 = (f32[1280,256]{1,0:T(8,128)}, f32[1280,256]{1,0:T(8,128)}, bf16[1280,256]{1,0:T(8,128)(2,1)}, f32[1280,2]{1,0:T(8,128)}, f32[2,256]{1,0:T(2,128)}, /*index=5*/bf16[64,8192]{1,0:T(8,128)(2,1)}) custom-call(bf16[1280,256]{1,0:T(8,128)(2,1)} %get-tuple-element.79.q_ref, bf16[1280,256]{1,0:T(8,128)(2,1)} %get-tuple-element.80.k_ref, ...), custom_call_target="tpu_custom_call" | custom-call | flops 24999999488 | bytes 75000000 | tf_op jit(solution)/shard_map/pallas_call | solution.py:439
  497.7 1.9 copy.58
  499.6 0.7 constant_dynamic-update-slice_fusion
  500.4 0.3 copy.59
  500.7 0.9 pad.15.gain_ref
  501.6 6.1 shard_map.263
  507.7 0.7 broadcast_multiply_fusion.1
  508.4 3.3 multiply_convert_fusion.1
  511.7 1.4 pad_maximum_fusion.dq_ref.left
  513.1 28.6 %shard_map.264 = (bf16[2048,1152]{1,0:T(8,128)(2,1)}, bf16[64,8192]{1,0:T(8,128)(2,1)}) custom-call(bf16[1280,2048]{1,0:T(8,128)(2,1)} %get-tuple-element.100.x_far, bf16[1280,768]{1,0:T(8,128)(2,1)} %pad_maximum_fusion.dq_ref.left, bf16[1280,2048]{1,0:T(8,128)(2,1)} %get-tuple-element.101.gb_far, bf16[1280,256]{1,0:T(8,128)(2,1)} %get-tuple-element.82.left_far.low_ref, ...), custom_call_target="tpu_custom_call" | custom-call | flops 24999999488 | bytes 75000000 | tf_op jit(solution)/shard_map/pallas_call | solution.py:439
  541.8 2.8 convert_element_type.51
  544.5 1.5 convert_element_type.50
  546.1 68.9 %shard_map.265 = (bf16[160,2048]{1,0:T(8,128)(2,1)}, bf16[64,8192]{1,0:T(8,128)(2,1)}) custom-call(bf16[1280,768]{1,0:T(8,128)(2,1)} %pad_maximum_fusion.dq_ref.left, bf16[2048,896]{1,0:T(8,128)(2,1)} %all-gather.3.cloned.1.call-done.w_far.w_ref, f32[160,2048]{1,0:T(8,128)} %get-tuple-element.110.gh_ref, ...), custom_call_target="tpu_custom_call" | custom-call | flops 65000001536 | bytes 195000000 | tf_op jit(solution)/shard_map/pallas_call | solution.py:439
  615.0 31.3 %shard_map.266 = (bf16[64,2048]{1,0:T(8,128)(2,1)}, bf16[64,2048]{1,0:T(8,128)(2,1)}, bf16[64,2048]{1,0:T(8,128)(2,1)}, bf16[64,2048]{1,0:T(8,128)(2,1)}, bf16[64,1024]{1,0:T(8,128)(2,1)}) custom-call(bf16[512,1152]{1,0:T(8,128)(2,1)} %reduce-scatter.11.cloned.1.call-done.refs_0_), custom_call_target="tpu_custom_call" | custom-call | flops 30000001024 | bytes 90000000 | tf_op jit(solution)/shard_map/pallas_call | solution.py:439
  646.3 4.4 shard_map.267
  650.7 1.3 slice_bitcast_fusion
  (55 shorter events, 1.0 us)
Async XLA Ops:
  7.2 84.3 %all-gather.3.cloned.1.call-start = ((), (), s32[]{:S(2)}) async-start(), calls=%async_computation.5 | async-start | bytes 4587520 | tf_op jit(solution)/shard_map/all_gather | solution.py:43
  33.5 153.2 %all-gather.5.cloned.1.call-start = ((), (), s32[]{:S(2)}) async-start(), calls=%async_computation.6 | async-start | bytes 11796480 | tf_op jit(solution)/shard_map/all_gather | solution.py:43
  33.5 55.5 %copy-start.7 = (s32[1,2]{1,0:T(1,128)S(1)}, s32[1,2]{1,0:T(1,128)}, u32[]{:S(2)}) copy-start(s32[1,2]{1,0:T(1,128)} %param.31) | copy-start | bytes 28
  33.5 56.1 %copy-start.8 = (s32[1,160]{1,0:T(1,128)S(1)}, s32[1,160]{1,0:T(1,128)}, u32[]{:S(2)}) copy-start(s32[1,160]{1,0:T(1,128)} %param.29) | copy-start | bytes 1924
  154.8 10.0 %copy-start.3 = (f32[1280,2]{0,1:T(2,128)}, f32[1280,2]{0,1:T(2,128)S(1)}, u32[]{:S(2)}) copy-start(f32[1280,2]{0,1:T(2,128)S(1)} %rsqrt_bitcast_fusion) | copy-start | bytes 30724
  158.2 28.4 %all-to-all-start = ((bf16[64,8,1024]{2,0,1:T(8,128)(2,1)}), bf16[64,8,1024]{2,0,1:T(8,128)(2,1)}, u32[]{:S(2)}, u32[]{:S(2)}) async-start(bf16[64,8,1024]{2,0,1:T(8,128)(2,1)} %bitcast.41), calls=%async_computation | async-start | bytes 2097152 | tf_op jit(solution)/shard_map/all_to_all | solution.py:1412
  163.6 296.6 %reduce-scatter.5.cloned.1.call-start = ((), (), s32[]{:S(2)}) async-start(), calls=%async_computation.7 | async-start | bytes 5242880 | tf_op jit(solution)/shard_map/reduce_scatter | solution.py:47
  164.9 19.6 %copy-start.2 = (f32[8,2048]{1,0:T(8,128)}, f32[8,2048]{1,0:T(8,128)S(1)}, u32[]{:S(2)}) copy-start(f32[8,2048]{1,0:T(8,128)S(1)} %fusion.6.gains_ref) | copy-start | bytes 196612
  371.7 141.4 %reduce-scatter.7.cloned.1.call-start = ((), (), s32[]{:S(2)}) async-start(), calls=%async_computation.8 | async-start | bytes 5242880 | tf_op jit(solution)/shard_map/reduce_scatter | solution.py:47
  382.0 164.1 %reduce-scatter.9.cloned.1.call-start = ((), (), s32[]{:S(2)}) async-start(), calls=%async_computation.9 | async-start | bytes 5242880 | tf_op jit(solution)/shard_map/reduce_scatter | solution.py:47
  459.2 0.7 copy-start.4
  459.2 0.8 copy-start.5
  459.2 0.9 copy-start.6
  459.3 155.7 %reduce-scatter.11.cloned.1.call-start = ((), (), s32[]{:S(2)}) async-start(), calls=%async_computation.10 | async-start | bytes 5898240 | tf_op jit(solution)/shard_map/reduce_scatter | solution.py:47
  508.4 3.3 copy-start.1
  541.8 2.8 copy-start
Sparse Core Ops, SparseCore 0:
  33.6 48.8 all-gather.2
  88.5 96.8 all-gather.4
  371.8 58.6 reduce-scatter.4
  433.7 52.6 reduce-scatter.6
  489.2 52.6 reduce-scatter.8
  546.1 55.9 reduce-scatter.10

commit v6 on v5

--- a/solution.py
+++ b/solution.py
@@ -552,9 +552,9 @@
 
     def kernel(
         left_far, mid_far, down_far, x_far, go_far, gains_ref,
-        branch_far, out_ref, gg_ref, hid_far, mix_far, gm_far, dgu_far, first_ref,
+        branch_far, out_ref, gg_ref, hid_far, mix_far, gm_far, dgu_far, first_ref, turned_far,
         left, mid_ref, down_ref, x_ref, go_ref, branch_ref, hid_ref, mix_ref, gm_ref, dgu_ref,
-        down_turned, in_sem, out_sem, branch_sem, down_send, down_recv, *rest
+        down_turned, turned_sem, in_sem, out_sem, branch_sem, down_send, down_recv, *rest
     ):
         line = Line(ways)
         group = lax.axis_index("dp")
@@ -711,6 +711,8 @@
         advance(
             scatter, 1, back, 0, gate_up_back, turn_square if square else None, lambda: settle_mlp(1)
         )
+        keep_turned = pltpu.make_async_copy(mid_ref.at[:, gu_cols], turned_far, turned_sem)
+        keep_turned.start()
         scatter.of(dgu_ref, mid_ref.at[:, gu_cols], 1024, False, square)
 
         def keep_first():
@@ -725,6 +727,7 @@
         hidden.finish()
         back.finish()
         keep_branch.wait()
+        keep_turned.wait()
         outs.finish()
 
     return call(
@@ -738,6 +741,7 @@
             shape((row, width), bf16),
             shape((row, 2 * own_ff), bf16),
             shape((half, width), f32),
+            shape((width, 2 * own_ff), bf16),
         ],
         [
             pltpu.VMEM((row, own_feat), bf16),
@@ -751,6 +755,7 @@
             pltpu.VMEM((row, width), bf16),
             pltpu.VMEM((row, 2 * own_ff), bf16),
             pltpu.VMEM((own_ff, width) if square else (16, HEAD_DIM), bf16),
+            pltpu.SemaphoreType.DMA,
             pltpu.SemaphoreType.DMA((6,)),
             pltpu.SemaphoreType.DMA((4, ways)),
             pltpu.SemaphoreType.DMA,
@@ -764,12 +769,12 @@
         ident,
         150,
         range(5),
-        (0, 3, 4, 5, 6),
+        (0, 3, 4, 5, 6, 8),
     )
 
 
 def ff_to_attn_back(
-    grad_gu, first_half, m_mid, branch, grad_out, gain_row, grad_mlp, mixed_low, ways, ident
+    grad_gu, first_half, turned, m_mid, branch, grad_out, gain_row, grad_mlp, mixed_low, ways, ident
 ):
     tok, width = branch.shape
     half = tok // 2
@@ -779,11 +784,18 @@
     tiles = width // 256
 
     def kernel(
-        left, first_ref, w_ref, br_ref, go_ref, gain_ref, gm_far, mix_far,
+        left_far, first_ref, turned_far, w_far, br_ref, go_ref, gain_ref, gm_far, mix_far,
         gh_ref, gg_ref, all_far, ga_ref, dd_far,
-        all_ref, out_sem, gm_ref, mix_ref, dd_ref, gm_sem, mix_sem, dd_sem, *rest
+        left, turned_ref, w_ref, in_sem, all_ref, out_sem, gm_ref, mix_ref, dd_ref, gm_sem, mix_sem, dd_sem, *rest
     ):
         line = Line(ways)
+        wanted = [
+            pltpu.make_async_copy(w_far.at[:, pl.ds(2 * own_ff, own_feat)], w_ref, in_sem.at[0]),
+            pltpu.make_async_copy(turned_far, turned_ref, in_sem.at[2]),
+            pltpu.make_async_copy(left_far, left, in_sem.at[1]),
+        ]
+        for copy in wanted:
+            copy.start()
         mix_copy = pltpu.make_async_copy(mix_far, mix_ref, mix_sem)
 
         def fetch(i):
@@ -841,10 +853,12 @@
         def use(chip, h):
             at = rows_at(h * line.chips + chip, 2 * half)
             outs.send(0, chip, h)
-            ga_ref[at, :] = dot_nn(all_ref[at, :], w_ref[:, pl.ds(2 * own_ff, own_feat)])
-
-        scatter.of(left, w_ref.at[:, pl.ds(0, 2 * own_ff)], 1024, False)
+            ga_ref[at, :] = dot_nn(all_ref[at, :], w_ref[...])
+
+        scatter.of(left, turned_ref, 1024, False, width == 2 * own_ff)
         settle(0)
+        for copy in wanted:
+            copy.wait()
         advance(scatter, 1, gather, 0, use, settle=lambda: settle(1))
         mix_copy.start()
         fetch(0).start()
@@ -866,6 +880,10 @@
             shape((width, own_ff), bf16),
         ],
         [
+            pltpu.VMEM(grad_gu.shape, bf16),
+            pltpu.VMEM(turned.shape, bf16),
+            pltpu.VMEM((width, own_feat), bf16),
+            pltpu.SemaphoreType.DMA((3,)),
             pltpu.VMEM((row, width), bf16),
             pltpu.SemaphoreType.DMA((1, ways)),
             pltpu.VMEM((2, row, 256), bf16),
@@ -877,10 +895,10 @@
         ]
         + RowScatter.scratch(ways // 2, tok, width)
         + RowGather.scratch(ways // 2),
-        [grad_gu, first_half, m_mid, branch, grad_out, gain_row, grad_mlp, mixed_low],
+        [grad_gu, first_half, turned, m_mid, branch, grad_out, gain_row, grad_mlp, mixed_low],
         ident,
         70,
-        (6, 7),
+        (0, 2, 3, 7, 8),
         (2, 4),
     )
 
@@ -1419,7 +1437,7 @@
         [qkv, factors, cosine, sine, gain_qk] + places, min(row_len, 160)
     )
 
-    branch, layer_out, grad_gain_mlp, hidden_low, mixed_low, grad_mlp, grad_gu, first_half = (
+    branch, layer_out, grad_gain_mlp, hidden_low, mixed_low, grad_mlp, grad_gu, first_half, turned = (
         attn_out_and_ff(
             attn_low, m_mid, p_down, token_rows, cotangent[0], gains, groups, ways, 3
         )
@@ -1430,7 +1448,7 @@
     grad_gu, d_up = lax.optimization_barrier((grad_gu, d_up))
     d_gate, d_up = dp_sum(d_gate), dp_sum(d_up)
     grad_hidden, grad_gain_attn, grad_branch, grad_attn, d_down = ff_to_attn_back(
-        grad_gu, first_half, m_mid, branch, cotangent[0], gains[2:3], grad_mlp, mixed_low, ways, 5
+        grad_gu, first_half, turned, m_mid, branch, cotangent[0], gains[2:3], grad_mlp, mixed_low, ways, 5
     )
     d_down = dp_sum(d_down)
     c_q, c_k, grad_v, terms, gain_part, dw_gate = attend_back(

time: 660 us -> 659 us (level)
  no operation moved by 1% of the time
where the time goes in v6:
time: 659 us; the launch traced here: 658 us
  Pallas kernels  579 us (88%)
  matrix products  21.8 us (3%)
  other arithmetic  21.2 us (3%)
  between operations  15.1 us (2%)
  local copies, waits for them, and re-layouts  13.2 us (2%)
    pallas_call x9, Pallas kernels, call(): pl.pallas_call(kernel, out_shape=outs, in_specs=[space(i, far_in) for i i...  482 us
    pallas_call x2, Pallas kernels, exchange(): pl.pallas_call(kernel, out_shape=shape((ways * rows, sum(widths)), bf16),...  79.5 us
    dot_general x2, matrix products, dot_tn(): lax.dot_general(left, right, (((0,), (0,)), ((), ())), preferred_element_...  20.5 us
  transfers between devices with their start and end apart: 7, of which 1 were waited for; matrix products, arithmetic and copies ran while one was open for 6% of the time, Pallas kernels for 52%

profile of v6, /device:TPU:9, one launch (start us, length us, event | category | flops | bytes accessed | tf_op | source)
XLA Modules:
  0.0 658.3 jit_solution(7595499221872583193)
XLA Ops:
  7.2 0.7 pad_maximum_fusion.5
  8.1 0.7 copy.67
  8.8 24.7 %shard_map.255 = bf16[512,896]{1,0:T(8,128)(2,1)} custom-call(bf16[64,2048]{1,0:T(8,128)(2,1)} %refs_0_.1, bf16[64,2048]{1,0:T(8,128)(2,1)} %refs_1_.1, bf16[64,2048]{1,0:T(8,128)(2,1)} %refs_2_.1, bf16[64,1024]{1,0:T(8,128)(2,1)} %bitcast.48), custom_call_target="tpu_custom_call" | custom-call | flops 20000000000 | bytes 60000000 | tf_op jit(solution)/shard_map/pallas_call | solution.py:1291
  33.5 54.8 %shard_map.256 = bf16[512,2304]{1,0:T(8,128)(2,1)} custom-call(bf16[64,8192]{1,0:T(8,128)(2,1)} %refs_0_.2, bf16[64,8192]{1,0:T(8,128)(2,1)} %refs_1_.2, bf16[64,2048]{1,0:T(8,128)(2,1)} %bitcast.66), custom_call_target="tpu_custom_call" | custom-call | flops 49999998976 | bytes 150000000 | tf_op jit(solution)/shard_map/pallas_call | solution.py:1291
  89.0 0.6 fusion.15
  89.6 1.3 fusion.13
  90.9 0.6 pad.13
  91.5 46.9 %shard_map.257 = (bf16[1280,2048]{1,0:T(8,128)(2,1)}, s32[8,1,256]{2,1,0:T(1,128)}, f32[1280,768]{1,0:T(8,128)}) custom-call(bf16[160,2048]{1,0:T(8,128)(2,1)} %bitcast.59, s32[1,256]{1,0:T(1,128)} %bitcast.53, bf16[2048,896]{1,0:T(8,128)(2,1)} %all-gather.3.cloned.1.call-done.w_far.w_ref), custom_call_target="tpu_custom_call" | custom-call | flops 54999998464 | bytes 165000000 | tf_op jit(solution)/shard_map/pallas_call | solution.py:439
  138.4 0.7 slice_reduce_fusion
  139.4 0.2 reshape.256
  139.7 2.1 multiply_reduce_fusion.1
  141.8 0.6 pad_maximum_fusion.3.terms_ref
  142.4 11.7 %shard_map.258 = f32[2,1280]{1,0:T(2,128)} custom-call(f32[2,1280]{1,0:T(2,128)} %pad_maximum_fusion.3.terms_ref), custom_call_target="tpu_custom_call" | custom-call | flops 8000000000 | bytes 24000000 | tf_op jit(solution)/shard_map/pallas_call | solution.py:439
  154.1 0.7 rsqrt_bitcast_fusion
  154.9 1.1 copy.55.factor_ref
  156.0 2.3 copy.66
  158.3 5.3 all-to-all-start
  163.6 1.3 fusion.6.gains_ref
  164.9 0.6 fusion.14
  165.5 0.6 pad_maximum_fusion.4.gain_ref
  166.1 0.2 broadcast_multiply_fusion
  166.3 3.4 fusion.4
  169.8 0.6 compare_select_fusion
  170.4 1.2 add_select_fusion.qpos_ref
  171.7 12.8 %shard_map.259 = (bf16[1280,256]{1,0:T(8,128)(2,1)}, bf16[1280,256]{1,0:T(8,128)(2,1)}, bf16[1280,256]{1,0:T(8,128)(2,1)}, f32[1280,256]{1,0:T(8,128)}, bf16[1280,256]{1,0:T(8,128)(2,1)}, /*index=5*/f32[1280,2]{1,0:T(8,128)}) custom-call(f32[1280,768]{1,0:T(8,128)} %get-tuple-element.77.qkv_ref, f32[1280,2]{1,0:T(8,128)} %copy.55.factor_ref, ...), custom_call_target="tpu_custom_call" | custom-call | flops 1677721600 | bytes 60000000 | tf_op jit(solution)/shard_map/pallas_call | solution.py:1074
  184.5 2.2 all-to-all-done
  186.6 174.6 %shard_map.260 = (f32[160,2048]{1,0:T(8,128)}, bf16[160,2048]{1,0:T(8,128)(2,1)}, f32[8,2048]{1,0:T(8,128)}, bf16[1280,2048]{1,0:T(8,128)(2,1)}, bf16[1280,1024]...) custom-call(bf16[1280,256]{1,0:T(8,128)(2,1)} %get-tuple-element.83., ...), custom_call_target="tpu_custom_call" | custom-call | flops 149999992832 | bytes 450000000 | tf_op jit(solution)/shard_map/pallas_call | solution.py:439
  361.3 10.4 %convolution_convert_fusion.1 = bf16[2048,1024]{1,0:T(8,128)(2,1)} fusion(bf16[1280,2048]{1,0:T(8,128)(2,1)} %get-tuple-element.86, bf16[1280,2048]{1,0:T(8,128)(2,1)} %get-tuple-element.88.left_far), kind=kOutput, calls=%fused_computation.1 | convolution fusion | flops 5370806272 | bytes 12058624 | tf_op jit(solution)/shard_map/dot_general | solution.py:39
  371.7 10.1 %convolution_convert_fusion = bf16[2048,1024]{1,0:T(8,128)(2,1)} fusion(bf16[1280,2048]{1,0:T(8,128)(2,1)} %get-tuple-element.86, bf16[1280,2048]{1,0:T(8,128)(2,1)} %get-tuple-element.88.left_far), kind=kOutput, calls=%fused_computation | convolution fusion | flops 5370806272 | bytes 12058624 | tf_op jit(solution)/shard_map/dot_general | solution.py:39
  382.0 75.3 %shard_map.261 = (f32[160,2048]{1,0:T(8,128)}, f32[8,2048]{1,0:T(8,128)}, bf16[1280,2048]{1,0:T(8,128)(2,1)}, f32[1280,256]{1,0:T(8,128)}, bf16[2048,1024]{1,0:T(8,128)(2,1)}) custom-call(bf16[1280,2048]{1,0:T(8,128)(2,1)} %get-tuple-element.88.left_far, f32[80,2048]{1,0:T(8,128)} %get-tuple-element.89.first_ref, ...), custom_call_target="tpu_custom_call" | custom-call | flops 70000001024 | bytes 210000000 | tf_op jit(solution)/shard_map/pallas_call | solution.py:439
  457.4 0.6 copy-done.4
  458.1 0.1 copy-done.5
  458.3 38.6 %shard_map.262 = (f32[1280,256]{1,0:T(8,128)}, f32[1280,256]{1,0:T(8,128)}, bf16[1280,256]{1,0:T(8,128)(2,1)}, f32[1280,2]{1,0:T(8,128)}, f32[2,256]{1,0:T(2,128)}, /*index=5*/bf16[64,8192]{1,0:T(8,128)(2,1)}) custom-call(bf16[1280,256]{1,0:T(8,128)(2,1)} %get-tuple-element.80.q_ref, bf16[1280,256]{1,0:T(8,128)(2,1)} %get-tuple-element.81.k_ref, ...), custom_call_target="tpu_custom_call" | custom-call | flops 24999999488 | bytes 75000000 | tf_op jit(solution)/shard_map/pallas_call | solution.py:439
  496.9 1.9 copy.58
  498.8 0.7 constant_dynamic-update-slice_fusion
  499.5 0.3 copy.59
  499.8 0.9 pad.15.gain_ref
  500.7 6.2 shard_map.263
  506.9 0.7 broadcast_multiply_fusion.1
  507.7 3.1 multiply_convert_fusion.1
  510.8 1.4 pad_maximum_fusion.dq_ref.left
  512.2 28.9 %shard_map.264 = (bf16[2048,1152]{1,0:T(8,128)(2,1)}, bf16[64,8192]{1,0:T(8,128)(2,1)}) custom-call(bf16[1280,2048]{1,0:T(8,128)(2,1)} %get-tuple-element.102.x_far, bf16[1280,768]{1,0:T(8,128)(2,1)} %pad_maximum_fusion.dq_ref.left, bf16[1280,2048]{1,0:T(8,128)(2,1)} %get-tuple-element.103.gb_far, bf16[1280,256]{1,0:T(8,128)(2,1)} %get-tuple-element.83.left_far.low_ref, ...), custom_call_target="tpu_custom_call" | custom-call | flops 24999999488 | bytes 75000000 | tf_op jit(solution)/shard_map/pallas_call | solution.py:439
  541.1 2.8 convert_element_type.51
  543.9 1.5 convert_element_type.50
  545.4 68.9 %shard_map.265 = (bf16[160,2048]{1,0:T(8,128)(2,1)}, bf16[64,8192]{1,0:T(8,128)(2,1)}) custom-call(bf16[1280,768]{1,0:T(8,128)(2,1)} %pad_maximum_fusion.dq_ref.left, bf16[2048,896]{1,0:T(8,128)(2,1)} %all-gather.3.cloned.1.call-done.w_far.w_ref, f32[160,2048]{1,0:T(8,128)} %get-tuple-element.112.gh_ref, ...), custom_call_target="tpu_custom_call" | custom-call | flops 65000001536 | bytes 195000000 | tf_op jit(solution)/shard_map/pallas_call | solution.py:439
  614.3 31.3 %shard_map.266 = (bf16[64,2048]{1,0:T(8,128)(2,1)}, bf16[64,2048]{1,0:T(8,128)(2,1)}, bf16[64,2048]{1,0:T(8,128)(2,1)}, bf16[64,2048]{1,0:T(8,128)(2,1)}, bf16[64,1024]{1,0:T(8,128)(2,1)}) custom-call(bf16[512,1152]{1,0:T(8,128)(2,1)} %reduce-scatter.11.cloned.1.call-done.refs_0_), custom_call_target="tpu_custom_call" | custom-call | flops 30000001024 | bytes 90000000 | tf_op jit(solution)/shard_map/pallas_call | solution.py:439
  645.6 4.4 shard_map.267
  650.1 1.3 slice_bitcast_fusion
  (55 shorter events, 1.0 us)
Async XLA Ops:
  7.2 84.3 %all-gather.3.cloned.1.call-start = ((), (), s32[]{:S(2)}) async-start(), calls=%async_computation.5 | async-start | bytes 4587520 | tf_op jit(solution)/shard_map/all_gather | solution.py:43
  33.5 153.2 %all-gather.5.cloned.1.call-start = ((), (), s32[]{:S(2)}) async-start(), calls=%async_computation.6 | async-start | bytes 11796480 | tf_op jit(solution)/shard_map/all_gather | solution.py:43
  33.5 55.5 %copy-start.7 = (s32[1,2]{1,0:T(1,128)S(1)}, s32[1,2]{1,0:T(1,128)}, u32[]{:S(2)}) copy-start(s32[1,2]{1,0:T(1,128)} %param.31) | copy-start | bytes 28
  33.5 56.1 %copy-start.8 = (s32[1,160]{1,0:T(1,128)S(1)}, s32[1,160]{1,0:T(1,128)}, u32[]{:S(2)}) copy-start(s32[1,160]{1,0:T(1,128)} %param.29) | copy-start | bytes 1924
  154.9 10.0 %copy-start.3 = (f32[1280,2]{0,1:T(2,128)}, f32[1280,2]{0,1:T(2,128)S(1)}, u32[]{:S(2)}) copy-start(f32[1280,2]{0,1:T(2,128)S(1)} %rsqrt_bitcast_fusion) | copy-start | bytes 30724
  158.3 28.4 %all-to-all-start = ((bf16[64,8,1024]{2,0,1:T(8,128)(2,1)}), bf16[64,8,1024]{2,0,1:T(8,128)(2,1)}, u32[]{:S(2)}, u32[]{:S(2)}) async-start(bf16[64,8,1024]{2,0,1:T(8,128)(2,1)} %bitcast.41), calls=%async_computation | async-start | bytes 2097152 | tf_op jit(solution)/shard_map/all_to_all | solution.py:1430
  163.6 294.7 %reduce-scatter.5.cloned.1.call-start = ((), (), s32[]{:S(2)}) async-start(), calls=%async_computation.7 | async-start | bytes 5242880 | tf_op jit(solution)/shard_map/reduce_scatter | solution.py:47
  164.9 19.6 %copy-start.2 = (f32[8,2048]{1,0:T(8,128)}, f32[8,2048]{1,0:T(8,128)S(1)}, u32[]{:S(2)}) copy-start(f32[8,2048]{1,0:T(8,128)S(1)} %fusion.6.gains_ref) | copy-start | bytes 196612
  371.7 140.5 %reduce-scatter.7.cloned.1.call-start = ((), (), s32[]{:S(2)}) async-start(), calls=%async_computation.8 | async-start | bytes 5242880 | tf_op jit(solution)/shard_map/reduce_scatter | solution.py:47
  381.9 163.5 %reduce-scatter.9.cloned.1.call-start = ((), (), s32[]{:S(2)}) async-start(), calls=%async_computation.9 | async-start | bytes 5242880 | tf_op jit(solution)/shard_map/reduce_scatter | solution.py:47
  457.3 0.7 copy-start.4
  457.3 0.9 copy-start.5
  457.3 0.9 copy-start.6
  457.4 156.9 %reduce-scatter.11.cloned.1.call-start = ((), (), s32[]{:S(2)}) async-start(), calls=%async_computation.10 | async-start | bytes 5898240 | tf_op jit(solution)/shard_map/reduce_scatter | solution.py:47
  507.6 3.1 copy-start.1
  541.0 2.8 copy-start
Sparse Core Ops, SparseCore 0:
  33.6 48.8 all-gather.2
  88.5 96.8 all-gather.4
  371.8 58.5 reduce-scatter.4
  433.5 52.6 reduce-scatter.6
  489.1 52.6 reduce-scatter.8
  545.5 56.4 reduce-scatter.10

commit v7 on v6

--- a/solution.py
+++ b/solution.py
@@ -1417,7 +1417,9 @@
 
     code_pad = -tok_count % HEAD_DIM
     local_code = jnp.pad(local_pos * 2 + key_ok, (0, code_pad))[None]
-    local_code, p_mid = lax.optimization_barrier((local_code, p_mid))
+    down_blocks = jnp.transpose(w_down).reshape(w_down.shape[1], ways, own_ff)
+    down_blocks = jnp.transpose(down_blocks, (1, 0, 2))
+    local_code, p_mid, down_blocks = lax.optimization_barrier((local_code, p_mid, down_blocks))
     x_row, codes, qkv = gather_project(token_rows, local_code, m_qkv, ways, 1)
     key_code = codes[:, 0, :tok_count].reshape(ways, 2, half_len)
     key_code = jnp.transpose(key_code, (1, 0, 2)).reshape(row_len)
@@ -1426,8 +1428,9 @@
     squares = line_sum(
         jnp.stack([jnp.sum(q_raw * q_raw, axis=-1), jnp.sum(k_raw * k_raw, axis=-1)]), ways, 2
     )
-    squares, w_down_t = lax.optimization_barrier((squares, jnp.transpose(w_down)))
-    p_down = lax.all_to_all(w_down_t, "seq", split_axis=1, concat_axis=0, tiled=True)
+    squares, down_blocks = lax.optimization_barrier((squares, down_blocks))
+    p_down = lax.all_to_all(down_blocks, "seq", split_axis=0, concat_axis=0, tiled=True)
+    p_down = p_down.reshape(-1, own_ff)
     factors = jnp.transpose(lax.rsqrt(squares / feat_width + norm_eps))
     cosine, sine = rope_tables(pos, HEAD_DIM)
     key_most = jnp.where(key_code % 2 == 1, jnp.int32(2**30), pos)

time: 659 us -> 656 us (level)
  transfers between devices with their start and end apart: 7 -> 7, of which waited for: 1 -> 2; matrix products, arithmetic and copies ran while one was open for 6% -> 6% of each run, Pallas kernels for 52% -> 52%
where the time goes in v7:
time: 656 us; the launch traced here: 655 us
  Pallas kernels  577 us (88%)
  matrix products  21.8 us (3%)
  other arithmetic  21.2 us (3%)
  between operations  15.2 us (2%)
  local copies, waits for them, and re-layouts  12 us (2%)
    pallas_call x9, Pallas kernels, call(): pl.pallas_call(kernel, out_shape=outs, in_specs=[space(i, far_in) for i i...  480 us
    pallas_call x2, Pallas kernels, exchange(): pl.pallas_call(kernel, out_shape=shape((ways * rows, sum(widths)), bf16),...  79.5 us
    dot_general x2, matrix products, dot_tn(): lax.dot_general(left, right, (((0,), (0,)), ((), ())), preferred_element_...  20.5 us
  transfers between devices with their start and end apart: 7, of which 2 were waited for; matrix products, arithmetic and copies ran while one was open for 6% of the time, Pallas kernels for 52%

profile of v7, /device:TPU:9, one launch (start us, length us, event | category | flops | bytes accessed | tf_op | source)
XLA Modules:
  0.0 655.1 jit_solution(12914493958397093967)
XLA Ops:
  7.2 0.7 pad_maximum_fusion.5
  8.1 0.7 copy.67
  8.8 24.7 %shard_map.255 = bf16[512,896]{1,0:T(8,128)(2,1)} custom-call(bf16[64,2048]{1,0:T(8,128)(2,1)} %refs_0_.1, bf16[64,2048]{1,0:T(8,128)(2,1)} %refs_1_.1, bf16[64,2048]{1,0:T(8,128)(2,1)} %refs_2_.1, bf16[64,1024]{1,0:T(8,128)(2,1)} %bitcast.50), custom_call_target="tpu_custom_call" | custom-call | flops 20000000000 | bytes 60000000 | tf_op jit(solution)/shard_map/pallas_call | solution.py:1291
  33.5 54.8 %shard_map.256 = bf16[512,2304]{1,0:T(8,128)(2,1)} custom-call(bf16[64,8192]{1,0:T(8,128)(2,1)} %refs_0_.2, bf16[64,8192]{1,0:T(8,128)(2,1)} %refs_1_.2, bf16[64,2048]{1,0:T(8,128)(2,1)} %bitcast.68), custom_call_target="tpu_custom_call" | custom-call | flops 49999998976 | bytes 150000000 | tf_op jit(solution)/shard_map/pallas_call | solution.py:1291
  89.1 0.6 fusion.15
  89.7 1.3 fusion.13
  91.0 0.6 pad.13
  91.6 1.1 copy.66
  92.7 46.9 %shard_map.257 = (bf16[1280,2048]{1,0:T(8,128)(2,1)}, s32[8,1,256]{2,1,0:T(1,128)}, f32[1280,768]{1,0:T(8,128)}) custom-call(bf16[160,2048]{1,0:T(8,128)(2,1)} %bitcast.61, s32[1,256]{1,0:T(1,128)} %bitcast.55, bf16[2048,896]{1,0:T(8,128)(2,1)} %all-gather.3.cloned.1.call-done.w_far.w_ref), custom_call_target="tpu_custom_call" | custom-call | flops 54999998464 | bytes 165000000 | tf_op jit(solution)/shard_map/pallas_call | solution.py:439
  139.6 0.7 slice_reduce_fusion
  140.6 0.2 reshape.261
  140.8 2.1 multiply_reduce_fusion.1
  143.0 0.6 pad_maximum_fusion.3.terms_ref
  143.6 11.7 %shard_map.258 = f32[2,1280]{1,0:T(2,128)} custom-call(f32[2,1280]{1,0:T(2,128)} %pad_maximum_fusion.3.terms_ref), custom_call_target="tpu_custom_call" | custom-call | flops 8000000000 | bytes 24000000 | tf_op jit(solution)/shard_map/pallas_call | solution.py:439
  155.3 5.4 all-to-all-start
  160.6 0.7 rsqrt_bitcast_fusion
  161.4 1.1 copy.56.factor_ref
  162.5 1.3 fusion.6.gains_ref
  163.8 0.6 fusion.14
  164.4 0.6 pad_maximum_fusion.4.gain_ref
  165.0 0.2 broadcast_multiply_fusion
  165.2 3.4 fusion.4
  168.7 0.6 compare_select_fusion
  169.3 1.2 add_select_fusion.qpos_ref
  170.5 12.8 %shard_map.259 = (bf16[1280,256]{1,0:T(8,128)(2,1)}, bf16[1280,256]{1,0:T(8,128)(2,1)}, bf16[1280,256]{1,0:T(8,128)(2,1)}, f32[1280,256]{1,0:T(8,128)}, bf16[1280,256]{1,0:T(8,128)(2,1)}, /*index=5*/f32[1280,2]{1,0:T(8,128)}) custom-call(f32[1280,768]{1,0:T(8,128)} %get-tuple-element.78.qkv_ref, f32[1280,2]{1,0:T(8,128)} %copy.56.factor_ref, ...), custom_call_target="tpu_custom_call" | custom-call | flops 1677721600 | bytes 60000000 | tf_op jit(solution)/shard_map/pallas_call | solution.py:1074
  183.3 0.4 all-to-all-done
  183.7 1.7 all-gather.5.cloned.1.call-done.mid_far.w_far
  185.4 173.0 %shard_map.260 = (f32[160,2048]{1,0:T(8,128)}, bf16[160,2048]{1,0:T(8,128)(2,1)}, f32[8,2048]{1,0:T(8,128)}, bf16[1280,2048]{1,0:T(8,128)(2,1)}, bf16[1280,1024]...) custom-call(bf16[1280,256]{1,0:T(8,128)(2,1)} %get-tuple-element.85., ...), custom_call_target="tpu_custom_call" | custom-call | flops 149999992832 | bytes 450000000 | tf_op jit(solution)/shard_map/pallas_call | solution.py:439
  358.3 10.4 %convolution_convert_fusion.1 = bf16[2048,1024]{1,0:T(8,128)(2,1)} fusion(bf16[1280,2048]{1,0:T(8,128)(2,1)} %get-tuple-element.88, bf16[1280,2048]{1,0:T(8,128)(2,1)} %get-tuple-element.90.left_far), kind=kOutput, calls=%fused_computation.1 | convolution fusion | flops 5370806272 | bytes 12058624 | tf_op jit(solution)/shard_map/dot_general | solution.py:39
  368.8 10.1 %convolution_convert_fusion = bf16[2048,1024]{1,0:T(8,128)(2,1)} fusion(bf16[1280,2048]{1,0:T(8,128)(2,1)} %get-tuple-element.88, bf16[1280,2048]{1,0:T(8,128)(2,1)} %get-tuple-element.90.left_far), kind=kOutput, calls=%fused_computation | convolution fusion | flops 5370806272 | bytes 12058624 | tf_op jit(solution)/shard_map/dot_general | solution.py:39
  379.0 75.1 %shard_map.261 = (f32[160,2048]{1,0:T(8,128)}, f32[8,2048]{1,0:T(8,128)}, bf16[1280,2048]{1,0:T(8,128)(2,1)}, f32[1280,256]{1,0:T(8,128)}, bf16[2048,1024]{1,0:T(8,128)(2,1)}) custom-call(bf16[1280,2048]{1,0:T(8,128)(2,1)} %get-tuple-element.90.left_far, f32[80,2048]{1,0:T(8,128)} %get-tuple-element.91.first_ref, ...), custom_call_target="tpu_custom_call" | custom-call | flops 70000001024 | bytes 210000000 | tf_op jit(solution)/shard_map/pallas_call | solution.py:439
  454.2 0.6 copy-done.5
  455.1 38.5 %shard_map.262 = (f32[1280,256]{1,0:T(8,128)}, f32[1280,256]{1,0:T(8,128)}, bf16[1280,256]{1,0:T(8,128)(2,1)}, f32[1280,2]{1,0:T(8,128)}, f32[2,256]{1,0:T(2,128)}, /*index=5*/bf16[64,8192]{1,0:T(8,128)(2,1)}) custom-call(bf16[1280,256]{1,0:T(8,128)(2,1)} %get-tuple-element.82.q_ref, bf16[1280,256]{1,0:T(8,128)(2,1)} %get-tuple-element.83.k_ref, ...), custom_call_target="tpu_custom_call" | custom-call | flops 24999999488 | bytes 75000000 | tf_op jit(solution)/shard_map/pallas_call | solution.py:439
  493.6 1.9 copy.58
  495.5 0.7 constant_dynamic-update-slice_fusion
  496.3 0.3 copy.59
  496.6 0.9 pad.15.gain_ref
  497.5 6.2 shard_map.263
  503.7 0.7 broadcast_multiply_fusion.1
  504.4 3.1 multiply_convert_fusion.1
  507.6 1.4 pad_maximum_fusion.dq_ref.left
  509.0 29.1 %shard_map.264 = (bf16[2048,1152]{1,0:T(8,128)(2,1)}, bf16[64,8192]{1,0:T(8,128)(2,1)}) custom-call(bf16[1280,2048]{1,0:T(8,128)(2,1)} %get-tuple-element.104.x_far, bf16[1280,768]{1,0:T(8,128)(2,1)} %pad_maximum_fusion.dq_ref.left, bf16[1280,2048]{1,0:T(8,128)(2,1)} %get-tuple-element.105.gb_far, bf16[1280,256]{1,0:T(8,128)(2,1)} %get-tuple-element.85.left_far.low_ref, ...), custom_call_target="tpu_custom_call" | custom-call | flops 24999999488 | bytes 75000000 | tf_op jit(solution)/shard_map/pallas_call | solution.py:439
  538.1 2.8 convert_element_type.51
  540.9 1.5 convert_element_type.50
  542.4 68.7 %shard_map.265 = (bf16[160,2048]{1,0:T(8,128)(2,1)}, bf16[64,8192]{1,0:T(8,128)(2,1)}) custom-call(bf16[1280,768]{1,0:T(8,128)(2,1)} %pad_maximum_fusion.dq_ref.left, bf16[2048,896]{1,0:T(8,128)(2,1)} %all-gather.3.cloned.1.call-done.w_far.w_ref, f32[160,2048]{1,0:T(8,128)} %get-tuple-element.114.gh_ref, ...), custom_call_target="tpu_custom_call" | custom-call | flops 65000001536 | bytes 195000000 | tf_op jit(solution)/shard_map/pallas_call | solution.py:439
  611.1 31.3 %shard_map.266 = (bf16[64,2048]{1,0:T(8,128)(2,1)}, bf16[64,2048]{1,0:T(8,128)(2,1)}, bf16[64,2048]{1,0:T(8,128)(2,1)}, bf16[64,2048]{1,0:T(8,128)(2,1)}, bf16[64,1024]{1,0:T(8,128)(2,1)}) custom-call(bf16[512,1152]{1,0:T(8,128)(2,1)} %reduce-scatter.11.cloned.1.call-done.refs_0_), custom_call_target="tpu_custom_call" | custom-call | flops 30000001024 | bytes 90000000 | tf_op jit(solution)/shard_map/pallas_call | solution.py:439
  642.4 4.4 shard_map.267
  646.9 1.3 slice_bitcast_fusion
  (57 shorter events, 1.2 us)
Async XLA Ops:
  7.2 85.5 %all-gather.3.cloned.1.call-start = ((), (), s32[]{:S(2)}) async-start(), calls=%async_computation.5 | async-start | bytes 4587520 | tf_op jit(solution)/shard_map/all_gather | solution.py:43
  33.5 151.9 %all-gather.5.cloned.1.call-start = ((), (), s32[]{:S(2)}) async-start(), calls=%async_computation.6 | async-start | bytes 11796480 | tf_op jit(solution)/shard_map/all_gather | solution.py:43
  33.5 55.6 %copy-start.8 = (s32[1,2]{1,0:T(1,128)S(1)}, s32[1,2]{1,0:T(1,128)}, u32[]{:S(2)}) copy-start(s32[1,2]{1,0:T(1,128)} %param.31) | copy-start | bytes 28
  33.5 56.2 %copy-start.9 = (s32[1,160]{1,0:T(1,128)S(1)}, s32[1,160]{1,0:T(1,128)}, u32[]{:S(2)}) copy-start(s32[1,160]{1,0:T(1,128)} %param.29) | copy-start | bytes 1924
  88.3 3.3 copy-start.1
  155.3 28.4 %all-to-all-start = ((bf16[8,64,1024]{2,1,0:T(8,128)(2,1)}), bf16[8,64,1024]{2,1,0:T(8,128)(2,1)}, u32[]{:S(2)}, u32[]{:S(2)}) async-start(bf16[8,64,1024]{2,1,0:T(8,128)(2,1)} %bitcast.46), calls=%async_computation | async-start | bytes 2097152 | tf_op jit(solution)/shard_map/all_to_all | solution.py:1432
  160.6 294.5 %reduce-scatter.5.cloned.1.call-start = ((), (), s32[]{:S(2)}) async-start(), calls=%async_computation.7 | async-start | bytes 5242880 | tf_op jit(solution)/shard_map/reduce_scatter | solution.py:47
  161.4 9.2 %copy-start.4 = (f32[1280,2]{0,1:T(2,128)}, f32[1280,2]{0,1:T(2,128)S(1)}, u32[]{:S(2)}) copy-start(f32[1280,2]{0,1:T(2,128)S(1)} %rsqrt_bitcast_fusion) | copy-start | bytes 30724
  163.8 19.6 %copy-start.3 = (f32[8,2048]{1,0:T(8,128)}, f32[8,2048]{1,0:T(8,128)S(1)}, u32[]{:S(2)}) copy-start(f32[8,2048]{1,0:T(8,128)S(1)} %fusion.6.gains_ref) | copy-start | bytes 196612
  368.7 140.2 %reduce-scatter.7.cloned.1.call-start = ((), (), s32[]{:S(2)}) async-start(), calls=%async_computation.8 | async-start | bytes 5242880 | tf_op jit(solution)/shard_map/reduce_scatter | solution.py:47
  379.0 163.4 %reduce-scatter.9.cloned.1.call-start = ((), (), s32[]{:S(2)}) async-start(), calls=%async_computation.9 | async-start | bytes 5242880 | tf_op jit(solution)/shard_map/reduce_scatter | solution.py:47
  454.1 0.7 copy-start.5
  454.1 0.9 copy-start.6
  454.1 0.9 copy-start.7
  454.2 156.9 %reduce-scatter.11.cloned.1.call-start = ((), (), s32[]{:S(2)}) async-start(), calls=%async_computation.10 | async-start | bytes 5898240 | tf_op jit(solution)/shard_map/reduce_scatter | solution.py:47
  504.4 3.2 copy-start.2
  538.1 2.8 copy-start
Sparse Core Ops, SparseCore 0:
  33.6 48.8 all-gather.2
  88.5 96.8 all-gather.4
  368.9 58.6 reduce-scatter.4
  430.6 52.6 reduce-scatter.6
  486.2 52.6 reduce-scatter.8
  542.5 56.5 reduce-scatter.10
